TPU v7x, 256 devices: a whole 4x4x8 slice. The times are simulated.
256 devices in a mesh: slab: 64 (over y, z, core), batch: 4 (over x).
Axes of the slice: x: 4, y: 4, z: 8, core: 2. Of those that a mesh axis runs over, the one named last changes fastest.
Arguments:
- velocity_old: float32 [512, 64, 2, 3, 128], P('slab', 'batch'), may hold values from -6 to 6
- traction: bfloat16 [49152, 3, 169], P(('slab', 'batch')), may hold values from -6 to 6
- offsets: bfloat16 [49152, 3, 338], P(('slab', 'batch')), may hold values from -1 to 2
- owner_slab: int32 [49152, 1], P(('slab', 'batch')), may hold values from 0 to 63; in each aligned block of 192 rows (0 to 191, 192 to 383, ...) at most 6 rows name the same one
- anchor: int32 [49152, 3], P(('slab', 'batch')), may hold values from 1 to 253, as said below
- blocks: int32 [49152, 16], P(('slab', 'batch')), may hold values from 0 to 1023, as said below
- block_count: int32 [49152], P(('slab', 'batch')), may hold values from 8 to 16, as said below
- synthesis: bfloat16 [169, 338], replicated, may hold values from -0.5 to 0.5
- analysis: bfloat16 [169, 338], replicated, may hold values from -0.3125 to 0.3125
Outputs:
- velocity_new: float32 [512, 64, 2, 3, 128], P('slab', 'batch')
- velocity_coef: bfloat16 [49152, 3, 169], P(('slab', 'batch'))
Inputs may be any that keep to these rules, and one draw needn't show every extreme that they name: `owner_slab`: among the 192 cells of one device at most 6 name the same slab, and that bound is reached. `anchor`: in the owner's slab: first coordinate 1 to 5, second 1 to 61, third 1 to 125 within its tile of 128 points. `blocks`: the first block_count entries of a cell are distinct lines within two cells of its anchor in the first two dimensions, in its anchor's tile along the third; the remaining entries are padding with any tile number. `block_count`: some cells of every device use all 16 blocks.
All inputs are finite; a program needn't handle non-finite values.
Results may differ from a plain program's by a relative error of at most 0.012.
Values may be sent and summed in bfloat16 or wider, within the bound.
A program may use at most 64 MiB of HBM per device.

v0:
```python
import math

import jax
import jax.numpy as jnp
from jax import lax
from jax.sharding import PartitionSpec as P

SWEEPS = 2
GX = 8
NY = 64
NZ = 256


kernel_width = 0.8
kernel_norm = 1.0 / (0.8 * math.sqrt(2.0 * math.pi))
coupling = 2.0


def padded_2(block, sides, width):
    for axis, dim in sides:
        count = lax.axis_size(axis)
        forward = [(i, i + 1) for i in range(count - 1)]
        backward = [(target, source) for source, target in forward]
        low = lax.ppermute(
            lax.slice_in_dim(block, block.shape[dim] - width, None, axis=dim), axis, forward
        )
        high = lax.ppermute(lax.slice_in_dim(block, 0, width, axis=dim), axis, backward)
        block = jnp.concatenate([low, block, high], axis=dim)
    return block


def kernel_value(distance):
    scaled = distance / kernel_width
    return jnp.exp(-0.5 * scaled * scaled) * kernel_norm


def stencil_weights(anchor_part, offset_part, block_part, count_part):
    layers = NZ // 128
    points = anchor_part[:, :, None].astype(jnp.float32) + offset_part.astype(jnp.float32)
    tile_x = (block_part // (NY * layers)).astype(jnp.float32)
    tile_y = (block_part // layers % NY).astype(jnp.float32)
    live_mask = (jnp.arange(block_part.shape[1])[None, :] < count_part[:, None]).astype(jnp.float32)
    weight_xy = (
        kernel_value(points[:, 0, None, :] - tile_x[:, :, None])
        * kernel_value(points[:, 1, None, :] - tile_y[:, :, None])
        * live_mask[:, :, None]
    )
    z_root = (anchor_part[:, 2] // 128 * 128).astype(jnp.float32)
    heights = z_root[:, None, None] + jnp.arange(128, dtype=jnp.float32)[None, None, :]
    weight_z = kernel_value(points[:, 2, :, None] - heights).astype(jnp.bfloat16)
    return (weight_xy, weight_z)


def neighbours(padded):
    centre = padded[1:-1, 1:-1]
    total = padded[2:, 1:-1] + padded[:-2, 1:-1] + padded[1:-1, 2:] + padded[1:-1, :-2]
    zero_edge = jnp.zeros(centre.shape[:2] + (1, centre.shape[3], 1), centre.dtype)
    after = jnp.concatenate([centre[:, :, 1:, :, :1], zero_edge], axis=2)
    before = jnp.concatenate([zero_edge, centre[:, :, :-1, :, -1:]], axis=2)
    upper = jnp.concatenate([centre[..., 1:], after], axis=-1)
    lower = jnp.concatenate([before, centre[..., :-1]], axis=-1)
    return total + upper + lower


def relax(drive, widen):
    state = drive
    for sweep_index in range(SWEEPS):
        state = (drive + coupling * neighbours(widen(state))) / (1.0 + 6.0 * coupling)
    return state


def local(
    velocity_old, traction, offsets, owner_slab, anchor, blocks, block_count, synthesis, analysis
):
    cell_total = traction.shape[0]
    slab_count = lax.axis_size("slab")
    capacity = 2 * cell_total // slab_count
    slot_total = slab_count * capacity
    destination = owner_slab[:, 0]
    member = (destination[:, None] == jnp.arange(slab_count)[None, :]).astype(jnp.int32)
    bucket_rank = jnp.sum((jnp.cumsum(member, axis=0) - member) * member, axis=1)
    slot_index = destination * capacity + bucket_rank

    def placed(values):
        empty = jnp.zeros((slot_total,) + values.shape[1:], values.dtype)
        return empty.at[slot_index].set(values)

    sent_coef, sent_offsets = (
        lax.all_to_all(placed(traction), "slab", split_axis=0, concat_axis=0, tiled=True),
        lax.all_to_all(placed(offsets), "slab", split_axis=0, concat_axis=0, tiled=True),
    )
    sent_anchor, sent_blocks, sent_count = (
        lax.all_to_all(placed(anchor), "slab", split_axis=0, concat_axis=0, tiled=True),
        lax.all_to_all(placed(blocks), "slab", split_axis=0, concat_axis=0, tiled=True),
        lax.all_to_all(placed(block_count), "slab", split_axis=0, concat_axis=0, tiled=True),
    )
    block_rows = 16
    steps_total = slot_total // block_rows

    def grouped(values):
        return values.reshape((steps_total, block_rows) + values.shape[1:])

    received = tuple(
        (
            grouped(values)
            for values in (sent_coef, sent_offsets, sent_anchor, sent_blocks, sent_count)
        )
    )
    layers = NZ // 128

    def spread_step(grid_sum, piece):
        coef_part, offset_part, anchor_part, block_part, count_part = piece
        weight_xy, weight_z = stencil_weights(anchor_part, offset_part, block_part, count_part)
        forces = jnp.einsum("ckl,lq->ckq", coef_part, synthesis, preferred_element_type=jnp.float32)
        weighted = (forces[:, None] * weight_xy[:, :, None]).astype(jnp.bfloat16)
        tile_terms = jnp.einsum(
            "cbkq,cqi->cbki", weighted, weight_z, preferred_element_type=jnp.float32
        )
        return (grid_sum.at[block_part.reshape(-1)].add(tile_terms.reshape(-1, 3, 128)), None)

    start = jnp.zeros((GX * NY * layers, 3, 128), jnp.float32)
    partial_value, ignored = lax.scan(spread_step, start, received)
    partial_value = partial_value.reshape(GX, NY, layers, 3, 128)
    drive = velocity_old + lax.psum_scatter(
        partial_value.astype(jnp.bfloat16), "batch", scatter_dimension=1, tiled=True
    ).astype(jnp.float32)

    def widen(state):
        return padded_2(state.astype(jnp.bfloat16), (("slab", 0), ("batch", 1)), 1).astype(
            state.dtype
        )

    velocity_new = relax(drive, widen)
    slab_velocity = lax.all_gather(velocity_new.astype(jnp.bfloat16), "batch", axis=1, tiled=True)
    flat_velocity = slab_velocity.reshape(-1, 3, 128)

    def sample_step(piece):
        offset_part, anchor_part, block_part, count_part = piece
        weight_xy, weight_z = stencil_weights(anchor_part, offset_part, block_part, count_part)
        gathered = flat_velocity[block_part]
        projected = jnp.einsum(
            "cbki,cqi->cbkq", gathered, weight_z, preferred_element_type=jnp.float32
        )
        return jnp.sum(projected * weight_xy[:, :, None, :], axis=1).astype(jnp.bfloat16)

    sampled = lax.map(sample_step, received[1:])
    sampled = sampled.reshape((slot_total,) + sampled.shape[2:])
    returned = lax.all_to_all(sampled, "slab", split_axis=0, concat_axis=0, tiled=True)
    velocity_coef = jnp.einsum(
        "ckq,lq->ckl", returned[slot_index], analysis, preferred_element_type=jnp.float32
    ).astype(jnp.bfloat16)
    return (velocity_new, velocity_coef)


def solution(mesh):
    in_specs = (
        P("slab", "batch", None, None, None),
        P(("slab", "batch"), None, None),
        P(("slab", "batch"), None, None),
        P(("slab", "batch"), None),
        P(("slab", "batch"), None),
        P(("slab", "batch"), None),
        P(("slab", "batch")),
        P(),
        P(),
    )
    out_specs = (P("slab", "batch", None, None, None), P(("slab", "batch"), None, None))
    return jax.shard_map(local, mesh=mesh, in_specs=in_specs, out_specs=out_specs, check_vma=False)
```

profile of v0, /device:TPU:1, one launch (start us, length us, event | category | flops | bytes accessed | tf_op | source)
XLA Modules:
  0.0 691.6 jit_solution(1177305273273211334)
XLA Ops:
  12.4 13.1 %all-to-all-start.4 = ((s32[64,6,1]{1,2,0:T(1,128)}), s32[64,6,1]{1,2,0:T(1,128)S(1)}, u32[]{:S(2)}, u32[]{:S(2)}) async-start(s32[64,6,1]{1,2,0:T(1,128)} %bitcast.32), calls=%async_computation.4 | async-start | bytes 65536 | tf_op jit(solution)/shard_map/all_to_all | solution.py:95
  28.4 6.4 all-to-all-done.4
  34.8 4.7 all-to-all-start.2
  42.1 7.8 %all-to-all-done.2 = s32[64,6,3]{1,2,0:T(4,128)S(1)} async-done(((s32[64,6,3]{1,2,0:T(4,128)}), s32[64,6,3]{1,2,0:T(4,128)S(1)}, u32[]{:S(2)}, u32[]{:S(2)}) %all-to-all-start.2) | async-done | bytes 4640 | tf_op jit(solution)/shard_map/all_to_all | solution.py:93
  50.0 4.9 all-to-all-start
  55.4 6.2 scatter_fusion.1
  63.3 3.6 all-to-all-done
  66.8 6.8 all-to-all-start.1
  75.3 21.4 %scatter_fusion.2 = bf16[384,3,338]{2,1,0:T(4,128)(2,1)} fusion(bf16[384,3,338]{2,1,0:T(4,128)(2,1)} %broadcast_in_dim.23, s32[192]{0:T(256)S(1)} %bitcast.192, bf16[192,3,338]{2,1,0:T(4,128)(2,1)S(1)} %copy.92), kind=kCustom, calls=%fused_computation.6 | custom fusion | bytes 1168896 | tf_op jit(solution)/shard_map/scatter | solution.py:86
  96.7 10.4 %all-to-all-start.3 = ((bf16[384,3,338]{2,1,0:T(4,128)(2,1)}), bf16[384,3,338]{2,1,0:T(4,128)(2,1)S(1)}, u32[]{:S(2)}, u32[]{:S(2)}) async-start(bf16[384,3,338]{2,1,0:T(4,128)(2,1)} %scatter_fusion.2), calls=%async_computation.3 | async-start | bytes 2359296 | tf_op jit(solution)/shard_map/all_to_all | solution.py:90
  110.7 27.7 %all-to-all-done.3 = bf16[384,3,338]{2,1,0:T(4,128)(2,1)S(1)} async-done(((bf16[384,3,338]{2,1,0:T(4,128)(2,1)}), bf16[384,3,338]{2,1,0:T(4,128)(2,1)S(1)}, u32[]{:S(2)}, u32[]{:S(2)}) %all-to-all-start.3) | async-done | bytes 778784 | tf_op jit(solution)/shard_map/all_to_all | solution.py:90
  139.8 317.2 %while.26 = (s32[]{:T(128)}, f32[1024,3,128]{2,1,0:T(4,128)S(1)}, s32[24,16,16]{2,1,0:T(8,128)S(1)}, bf16[24,16,3,169]{3,1,2,0:T(8,128)(2,1)}, bf16[169,338]{1,0...) while((s32[]{:T(128)}, f32[1024,3,128]{2,1,0:T(4,128)S(1)}, ...), condition=%wide.region_10.11_spmd, body=%wide.region_8.10_spmd.sunk | while | flops 77793472 | bytes 3774449 | solution.py:122
  144.2 8.8 %scatter_fusion = f32[1024,3,128]{2,1,0:T(4,128)S(1)} fusion(f32[1024,3,128]{2,1,0:T(4,128)S(1)} %get-tuple-element.536, s32[256]{0:T(256)S(1)} %bitcast.187, f32[256,3,128]{2,1,0:T(4,128)S(1)} %copy.136), kind=kCustom, calls=%fused_computation.2.clone.1 | custom fusion | flops 98304 | bytes 1180672 | tf_op jit(solution)/shard_map/while/body/eval_jaxpr/scatter-add | solution.py:119
  157.4 8.8 %scatter_fusion = f32[1024,3,128]{2,1,0:T(4,128)S(1)} fusion(f32[1024,3,128]{2,1,0:T(4,128)S(1)} %get-tuple-element.536, s32[256]{0:T(256)S(1)} %bitcast.187, f32[256,3,128]{2,1,0:T(4,128)S(1)} %copy.136), kind=kCustom, calls=%fused_computation.2.clone.1 | custom fusion | flops 98304 | bytes 1180672 | tf_op jit(solution)/shard_map/while/body/eval_jaxpr/scatter-add | solution.py:119
  170.6 8.9 %scatter_fusion = f32[1024,3,128]{2,1,0:T(4,128)S(1)} fusion(f32[1024,3,128]{2,1,0:T(4,128)S(1)} %get-tuple-element.536, s32[256]{0:T(256)S(1)} %bitcast.187, f32[256,3,128]{2,1,0:T(4,128)S(1)} %copy.136), kind=kCustom, calls=%fused_computation.2.clone.1 | custom fusion | flops 98304 | bytes 1180672 | tf_op jit(solution)/shard_map/while/body/eval_jaxpr/scatter-add | solution.py:119
  183.9 8.8 %scatter_fusion = f32[1024,3,128]{2,1,0:T(4,128)S(1)} fusion(f32[1024,3,128]{2,1,0:T(4,128)S(1)} %get-tuple-element.536, s32[256]{0:T(256)S(1)} %bitcast.187, f32[256,3,128]{2,1,0:T(4,128)S(1)} %copy.136), kind=kCustom, calls=%fused_computation.2.clone.1 | custom fusion | flops 98304 | bytes 1180672 | tf_op jit(solution)/shard_map/while/body/eval_jaxpr/scatter-add | solution.py:119
  197.1 8.8 %scatter_fusion = f32[1024,3,128]{2,1,0:T(4,128)S(1)} fusion(f32[1024,3,128]{2,1,0:T(4,128)S(1)} %get-tuple-element.536, s32[256]{0:T(256)S(1)} %bitcast.187, f32[256,3,128]{2,1,0:T(4,128)S(1)} %copy.136), kind=kCustom, calls=%fused_computation.2.clone.1 | custom fusion | flops 98304 | bytes 1180672 | tf_op jit(solution)/shard_map/while/body/eval_jaxpr/scatter-add | solution.py:119
  210.3 8.9 %scatter_fusion = f32[1024,3,128]{2,1,0:T(4,128)S(1)} fusion(f32[1024,3,128]{2,1,0:T(4,128)S(1)} %get-tuple-element.536, s32[256]{0:T(256)S(1)} %bitcast.187, f32[256,3,128]{2,1,0:T(4,128)S(1)} %copy.136), kind=kCustom, calls=%fused_computation.2.clone.1 | custom fusion | flops 98304 | bytes 1180672 | tf_op jit(solution)/shard_map/while/body/eval_jaxpr/scatter-add | solution.py:119
  223.6 8.8 %scatter_fusion = f32[1024,3,128]{2,1,0:T(4,128)S(1)} fusion(f32[1024,3,128]{2,1,0:T(4,128)S(1)} %get-tuple-element.536, s32[256]{0:T(256)S(1)} %bitcast.187, f32[256,3,128]{2,1,0:T(4,128)S(1)} %copy.136), kind=kCustom, calls=%fused_computation.2.clone.1 | custom fusion | flops 98304 | bytes 1180672 | tf_op jit(solution)/shard_map/while/body/eval_jaxpr/scatter-add | solution.py:119
  236.8 8.8 %scatter_fusion = f32[1024,3,128]{2,1,0:T(4,128)S(1)} fusion(f32[1024,3,128]{2,1,0:T(4,128)S(1)} %get-tuple-element.536, s32[256]{0:T(256)S(1)} %bitcast.187, f32[256,3,128]{2,1,0:T(4,128)S(1)} %copy.136), kind=kCustom, calls=%fused_computation.2.clone.1 | custom fusion | flops 98304 | bytes 1180672 | tf_op jit(solution)/shard_map/while/body/eval_jaxpr/scatter-add | solution.py:119
  249.9 8.9 %scatter_fusion = f32[1024,3,128]{2,1,0:T(4,128)S(1)} fusion(f32[1024,3,128]{2,1,0:T(4,128)S(1)} %get-tuple-element.536, s32[256]{0:T(256)S(1)} %bitcast.187, f32[256,3,128]{2,1,0:T(4,128)S(1)} %copy.136), kind=kCustom, calls=%fused_computation.2.clone.1 | custom fusion | flops 98304 | bytes 1180672 | tf_op jit(solution)/shard_map/while/body/eval_jaxpr/scatter-add | solution.py:119
  263.2 8.8 %scatter_fusion = f32[1024,3,128]{2,1,0:T(4,128)S(1)} fusion(f32[1024,3,128]{2,1,0:T(4,128)S(1)} %get-tuple-element.536, s32[256]{0:T(256)S(1)} %bitcast.187, f32[256,3,128]{2,1,0:T(4,128)S(1)} %copy.136), kind=kCustom, calls=%fused_computation.2.clone.1 | custom fusion | flops 98304 | bytes 1180672 | tf_op jit(solution)/shard_map/while/body/eval_jaxpr/scatter-add | solution.py:119
  276.4 8.8 %scatter_fusion = f32[1024,3,128]{2,1,0:T(4,128)S(1)} fusion(f32[1024,3,128]{2,1,0:T(4,128)S(1)} %get-tuple-element.536, s32[256]{0:T(256)S(1)} %bitcast.187, f32[256,3,128]{2,1,0:T(4,128)S(1)} %copy.136), kind=kCustom, calls=%fused_computation.2.clone.1 | custom fusion | flops 98304 | bytes 1180672 | tf_op jit(solution)/shard_map/while/body/eval_jaxpr/scatter-add | solution.py:119
  289.6 8.9 %scatter_fusion = f32[1024,3,128]{2,1,0:T(4,128)S(1)} fusion(f32[1024,3,128]{2,1,0:T(4,128)S(1)} %get-tuple-element.536, s32[256]{0:T(256)S(1)} %bitcast.187, f32[256,3,128]{2,1,0:T(4,128)S(1)} %copy.136), kind=kCustom, calls=%fused_computation.2.clone.1 | custom fusion | flops 98304 | bytes 1180672 | tf_op jit(solution)/shard_map/while/body/eval_jaxpr/scatter-add | solution.py:119
  302.9 8.8 %scatter_fusion = f32[1024,3,128]{2,1,0:T(4,128)S(1)} fusion(f32[1024,3,128]{2,1,0:T(4,128)S(1)} %get-tuple-element.536, s32[256]{0:T(256)S(1)} %bitcast.187, f32[256,3,128]{2,1,0:T(4,128)S(1)} %copy.136), kind=kCustom, calls=%fused_computation.2.clone.1 | custom fusion | flops 98304 | bytes 1180672 | tf_op jit(solution)/shard_map/while/body/eval_jaxpr/scatter-add | solution.py:119
  316.1 8.8 %scatter_fusion = f32[1024,3,128]{2,1,0:T(4,128)S(1)} fusion(f32[1024,3,128]{2,1,0:T(4,128)S(1)} %get-tuple-element.536, s32[256]{0:T(256)S(1)} %bitcast.187, f32[256,3,128]{2,1,0:T(4,128)S(1)} %copy.136), kind=kCustom, calls=%fused_computation.2.clone.1 | custom fusion | flops 98304 | bytes 1180672 | tf_op jit(solution)/shard_map/while/body/eval_jaxpr/scatter-add | solution.py:119
  329.3 8.9 %scatter_fusion = f32[1024,3,128]{2,1,0:T(4,128)S(1)} fusion(f32[1024,3,128]{2,1,0:T(4,128)S(1)} %get-tuple-element.536, s32[256]{0:T(256)S(1)} %bitcast.187, f32[256,3,128]{2,1,0:T(4,128)S(1)} %copy.136), kind=kCustom, calls=%fused_computation.2.clone.1 | custom fusion | flops 98304 | bytes 1180672 | tf_op jit(solution)/shard_map/while/body/eval_jaxpr/scatter-add | solution.py:119
  342.6 8.7 %scatter_fusion = f32[1024,3,128]{2,1,0:T(4,128)S(1)} fusion(f32[1024,3,128]{2,1,0:T(4,128)S(1)} %get-tuple-element.536, s32[256]{0:T(256)S(1)} %bitcast.187, f32[256,3,128]{2,1,0:T(4,128)S(1)} %copy.136), kind=kCustom, calls=%fused_computation.2.clone.1 | custom fusion | flops 98304 | bytes 1180672 | tf_op jit(solution)/shard_map/while/body/eval_jaxpr/scatter-add | solution.py:119
  355.7 8.8 %scatter_fusion = f32[1024,3,128]{2,1,0:T(4,128)S(1)} fusion(f32[1024,3,128]{2,1,0:T(4,128)S(1)} %get-tuple-element.536, s32[256]{0:T(256)S(1)} %bitcast.187, f32[256,3,128]{2,1,0:T(4,128)S(1)} %copy.136), kind=kCustom, calls=%fused_computation.2.clone.1 | custom fusion | flops 98304 | bytes 1180672 | tf_op jit(solution)/shard_map/while/body/eval_jaxpr/scatter-add | solution.py:119
  368.9 8.9 %scatter_fusion = f32[1024,3,128]{2,1,0:T(4,128)S(1)} fusion(f32[1024,3,128]{2,1,0:T(4,128)S(1)} %get-tuple-element.536, s32[256]{0:T(256)S(1)} %bitcast.187, f32[256,3,128]{2,1,0:T(4,128)S(1)} %copy.136), kind=kCustom, calls=%fused_computation.2.clone.1 | custom fusion | flops 98304 | bytes 1180672 | tf_op jit(solution)/shard_map/while/body/eval_jaxpr/scatter-add | solution.py:119
  382.2 8.8 %scatter_fusion = f32[1024,3,128]{2,1,0:T(4,128)S(1)} fusion(f32[1024,3,128]{2,1,0:T(4,128)S(1)} %get-tuple-element.536, s32[256]{0:T(256)S(1)} %bitcast.187, f32[256,3,128]{2,1,0:T(4,128)S(1)} %copy.136), kind=kCustom, calls=%fused_computation.2.clone.1 | custom fusion | flops 98304 | bytes 1180672 | tf_op jit(solution)/shard_map/while/body/eval_jaxpr/scatter-add | solution.py:119
  395.4 8.8 %scatter_fusion = f32[1024,3,128]{2,1,0:T(4,128)S(1)} fusion(f32[1024,3,128]{2,1,0:T(4,128)S(1)} %get-tuple-element.536, s32[256]{0:T(256)S(1)} %bitcast.187, f32[256,3,128]{2,1,0:T(4,128)S(1)} %copy.136), kind=kCustom, calls=%fused_computation.2.clone.1 | custom fusion | flops 98304 | bytes 1180672 | tf_op jit(solution)/shard_map/while/body/eval_jaxpr/scatter-add | solution.py:119
  408.6 8.8 %scatter_fusion = f32[1024,3,128]{2,1,0:T(4,128)S(1)} fusion(f32[1024,3,128]{2,1,0:T(4,128)S(1)} %get-tuple-element.536, s32[256]{0:T(256)S(1)} %bitcast.187, f32[256,3,128]{2,1,0:T(4,128)S(1)} %copy.136), kind=kCustom, calls=%fused_computation.2.clone.1 | custom fusion | flops 98304 | bytes 1180672 | tf_op jit(solution)/shard_map/while/body/eval_jaxpr/scatter-add | solution.py:119
  421.8 8.8 %scatter_fusion = f32[1024,3,128]{2,1,0:T(4,128)S(1)} fusion(f32[1024,3,128]{2,1,0:T(4,128)S(1)} %get-tuple-element.536, s32[256]{0:T(256)S(1)} %bitcast.187, f32[256,3,128]{2,1,0:T(4,128)S(1)} %copy.136), kind=kCustom, calls=%fused_computation.2.clone.1 | custom fusion | flops 98304 | bytes 1180672 | tf_op jit(solution)/shard_map/while/body/eval_jaxpr/scatter-add | solution.py:119
  435.0 8.8 %scatter_fusion = f32[1024,3,128]{2,1,0:T(4,128)S(1)} fusion(f32[1024,3,128]{2,1,0:T(4,128)S(1)} %get-tuple-element.536, s32[256]{0:T(256)S(1)} %bitcast.187, f32[256,3,128]{2,1,0:T(4,128)S(1)} %copy.136), kind=kCustom, calls=%fused_computation.2.clone.1 | custom fusion | flops 98304 | bytes 1180672 | tf_op jit(solution)/shard_map/while/body/eval_jaxpr/scatter-add | solution.py:119
  448.2 8.8 %scatter_fusion = f32[1024,3,128]{2,1,0:T(4,128)S(1)} fusion(f32[1024,3,128]{2,1,0:T(4,128)S(1)} %get-tuple-element.536, s32[256]{0:T(256)S(1)} %bitcast.187, f32[256,3,128]{2,1,0:T(4,128)S(1)} %copy.136), kind=kCustom, calls=%fused_computation.2.clone.1 | custom fusion | flops 98304 | bytes 1180672 | tf_op jit(solution)/shard_map/while/body/eval_jaxpr/scatter-add | solution.py:119
  459.1 19.8 %reduce-scatter.2.cloned.1.call-done = bf16[8,16,2,3,128]{4,0,3,2,1:T(8,128)(2,1)} async-done(((bf16[8,64,2,3,128]{4,0,3,2,1:T(8,128)(2,1)}), bf16[8,16,2,3,128]{4,0,3,2,1:T(8,128)(2,1)}) %reduce-scatter.2.cloned.1.call-update) | async-done | bytes 196624 | tf_op jit(solution)/shard_map/reduce_scatter | solution.py:124
  480.2 5.9 collective-permute-start
  488.0 3.5 collective-permute-done.1
  494.1 3.3 collective-permute-done.3
  498.5 3.0 collective-permute-start.4
  503.5 3.5 collective-permute-done.5
  507.0 3.6 collective-permute-start.6
  511.9 3.3 collective-permute-done.7
  516.2 12.8 %all_gather.3 = bf16[8,64,2,3,128]{4,0,3,2,1:T(8,128)(2,1)S(1)} all-gather(bf16[8,16,2,3,128]{4,0,3,2,1:T(8,128)(2,1)S(1)} %get-tuple-element.382), channel_id=1, replica_groups=mesh['slab'=64,'batch'=4] {'batch'}, dimensions={1}, use_global_device_ids=true | all-gather | bytes 983040 | tf_op jit(solution)/shard_map/all_gather | solution.py:134
  530.4 107.3 %while.27 = (s32[]{:T(128)}, bf16[24,16,3,338]{3,2,1,0:T(4,128)(2,1)}, s32[24,16,16]{2,1,0:T(8,128)S(1)}, bf16[1024,3,128]{2,1,0:T(4,128)(2,1)S(1)}, s32[24,16,3...) while((s32[]{:T(128)}, ...), condition=%wide.region_14.15_spmd, body=%wide.region_12.14_spmd.sunk | while | flops 72195744 | bytes 1725229 | solution.py:146
  637.8 13.3 %all-to-all-start.5 = ((bf16[384,3,338]{2,1,0:T(4,128)(2,1)}), bf16[384,3,338]{2,1,0:T(4,128)(2,1)S(1)}, u32[]{:S(2)}, u32[]{:S(2)}) async-start(bf16[384,3,338]{2,1,0:T(4,128)(2,1)} %bitcast.35), calls=%async_computation.6 | async-start | bytes 2359296 | tf_op jit(solution)/shard_map/all_to_all | solution.py:148
  652.1 30.4 %all-to-all-done.5 = bf16[384,3,338]{2,1,0:T(4,128)(2,1)S(1)} async-done(((bf16[384,3,338]{2,1,0:T(4,128)(2,1)}), bf16[384,3,338]{2,1,0:T(4,128)(2,1)S(1)}, u32[]{:S(2)}, u32[]{:S(2)}) %all-to-all-start.5) | async-done | bytes 778784 | tf_op jit(solution)/shard_map/all_to_all | solution.py:148
  (850 shorter events, 246.6 us)
Async XLA Ops:
  7.2 676.5 %copy-start = (bf16[169,338]{1,0:T(8,128)(2,1)S(1)}, bf16[169,338]{1,0:T(8,128)(2,1)}, u32[]{:S(2)}) copy-start(bf16[169,338]{1,0:T(8,128)(2,1)} %param.21) | copy-start | bytes 342736
  7.2 47.7 %copy-start.5 = (bf16[192,3,169]{0,2,1:T(8,128)(2,1)S(1)}, bf16[192,3,169]{0,2,1:T(8,128)(2,1)}, u32[]{:S(2)}) copy-start(bf16[192,3,169]{0,2,1:T(8,128)(2,1)} %param.14) | copy-start | bytes 584068
  12.4 22.4 %all-to-all-start.4 = ((s32[64,6,1]{1,2,0:T(1,128)}), s32[64,6,1]{1,2,0:T(1,128)S(1)}, u32[]{:S(2)}, u32[]{:S(2)}) async-start(s32[64,6,1]{1,2,0:T(1,128)} %bitcast.32), calls=%async_computation.4 | async-start | bytes 65536 | tf_op jit(solution)/shard_map/all_to_all | solution.py:95
  34.8 15.2 %all-to-all-start.2 = ((s32[64,6,3]{1,2,0:T(4,128)}), s32[64,6,3]{1,2,0:T(4,128)S(1)}, u32[]{:S(2)}, u32[]{:S(2)}) async-start(s32[64,6,3]{1,2,0:T(4,128)} %copy.90), calls=%async_computation.2 | async-start | bytes 262144 | tf_op jit(solution)/shard_map/all_to_all | solution.py:93
  50.0 16.9 %all-to-all-start = ((s32[64,6,16]{2,1,0:T(8,128)}), s32[64,6,16]{2,1,0:T(8,128)S(1)}, u32[]{:S(2)}, u32[]{:S(2)}) async-start(s32[64,6,16]{2,1,0:T(8,128)} %all_to_all.27), calls=%async_computation | async-start | bytes 524288 | tf_op jit(solution)/shard_map/all_to_all | solution.py:94
  55.1 18.5 %copy-start.4 = (bf16[192,3,338]{2,0,1:T(8,128)(2,1)S(1)}, bf16[192,3,338]{2,0,1:T(8,128)(2,1)}, u32[]{:S(2)}) copy-start(bf16[192,3,338]{2,0,1:T(8,128)(2,1)} %param.15) | copy-start | bytes 1168132
  66.8 29.9 %all-to-all-start.1 = ((bf16[64,2,1521]{2,1,0:T(2,128)(2,1)}), bf16[64,2,1521]{2,1,0:T(2,128)(2,1)S(1)}, u32[]{:S(2)}, u32[]{:S(2)}) async-start(bf16[64,2,1521]{2,1,0:T(2,128)(2,1)} %reshape.637), calls=%async_computation.1 | async-start | bytes 786432 | tf_op jit(solution)/shard_map/all_to_all | solution.py:89
  96.7 41.7 %all-to-all-start.3 = ((bf16[384,3,338]{2,1,0:T(4,128)(2,1)}), bf16[384,3,338]{2,1,0:T(4,128)(2,1)S(1)}, u32[]{:S(2)}, u32[]{:S(2)}) async-start(bf16[384,3,338]{2,1,0:T(4,128)(2,1)} %scatter_fusion.2), calls=%async_computation.3 | async-start | bytes 2359296 | tf_op jit(solution)/shard_map/all_to_all | solution.py:90
  107.1 371.8 %reduce-scatter.2.cloned.1.call-start = ((), (), s32[]{:S(2)}) async-start(), calls=%async_computation.7 | async-start | bytes 983040 | tf_op jit(solution)/shard_map/reduce_scatter | solution.py:124
  138.5 1.3 copy-start.2
  457.1 21.8 %copy-start.1 = (f32[8,16,2,3,128]{4,2,3,1,0:T(2,128)S(1)}, f32[8,16,2,3,128]{4,2,3,1,0:T(2,128)}, u32[]{:S(2)}) copy-start(f32[8,16,2,3,128]{4,2,3,1,0:T(2,128)} %param.13) | copy-start | bytes 1179652
  480.1 17.8 %copy-start.3 = (bf16[8,16,2,3,128]{4,0,3,2,1:T(8,128)(2,1)S(1)}, bf16[8,16,2,3,128]{4,0,3,2,1:T(8,128)(2,1)}, u32[]{:S(2)}) copy-start(bf16[8,16,2,3,128]{4,0,3,2,1:T(8,128)(2,1)} %reduce-scatter.2.cloned.1.call-done) | copy-start | bytes 589828
  480.2 7.8 %collective-permute-start = (bf16[1,16,2,3,128]{4,0,3,2,1:T(2,128)(2,1)S(1)}, bf16[1,16,2,3,128]{4,0,3,2,1:T(2,128)(2,1)S(1)}, u32[]{:S(2)}, u32[]{:S(2)}) collective-permute-start(bf16[1,16,2,3,128]{4,0,3,2,1:T(2,128)(2,1)S(1)} %get-tuple-element.404), channel_id=1, source_target_pairs={{0,4},{4,8},{8,12},{12,16},{16,20},{20,24},{24,28},{28,32},{32,36}... | collective-permute-start | bytes 73736 | tf_op jit(solution)/shard_map/ppermute | solution.py:24
  486.1 5.4 collective-permute-start.1
  491.5 2.6 collective-permute-start.2
  492.8 4.6 collective-permute-start.3
  498.5 5.0 collective-permute-start.4
  501.5 5.4 collective-permute-start.5
  507.0 5.0 collective-permute-start.6
  510.6 4.6 collective-permute-start.7
  637.8 44.7 %all-to-all-start.5 = ((bf16[384,3,338]{2,1,0:T(4,128)(2,1)}), bf16[384,3,338]{2,1,0:T(4,128)(2,1)S(1)}, u32[]{:S(2)}, u32[]{:S(2)}) async-start(bf16[384,3,338]{2,1,0:T(4,128)(2,1)} %bitcast.35), calls=%async_computation.6 | async-start | bytes 2359296 | tf_op jit(solution)/shard_map/all_to_all | solution.py:148
Sparse Core Ops, SparseCore 0:
  459.2 19.6 reduce-scatter.1
where the time goes:
time: 697 us; the launch traced here: 692 us
  other arithmetic  282 us (40%)
  waiting for transfers between devices  109 us (16%)
  local copies, waits for them, and re-layouts  101 us (14%)
  matrix products  94.4 us (14%)
  starting transfers between devices  73.7 us (11%)
  between operations  14.5 us (2%)
  blocking collectives  12.8 us (2%)
    scatter-add x24, other arithmetic, spread_step(): grid_sum.at[block_part.reshape(-1)].add(tile_terms.reshape(-1, 3, 128))  212 us
    add x48, other arithmetic, stencil_weights(): anchor_part[:, :, None].astype(jnp.float32)  40.7 us
    dot_general x24, matrix products, spread_step(): jnp.einsum('cbkq,cqi->cbki', weighted, weight_z, preferred_element_type=j...  40.2 us
    dot_general x24, matrix products, sample_step(): jnp.einsum('cbki,cqi->cbkq', gathered, weight_z, preferred_element_type=j...  32.1 us
    scatter x6, local copies, waits for them, and re-layouts, placed(): return empty.at[slot_index].set(values)  31.1 us
    all_to_all x1, waiting for transfers between devices, local(): lax.all_to_all(sampled, 'slab', split_axis=0, concat_axis=0, tiled=True)  30.4 us
    all_to_all x1, waiting for transfers between devices, local(): lax.all_to_all(placed(offsets), 'slab', split_axis=0, concat_axis=0, tile...  27.7 us
    gather x24, local copies, waits for them, and re-layouts, sample_step(): gathered = flat_velocity[block_part]  23.6 us
  transfers between devices with their start and end apart: 15, of which 10 were waited for; matrix products, arithmetic and copies ran while one was open for 6% of the time, Pallas kernels for 0%

commit v1 on v0

v1 whole, which is shorter than its diff:
```python
import math

import jax
import jax.numpy as jnp
from jax import lax
from jax.experimental import pallas as pl
from jax.experimental.pallas import tpu as pltpu
from jax.sharding import PartitionSpec as P

SWEEPS = 2
GX = 8
NY = 64
NZ = 256
LAYERS = NZ // 128

L = 169
Q = 338
B = 16
REM = L - 128

CAP = 6
PLANES = 13
OUT_PLANES = 4
QP = 384

TILES = GX * NY * LAYERS
ROWS = TILES * 3
DUMMY = ROWS

kernel_width = 0.8
coupling = 2.0
SCALE = math.sqrt(0.5 * math.log2(math.e)) / kernel_width
LOG_NORM = -math.log2(0.8 * math.sqrt(2.0 * math.pi))
FAR = 1.0e4

F32 = jnp.float32
BF16 = jnp.bfloat16
NT = (((1,), (1,)), ((), ()))
NN = (((1,), (0,)), ((), ()))
TN = (((0,), (0,)), ((), ()))

VMEM_SPEC = pl.BlockSpec(memory_space=pltpu.VMEM)
ANY_SPEC = pl.BlockSpec(memory_space=pl.ANY)


def dot(a, b, dims):
    return lax.dot_general(a, b, dims, preferred_element_type=F32)


def slot_onehot(row_ref, col_ref, slots):
    cells = row_ref.shape[1]
    row, col = row_ref[...], col_ref[...]
    before = lax.broadcasted_iota(jnp.int32, (cells, cells), 0) < lax.broadcasted_iota(
        jnp.int32, (cells, cells), 1
    )
    same = jnp.where((col == row) & before, 1.0, 0.0)
    rank = jnp.sum(same, axis=0, keepdims=True)
    slot = row * CAP + rank.astype(jnp.int32)
    at = lax.broadcasted_iota(jnp.int32, (slots, cells), 0)
    return jnp.where(at == slot, 1.0, 0.0).astype(BF16)


def pack_kernel(row_ref, col_ref, coef_ref, offs_ref, ints_ref, out_ref, x_ref, blk_ref):
    slab_count = out_ref.shape[0]
    slots = slab_count * CAP
    hot = slot_onehot(row_ref, col_ref, slots)
    for r in range(4):
        x_ref[r] = dot(hot, coef_ref[r], NT)
    tail = jnp.zeros((slots, QP - Q), F32)
    for k in range(3):
        got = dot(hot, offs_ref[k], NN)
        x_ref[4 + 3 * k] = got[:, :128]
        x_ref[5 + 3 * k] = got[:, 128:256]
        x_ref[6 + 3 * k] = jnp.concatenate([got[:, 256:], tail], axis=1) + dot(
            hot, ints_ref[k], NT
        )

    def step(target, carry):
        for r in range(PLANES):
            blk_ref[pl.ds(r * CAP, CAP), :] = x_ref[r, pl.ds(target * CAP, CAP), :]
        out_ref[target] = blk_ref[...].astype(BF16)
        return carry

    blk_ref[...] = jnp.zeros_like(blk_ref)
    lax.fori_loop(0, slab_count, step, 0)


def pack(row, col, coef_t, offs, ints_t, slab_count):
    block_rows = -(-PLANES * CAP // 16) * 16
    return pl.pallas_call(
        pack_kernel,
        out_shape=jax.ShapeDtypeStruct((slab_count, block_rows, 128), BF16),
        in_specs=[VMEM_SPEC] * 5,
        out_specs=VMEM_SPEC,
        scratch_shapes=[
            pltpu.VMEM((PLANES, slab_count * CAP, 128), F32),
            pltpu.VMEM((block_rows, 128), F32),
        ],
        name="pack",
    )(row, col, coef_t, offs, ints_t)


def unpack_kernel(row_ref, col_ref, back_ref, out_ref, blk_ref, r_ref):
    slab_count = back_ref.shape[0]
    slots = slab_count * CAP
    hot = slot_onehot(row_ref, col_ref, slots)

    def step(source, carry):
        blk_ref[...] = back_ref[source].astype(F32)
        for r in range(OUT_PLANES):
            r_ref[r, pl.ds(source * CAP, CAP), :] = blk_ref[pl.ds(r * CAP, CAP), :]
        return carry

    lax.fori_loop(0, slab_count, step, 0)
    rem = dot(r_ref[3].astype(BF16), hot, TN)
    for k in range(3):
        main = dot(r_ref[k].astype(BF16), hot, TN)
        out_ref[k] = jnp.concatenate([main, rem[k * REM : (k + 1) * REM]], axis=0).astype(BF16)


def unpack(row, col, back):
    slab_count, block_rows, _ = back.shape
    cells = row.shape[1]
    return pl.pallas_call(
        unpack_kernel,
        out_shape=jax.ShapeDtypeStruct((3, L, cells), BF16),
        in_specs=[VMEM_SPEC] * 3,
        out_specs=VMEM_SPEC,
        scratch_shapes=[
            pltpu.VMEM((block_rows, 128), F32),
            pltpu.VMEM((OUT_PLANES, slab_count * CAP, 128), F32),
        ],
        name="unpack",
    )(row, col, back)


def exchange_kernel(x_ref, out_ref, send_sem, recv_sem, local_sem):
    count = x_ref.shape[0]
    me = lax.axis_index("slab")
    barrier = pltpu.get_barrier_semaphore()

    def peer_of(step):
        y = (me // 16 + step // 16) % 4
        z = (me // 2 % 8 + step // 2 % 8) % 8
        core = (me % 2 + step % 2) % 2
        return y * 16 + z * 2 + core

    def greet(step, carry):
        pl.semaphore_signal(
            barrier, inc=1, device_id={"slab": peer_of(step)},
            device_id_type=pl.DeviceIdType.MESH,
        )
        return carry

    lax.fori_loop(1, count, greet, 0)
    pl.semaphore_wait(barrier, count - 1)

    def send(step, carry):
        peer = peer_of(step)
        pltpu.make_async_remote_copy(
            src_ref=x_ref.at[peer],
            dst_ref=out_ref.at[me],
            send_sem=send_sem,
            recv_sem=recv_sem,
            device_id={"slab": peer},
            device_id_type=pl.DeviceIdType.MESH,
        ).start()
        return carry

    lax.fori_loop(1, count, send, 0)
    own = pltpu.make_async_copy(x_ref.at[me], out_ref.at[me], local_sem)
    own.start()
    own.wait()
    others = pl.ds(0, count - 1)
    pltpu.make_async_copy(x_ref.at[others], x_ref.at[others], send_sem).wait()
    pltpu.make_async_copy(out_ref.at[others], out_ref.at[others], recv_sem).wait()


def exchange(x, collective_id):
    return pl.pallas_call(
        exchange_kernel,
        out_shape=jax.ShapeDtypeStruct(x.shape, x.dtype),
        in_specs=[ANY_SPEC],
        out_specs=ANY_SPEC,
        scratch_shapes=[pltpu.SemaphoreType.DMA] * 3,
        compiler_params=pltpu.CompilerParams(collective_id=collective_id, has_side_effects=True),
        name="exchange",
    )(x)


def z_weights(pz):
    step = lax.broadcasted_iota(jnp.int32, (8, QP), 0).astype(F32) * SCALE
    base = pz - step
    parts = []
    for g in range(16):
        d = base - (8.0 * g * SCALE)
        parts.append(jnp.exp2(LOG_NORM - d * d))
    return jnp.concatenate(parts, axis=0).astype(BF16)


def xy_weights(px, py, tx, ty):
    dx = px - tx
    dy = py - ty
    return jnp.exp2(2.0 * LOG_NORM - (dx * dx + dy * dy))


def prepare_kernel_part(recv_ref, blk_ref, r_ref, p_ref, tx_ref, ty_ref, idx_ref):
    slab_count = recv_ref.shape[0]

    def step(source, carry):
        blk_ref[...] = recv_ref[source].astype(F32)
        for r in range(PLANES):
            r_ref[r, pl.ds(source * CAP, CAP), :] = blk_ref[pl.ds(r * CAP, CAP), :]
        return carry

    lax.fori_loop(0, slab_count, step, 0)
    line = lax.broadcasted_iota(jnp.int32, (B, 128), 0)
    for m in range(tx_ref.shape[0]):
        rows = pl.ds(m * 128, 128)
        for k in range(3):
            anchor = r_ref[6 + 3 * k, rows, :][:, 112:113]
            for t in range(3):
                p_ref[k, rows, pl.ds(t * 128, 128)] = (
                    r_ref[4 + 3 * k + t, rows, :] + anchor
                ) * SCALE
        first = jnp.transpose(r_ref[6, rows, :])
        second = jnp.transpose(r_ref[9, rows, :])
        x = first[96:112]
        live = line.astype(F32) < first[113:114]
        v = second[96:112]
        y = jnp.floor(v * 0.5)
        tx_ref[m] = jnp.where(live, x * SCALE, FAR)
        ty_ref[m] = y * SCALE
        row = (x * NY + y) * (3 * LAYERS) + (v - 2.0 * y)
        idx_ref[m] = jnp.where(live, row.astype(jnp.int32), DUMMY + 8 * line)


def group_columns(tx_ref, ty_ref, g):
    m = g // 16
    shift = (128 - (g % 16) * 8) % 128
    return pltpu.roll(tx_ref[m], shift, 1), pltpu.roll(ty_ref[m], shift, 1)


def spread_kernel(
    recv_ref, syn_ref, out_ref, p_ref, tx_ref, ty_ref, idx_ref,
    blk_ref, r_ref, f_ref, acc_ref, t_ref, idx_smem,
):
    prepare_kernel_part(recv_ref, blk_ref, r_ref, p_ref, tx_ref, ty_ref, idx_ref)
    pltpu.sync_copy(idx_ref, idx_smem)
    for k in range(3):
        coef = jnp.concatenate([r_ref[k], r_ref[3]], axis=1).astype(BF16)
        f_ref[k] = dot(coef, syn_ref[k], NN)
    acc_ref[...] = jnp.zeros_like(acc_ref)

    def group(g, carry):
        txs, tys = group_columns(tx_ref, ty_ref, g)
        for u in range(8):
            c = g * 8 + u
            wxy = xy_weights(
                p_ref[0, pl.ds(c, 1), :], p_ref[1, pl.ds(c, 1), :],
                txs[:, u : u + 1], tys[:, u : u + 1],
            )
            weighted = jnp.concatenate(
                [wxy * f_ref[k, pl.ds(c, 1), :] for k in range(3)], axis=0
            ).astype(BF16)
            wz = z_weights(p_ref[2, pl.ds(c, 1), :])
            t_ref[u] = dot(weighted, wz, NT)
        for u in range(8):
            m, lane = g // 16, (g % 16) * 8 + u
            starts = [idx_smem[m, j, lane] for j in range(B)]
            sums = [
                acc_ref[pl.ds(starts[j], 3, stride=2), :] + t_ref[u, pl.ds(j, 3, stride=B), :]
                for j in range(B)
            ]
            for j in range(B):
                acc_ref[pl.ds(starts[j], 3, stride=2), :] = sums[j]
        return carry

    lax.fori_loop(0, recv_ref.shape[0] * CAP // 8, group, 0)
    out_ref[...] = acc_ref[:ROWS, :].astype(BF16)


def spread(recv, syn):
    slab_count, block_rows, _ = recv.shape
    slots = slab_count * CAP
    chunks = slots // 128
    return pl.pallas_call(
        spread_kernel,
        out_shape=(
            jax.ShapeDtypeStruct((ROWS, 128), BF16),
            jax.ShapeDtypeStruct((3, slots, QP), F32),
            jax.ShapeDtypeStruct((chunks, B, 128), F32),
            jax.ShapeDtypeStruct((chunks, B, 128), F32),
            jax.ShapeDtypeStruct((chunks, B, 128), jnp.int32),
        ),
        in_specs=[VMEM_SPEC] * 2,
        out_specs=(VMEM_SPEC,) * 5,
        scratch_shapes=[
            pltpu.VMEM((block_rows, 128), F32),
            pltpu.VMEM((PLANES, slots, 128), F32),
            pltpu.VMEM((3, slots, QP), F32),
            pltpu.VMEM((ROWS + 8 * B, 128), F32),
            pltpu.VMEM((8, 3 * B, 128), F32),
            pltpu.SMEM((chunks, B, 128), jnp.int32),
        ],
        name="spread",
    )(recv, syn)


def sample_kernel(
    vel_ref, p_ref, tx_ref, ty_ref, idx_smem, ana_ref, out_ref,
    v_ref, g_ref, pv_ref, c_ref, blk_ref,
):
    v_ref[:ROWS, :] = vel_ref[...].astype(F32)
    v_ref[ROWS:, :] = jnp.zeros((v_ref.shape[0] - ROWS, 128), F32)
    slots = p_ref.shape[1]

    def group(g, carry):
        txs, tys = group_columns(tx_ref, ty_ref, g)
        for u in range(8):
            m, lane = g // 16, (g % 16) * 8 + u
            for j in range(B):
                start = idx_smem[m, j, lane]
                g_ref[u, pl.ds(j, 3, stride=B), :] = v_ref[pl.ds(start, 3, stride=2), :]
        for u in range(8):
            c = g * 8 + u
            wxy = xy_weights(
                p_ref[0, pl.ds(c, 1), :], p_ref[1, pl.ds(c, 1), :],
                txs[:, u : u + 1], tys[:, u : u + 1],
            )
            wz = z_weights(p_ref[2, pl.ds(c, 1), :])
            projected = dot(g_ref[u].astype(BF16), wz, NN)
            for k in range(3):
                pv_ref[k, pl.ds(c, 1), :] = jnp.sum(
                    projected[k * B : (k + 1) * B] * wxy, axis=0, keepdims=True
                )
        return carry

    lax.fori_loop(0, slots // 8, group, 0)
    rem = jnp.zeros((slots, 128), F32)
    for k in range(3):
        got = dot(pv_ref[k].astype(BF16), ana_ref[k], NN)
        c_ref[k] = got[:, :128]
        rem = rem + got[:, 128:]
    c_ref[3] = rem

    def step(target, carry):
        for r in range(OUT_PLANES):
            blk_ref[pl.ds(r * CAP, CAP), :] = c_ref[r, pl.ds(target * CAP, CAP), :]
        out_ref[target] = blk_ref[...].astype(BF16)
        return carry

    lax.fori_loop(0, out_ref.shape[0], step, 0)


def sample(vel, p, tx, ty, idx, ana, slab_count):
    slots = p.shape[1]
    block_rows = OUT_PLANES * CAP
    return pl.pallas_call(
        sample_kernel,
        out_shape=jax.ShapeDtypeStruct((slab_count, block_rows, 128), BF16),
        in_specs=[VMEM_SPEC] * 4 + [pl.BlockSpec(memory_space=pltpu.SMEM), VMEM_SPEC],
        out_specs=VMEM_SPEC,
        scratch_shapes=[
            pltpu.VMEM((ROWS + 8 * B, 128), F32),
            pltpu.VMEM((8, 3 * B, 128), F32),
            pltpu.VMEM((3, slots, QP), F32),
            pltpu.VMEM((OUT_PLANES, slots, 128), F32),
            pltpu.VMEM((block_rows, 128), F32),
        ],
        name="sample",
    )(vel, p, tx, ty, idx, ana)


def padded_2(block, sides, width):
    for axis, dim in sides:
        count = lax.axis_size(axis)
        forward = [(i, i + 1) for i in range(count - 1)]
        backward = [(target, source) for source, target in forward]
        low = lax.ppermute(
            lax.slice_in_dim(block, block.shape[dim] - width, None, axis=dim), axis, forward
        )
        high = lax.ppermute(lax.slice_in_dim(block, 0, width, axis=dim), axis, backward)
        block = jnp.concatenate([low, block, high], axis=dim)
    return block


def neighbours(padded):
    centre = padded[1:-1, 1:-1]
    total = padded[2:, 1:-1] + padded[:-2, 1:-1] + padded[1:-1, 2:] + padded[1:-1, :-2]
    zero_edge = jnp.zeros(centre.shape[:3] + (1, 1), centre.dtype)
    after = jnp.concatenate([centre[:, :, :, 1:, :1], zero_edge], axis=3)
    before = jnp.concatenate([zero_edge, centre[:, :, :, :-1, -1:]], axis=3)
    upper = jnp.concatenate([centre[..., 1:], after], axis=-1)
    lower = jnp.concatenate([before, centre[..., :-1]], axis=-1)
    return total + upper + lower


def relax(drive, widen):
    state = drive
    for sweep_index in range(SWEEPS):
        state = (drive + coupling * neighbours(widen(state))) / (1.0 + 6.0 * coupling)
    return state


def coef_planes(values):
    n = values.shape[2]
    rest = jnp.concatenate(
        [values[0, 128:], values[1, 128:], values[2, 128:], jnp.zeros((128 - 3 * REM, n), values.dtype)],
        axis=0,
    )
    return jnp.concatenate([values[:, :128], rest[None]], axis=0)


def basis_planes(basis):
    wide = jnp.pad(basis, ((0, 0), (0, QP - Q)))
    return jnp.stack(
        [
            jnp.concatenate(
                [wide[:128], jnp.pad(wide[128:], ((k * REM, 128 - (k + 1) * REM), (0, 0)))], axis=0
            )
            for k in range(3)
        ]
    )


def int_planes(anchor, blocks, count):
    cells = count.shape[0]
    anchor_t, blocks_t = anchor.T, blocks.T
    width = NY * LAYERS
    lists = (blocks_t // width, blocks_t % width, jnp.zeros_like(blocks_t))
    places = (anchor_t[0:1], anchor_t[1:2], anchor_t[2:3] % 128)
    planes = []
    for k in range(3):
        rows = [
            jnp.zeros((96, cells), jnp.int32), lists[k], places[k], count[None],
            jnp.zeros((14, cells), jnp.int32),
        ]
        planes.append(jnp.concatenate(rows, axis=0))
    return jnp.stack(planes).astype(BF16)


def local(
    velocity_old, traction, offsets, owner_slab, anchor, blocks, block_count, synthesis, analysis
):
    slab_count = lax.axis_size("slab")
    row = owner_slab[:, 0][None, :]
    sent = pack(
        row,
        owner_slab,
        coef_planes(traction.transpose(1, 2, 0)),
        offsets.transpose(1, 0, 2),
        int_planes(anchor, blocks, block_count),
        slab_count,
    )
    received = exchange(sent, 0)
    partial_value, p, tx, ty, idx = spread(received, basis_planes(synthesis))
    partial_value = partial_value.reshape(GX, NY, 3, LAYERS, 128)
    drive = velocity_old.transpose(0, 1, 3, 2, 4) + lax.psum_scatter(
        partial_value, "batch", scatter_dimension=1, tiled=True
    ).astype(F32)

    def widen(state):
        return padded_2(state.astype(BF16), (("slab", 0), ("batch", 1)), 1).astype(state.dtype)

    velocity_new = relax(drive, widen)
    slab_velocity = lax.all_gather(velocity_new.astype(BF16), "batch", axis=1, tiled=True)
    coefs = sample(
        slab_velocity.reshape(ROWS, 128), p, tx, ty, idx,
        basis_planes(analysis).transpose(0, 2, 1), slab_count,
    )
    velocity_coef = unpack(row, owner_slab, exchange(coefs, 1))
    return (velocity_new.transpose(0, 1, 3, 2, 4), velocity_coef.transpose(2, 0, 1))


def solution(mesh):
    in_specs = (
        P("slab", "batch", None, None, None),
        P(("slab", "batch"), None, None),
        P(("slab", "batch"), None, None),
        P(("slab", "batch"), None),
        P(("slab", "batch"), None),
        P(("slab", "batch"), None),
        P(("slab", "batch")),
        P(),
        P(),
    )
    out_specs = (P("slab", "batch", None, None, None), P(("slab", "batch"), None, None))
    return jax.shard_map(local, mesh=mesh, in_specs=in_specs, out_specs=out_specs, check_vma=False)
```

time: 697 us -> 247 us (0.35)
  other arithmetic: 282 us -> 8.97 us
  Pallas kernels: 0 us -> 143 us
  matrix products: 94.4 us -> 0 us
  local copies, waits for them, and re-layouts: 101 us -> 12.4 us
  waiting for transfers between devices: 109 us -> 34.8 us
  starting transfers between devices: 73.7 us -> 20.4 us
    scatter-add x24 -> x0, other arithmetic: 212 us -> none  [spread_step(): grid_sum.at[block_part.reshape(-1)].add(tile_terms.reshape(-1, 3, 128))]
    pallas_call x0 -> x6, Pallas kernels: none -> 143 us  [the longest x2 67.1 us: exchange(): pl.pallas_call(exchange_kernel, out_shape=jax.ShapeDtypeStruct(x.shape, x...]
    dot_general x73 -> x0, matrix products: 94.4 us -> none  [the longest x24 40.2 us: spread_step(): jnp.einsum('cbkq,cqi->cbki', weighted, weight_z, preferred_element_type=j...]
    all_to_all x6 -> x0, waiting for transfers between devices: 75.8 us -> none  [the longest x1 30.4 us: local(): lax.all_to_all(sampled, 'slab', split_axis=0, concat_axis=0, tiled=True)]
    all_to_all x6 -> x0, starting transfers between devices: 53.2 us -> none  [the longest x1 13.3 us: local(): lax.all_to_all(sampled, 'slab', split_axis=0, concat_axis=0, tiled=True)]
    add x96 -> x0, other arithmetic: 44.2 us -> none  [the longest x48 40.7 us: stencil_weights(): anchor_part[:, :, None].astype(jnp.float32)]
    scatter x6 -> x0, local copies, waits for them, and re-layouts: 31.1 us -> none  [placed(): return empty.at[slot_index].set(values)]
    gather x25 -> x0, local copies, waits for them, and re-layouts: 24.8 us -> none  [the longest x24 23.6 us: sample_step(): gathered = flat_velocity[block_part]]
  transfers between devices with their start and end apart: 15 -> 9, of which waited for: 10 -> 5; matrix products, arithmetic and copies ran while one was open for 6% -> 0% of each run, Pallas kernels for 0% -> 0%
where the time goes in v1:
time: 247 us; the launch traced here: 246 us
  Pallas kernels  143 us (58%)
  waiting for transfers between devices  34.8 us (14%)
  starting transfers between devices  20.4 us (8%)
  between operations  14.3 us (6%)
  blocking collectives  12.8 us (5%)
  local copies, waits for them, and re-layouts  12.4 us (5%)
  other arithmetic  8.97 us (4%)
    pallas_call x2, Pallas kernels, exchange(): pl.pallas_call(exchange_kernel, out_shape=jax.ShapeDtypeStruct(x.shape, x...  67.1 us
    pallas_call x1, Pallas kernels, spread(): pl.pallas_call(spread_kernel, out_shape=(jax.ShapeDtypeStruct((ROWS, 128)...  37.6 us
    pallas_call x1, Pallas kernels, sample(): pl.pallas_call(sample_kernel, out_shape=jax.ShapeDtypeStruct((slab_count,...  31 us
    reduce_scatter x1, waiting for transfers between devices, local(): lax.psum_scatter(partial_value, 'batch', scatter_dimension=1, tiled=True)  22.4 us
    ppermute x4, starting transfers between devices, padded_2(): lax.ppermute(lax.slice_in_dim(block, block.shape[dim] - width, None, axis...  13.9 us
    all_gather x1, blocking collectives, local(): lax.all_gather(velocity_new.astype(BF16), 'batch', axis=1, tiled=True)  12.8 us
    ppermute x4, waiting for transfers between devices, padded_2(): lax.ppermute(lax.slice_in_dim(block, 0, width, axis=dim), axis, backward)  12.4 us
    ppermute x4, starting transfers between devices, padded_2(): lax.ppermute(lax.slice_in_dim(block, 0, width, axis=dim), axis, backward)  6.43 us
  transfers between devices with their start and end apart: 9, of which 5 were waited for; matrix products, arithmetic and copies ran while one was open for 0% of the time, Pallas kernels for 0%

profile of v1, /device:TPU:1, one launch (start us, length us, event | category | flops | bytes accessed | tf_op | source)
XLA Modules:
  0.0 246.5 jit_solution(18202657414320182079)
XLA Ops:
  7.2 0.8 slice_bitcast_fusion.2
  8.0 0.9 slice.160
  8.9 0.9 pad_slice_fusion.3
  9.8 0.8 pad_slice_fusion.2
  10.6 0.7 convert.45
  11.3 0.7 fusion.24
  12.1 0.7 bitcast_convert_fusion
  12.8 0.7 fusion.29
  13.5 1.4 copy.22.col_ref
  14.9 0.2 concatenate.74
  15.1 0.2 concatenate.75
  15.2 0.2 concatenate.76
  15.6 0.8 pad_maximum_fusion.1.coef_ref
  16.3 0.7 pad_maximum_fusion.8.ints_ref
  17.0 4.3 %pack.1.x_ref = bf16[64,80,128]{2,1,0:T(8,128)(2,1)} custom-call(s32[1,192]{1,0:T(1,128)} %bitcast.79, s32[192,1]{1,0:T(8,128)} %copy.22.col_ref, bf16[4,128,192]{2,1,0:T(8,128)(2,1)} %pad_maximum_fusion.1.coef_ref, bf16[3,192,338]{2,1,0:T(8,128)(2,1)} %bitcast.72, bf16[3,128,192]{2,1,0:T(8,128)(2,1)} %pad_maximum_fusion.8.ints_ref), custom_call_target="tpu_custom_call" | custom-call | tf_op jit(solution)/shard_map/pack/pallas_call | solution.py:90
  21.3 42.5 %exchange.2.recv_ref = bf16[64,80,128]{2,1,0:T(8,128)(2,1)} custom-call(bf16[64,80,128]{2,1,0:T(8,128)(2,1)} %pack.1.x_ref), custom_call_target="tpu_custom_call" | custom-call | tf_op jit(solution)/shard_map/exchange/pallas_call | solution.py:180
  63.9 0.9 pad_maximum_fusion.syn_ref
  64.8 37.6 %spread.1 = (bf16[3072,128]{1,0:T(8,128)(2,1)}, f32[3,384,384]{2,1,0:T(8,128)}, f32[3,16,128]{2,1,0:T(8,128)}, f32[3,16,128]{2,1,0:T(8,128)}, s32[3,16,128]{2,1,0:T(8,128)}) custom-call(bf16[64,80,128]{2,1,0:T(8,128)(2,1)} %exchange.2.recv_ref, bf16[3,256,384]{2,1,0:T(8,128)(2,1)} %pad_maximum_fusion.syn_ref), custom_call_target="tpu_custom_call" | custom-call | tf_op jit(solution)/shard_map/spread/pallas_call | solution.py:287
  102.4 3.0 %copy.23 = bf16[8,64,3,2,128]{4,0,3,2,1:T(8,128)(2,1)} copy(bf16[8,64,3,2,128]{4,3,2,1,0:T(2,128)(2,1)} %bitcast.71) | data formatting | bytes 1572864 | tf_op jit(solution)/shard_map/reshape | solution.py:458
  105.5 0.1 copy.25
  105.6 22.4 %reduce-scatter.2.cloned.1.call-done = bf16[8,16,3,2,128]{4,0,3,2,1:T(8,128)(2,1)} async-done(((bf16[8,64,3,2,128]{4,0,3,2,1:T(8,128)(2,1)}), bf16[8,16,3,2,128]{4,0,3,2,1:T(8,128)(2,1)}) %reduce-scatter.2.cloned.1.call-update) | async-done | bytes 196624 | tf_op jit(solution)/shard_map/reduce_scatter | solution.py:459
  128.0 1.2 fusion.23
  129.2 5.9 %collective-permute-start = (bf16[1,16,3,2,128]{4,0,3,2,1:T(2,128)(2,1)S(1)}, bf16[1,16,3,2,128]{4,0,3,2,1:T(2,128)(2,1)S(1)}, u32[]{:S(2)}, u32[]{:S(2)}) collective-permute-start(bf16[1,16,3,2,128]{4,0,3,2,1:T(2,128)(2,1)S(1)} %get-tuple-element.38), channel_id=1, source_target_pairs={{0,4},{4,8},{8,12},{12,16},{16,20},{20,24},{24,28},{28,32},{32,36}... | collective-permute-start | bytes 73736 | tf_op jit(solution)/shard_map/ppermute | solution.py:380
  135.2 1.9 collective-permute-start.1
  137.1 3.4 %collective-permute-done.1 = bf16[1,16,3,2,128]{4,0,3,2,1:T(2,128)(2,1)S(1)} collective-permute-done((bf16[1,16,3,2,128]{4,0,3,2,1:T(2,128)(2,1)S(1)}, bf16[1,16,3,2,128]{4,0,3,2,1:T(2,128)(2,1)S(1)}, u32[]{:S(2)}, u32[]{:S(2)}) %collective-permute-start.1) | collective-permute-done | bytes 24608 | tf_op jit(solution)/shard_map/ppermute | solution.py:383
  140.6 1.3 collective-permute-start.2
  141.9 1.3 collective-permute-start.3
  143.2 3.3 %collective-permute-done.3 = bf16[10,1,3,2,128]{4,0,3,2,1:T(8,128)(2,1)S(1)} collective-permute-done((bf16[10,1,3,2,128]{4,0,3,2,1:T(8,128)(2,1)S(1)}, bf16[10,1,3,2,128]{4,0,3,2,1:T(8,128)(2,1)S(1)}, u32[]{:S(2)}, u32[]{:S(2)}) %collective-permute-start.3) | collective-permute-done | bytes 15392 | tf_op jit(solution)/shard_map/ppermute | solution.py:383
  146.5 0.2 maximum_convert_fusion
  146.7 0.2 fusion.35
  147.0 0.6 copy-done.1
  147.7 0.5 fusion.12
  148.2 3.0 %collective-permute-start.4 = (bf16[1,16,3,2,128]{4,0,3,2,1:T(2,128)(2,1)S(1)}, bf16[1,16,3,2,128]{4,0,3,2,1:T(2,128)(2,1)S(1)}, u32[]{:S(2)}, u32[]{:S(2)}) collective-permute-start(bf16[1,16,3,2,128]{4,0,3,2,1:T(2,128)(2,1)S(1)} %get-tuple-element.36), channel_id=1, source_target_pairs={{0,4},{4,8},{8,12},{12,16},{16,20},{20,24},{24,28},{28,32},{32,36}... | collective-permute-start | bytes 73736 | tf_op jit(solution)/shard_map/ppermute | solution.py:380
  151.3 1.9 collective-permute-start.5
  153.3 3.3 %collective-permute-done.5 = bf16[1,16,3,2,128]{4,0,3,2,1:T(2,128)(2,1)S(1)} collective-permute-done((bf16[1,16,3,2,128]{4,0,3,2,1:T(2,128)(2,1)S(1)}, bf16[1,16,3,2,128]{4,0,3,2,1:T(2,128)(2,1)S(1)}, u32[]{:S(2)}, u32[]{:S(2)}) %collective-permute-start.5) | collective-permute-done | bytes 24608 | tf_op jit(solution)/shard_map/ppermute | solution.py:383
  156.7 3.6 %collective-permute-start.6 = (bf16[10,1,3,2,128]{4,0,3,2,1:T(8,128)(2,1)S(1)}, bf16[10,1,3,2,128]{4,0,3,2,1:T(8,128)(2,1)S(1)}, u32[]{:S(2)}, u32[]{:S(2)}) collective-permute-start(bf16[10,1,3,2,128]{4,0,3,2,1:T(8,128)(2,1)S(1)} %get-tuple-element.26), channel_id=1, source_target_pairs={{0,1},{1,2},{2,3},{4,5},{5,6},{6,7},{8,9},{9,10},{10,11},{12,13},{... | collective-permute-start | bytes 46088 | tf_op jit(solution)/shard_map/ppermute | solution.py:380
  160.4 1.3 collective-permute-start.7
  161.7 0.9 maximum_bitcast_fusion.ana_ref
  162.5 2.4 collective-permute-done.7
  164.9 0.2 maximum_convert_fusion.1
  165.1 0.2 fusion.33
  165.4 0.5 fusion.31
  165.9 12.8 %all_gather.3 = bf16[8,64,3,2,128]{4,0,3,2,1:T(8,128)(2,1)S(1)} all-gather(bf16[8,16,3,2,128]{4,0,3,2,1:T(8,128)(2,1)S(1)} %get-tuple-element.16), channel_id=1, replica_groups=mesh['slab'=64,'batch'=4] {'batch'}, dimensions={1}, use_global_device_ids=true | all-gather | bytes 983040 | tf_op jit(solution)/shard_map/all_gather | solution.py:467
  178.7 1.5 copy.24
  180.2 31.0 %sample.1.x_ref = bf16[64,24,128]{2,1,0:T(8,128)(2,1)} custom-call(bf16[3072,128]{1,0:T(8,128)(2,1)} %bitcast.69, f32[3,384,384]{2,1,0:T(8,128)} %get-tuple-element.8.p_ref, f32[3,16,128]{2,1,0:T(8,128)} %get-tuple-element.9.tx_ref, f32[3,16,128]{2,1,0:T(8,128)} %get-tuple-element.10.ty_ref, s32[3,16,128]{2,1,0:T(8,128)} %get-tuple-element.11.idx_smem, ...), custom_call_target="tpu_custom_call" | custom-call | tf_op jit(solution)/shard_map/sample/pallas_call | solution.py:359
  211.3 24.5 %exchange.3.back_ref = bf16[64,24,128]{2,1,0:T(8,128)(2,1)} custom-call(bf16[64,24,128]{2,1,0:T(8,128)(2,1)} %sample.1.x_ref), custom_call_target="tpu_custom_call" | custom-call | tf_op jit(solution)/shard_map/exchange/pallas_call | solution.py:180
  235.8 2.9 %unpack.1 = bf16[3,169,192]{2,1,0:T(8,128)(2,1)} custom-call(s32[1,192]{1,0:T(1,128)} %bitcast.80, s32[192,1]{1,0:T(8,128)} %copy.22.col_ref, bf16[64,24,128]{2,1,0:T(8,128)(2,1)} %exchange.3.back_ref), custom_call_target="tpu_custom_call" | custom-call | tf_op jit(solution)/shard_map/unpack/pallas_call | solution.py:124
  238.7 0.9 copy.27
  (29 shorter events, 0.9 us)
Async XLA Ops:
  7.2 120.8 %reduce-scatter.2.cloned.1.call-start = ((), (), s32[]{:S(2)}) async-start(), calls=%async_computation.1 | async-start | bytes 983040 | tf_op jit(solution)/shard_map/reduce_scatter | solution.py:459
  102.4 3.0 %copy-start.2 = (bf16[169,338]{1,0:T(8,128)(2,1)S(1)}, bf16[169,338]{1,0:T(8,128)(2,1)}, u32[]{:S(2)}) copy-start(bf16[169,338]{1,0:T(8,128)(2,1)} %param.17) | copy-start | bytes 342736
  102.4 25.6 %copy-start = (f32[8,16,2,3,128]{4,2,3,1,0:T(2,128)S(1)}, f32[8,16,2,3,128]{4,2,3,1,0:T(2,128)}, u32[]{:S(2)}) copy-start(f32[8,16,2,3,128]{4,2,3,1,0:T(2,128)} %param.9) | copy-start | bytes 1179652
  129.2 7.9 %collective-permute-start = (bf16[1,16,3,2,128]{4,0,3,2,1:T(2,128)(2,1)S(1)}, bf16[1,16,3,2,128]{4,0,3,2,1:T(2,128)(2,1)S(1)}, u32[]{:S(2)}, u32[]{:S(2)}) collective-permute-start(bf16[1,16,3,2,128]{4,0,3,2,1:T(2,128)(2,1)S(1)} %get-tuple-element.38), channel_id=1, source_target_pairs={{0,4},{4,8},{8,12},{12,16},{16,20},{20,24},{24,28},{28,32},{32,36}... | collective-permute-start | bytes 73736 | tf_op jit(solution)/shard_map/ppermute | solution.py:380
  135.2 5.4 %collective-permute-start.1 = (bf16[1,16,3,2,128]{4,0,3,2,1:T(2,128)(2,1)S(1)}, bf16[1,16,3,2,128]{4,0,3,2,1:T(2,128)(2,1)S(1)}, u32[]{:S(2)}, u32[]{:S(2)}) collective-permute-start(bf16[1,16,3,2,128]{4,0,3,2,1:T(2,128)(2,1)S(1)} %get-tuple-element.39), channel_id=1, source_target_pairs={{4,0},{8,4},{12,8},{16,12},{20,16},{24,20},{28,24},{32,28},{36,32}... | collective-permute-start | bytes 73736 | tf_op jit(solution)/shard_map/ppermute | solution.py:383
  140.6 2.6 %collective-permute-start.2 = (bf16[10,1,3,2,128]{4,0,3,2,1:T(8,128)(2,1)S(1)}, bf16[10,1,3,2,128]{4,0,3,2,1:T(8,128)(2,1)S(1)}, u32[]{:S(2)}, u32[]{:S(2)}) collective-permute-start(bf16[10,1,3,2,128]{4,0,3,2,1:T(8,128)(2,1)S(1)} %get-tuple-element.28), channel_id=1, source_target_pairs={{0,1},{1,2},{2,3},{4,5},{5,6},{6,7},{8,9},{9,10},{10,11},{12,13},{... | collective-permute-start | bytes 46088 | tf_op jit(solution)/shard_map/ppermute | solution.py:380
  141.9 4.6 %collective-permute-start.3 = (bf16[10,1,3,2,128]{4,0,3,2,1:T(8,128)(2,1)S(1)}, bf16[10,1,3,2,128]{4,0,3,2,1:T(8,128)(2,1)S(1)}, u32[]{:S(2)}, u32[]{:S(2)}) collective-permute-start(bf16[10,1,3,2,128]{4,0,3,2,1:T(8,128)(2,1)S(1)} %get-tuple-element.29), channel_id=1, source_target_pairs={{1,0},{2,1},{3,2},{5,4},{6,5},{7,6},{9,8},{10,9},{11,10},{13,12},{... | collective-permute-start | bytes 46088 | tf_op jit(solution)/shard_map/ppermute | solution.py:383
  146.7 0.9 copy-start.1
  148.2 5.1 %collective-permute-start.4 = (bf16[1,16,3,2,128]{4,0,3,2,1:T(2,128)(2,1)S(1)}, bf16[1,16,3,2,128]{4,0,3,2,1:T(2,128)(2,1)S(1)}, u32[]{:S(2)}, u32[]{:S(2)}) collective-permute-start(bf16[1,16,3,2,128]{4,0,3,2,1:T(2,128)(2,1)S(1)} %get-tuple-element.36), channel_id=1, source_target_pairs={{0,4},{4,8},{8,12},{12,16},{16,20},{20,24},{24,28},{28,32},{32,36}... | collective-permute-start | bytes 73736 | tf_op jit(solution)/shard_map/ppermute | solution.py:380
  151.3 5.4 %collective-permute-start.5 = (bf16[1,16,3,2,128]{4,0,3,2,1:T(2,128)(2,1)S(1)}, bf16[1,16,3,2,128]{4,0,3,2,1:T(2,128)(2,1)S(1)}, u32[]{:S(2)}, u32[]{:S(2)}) collective-permute-start(bf16[1,16,3,2,128]{4,0,3,2,1:T(2,128)(2,1)S(1)} %get-tuple-element.37), channel_id=1, source_target_pairs={{4,0},{8,4},{12,8},{16,12},{20,16},{24,20},{28,24},{32,28},{36,32}... | collective-permute-start | bytes 73736 | tf_op jit(solution)/shard_map/ppermute | solution.py:383
  156.7 5.8 %collective-permute-start.6 = (bf16[10,1,3,2,128]{4,0,3,2,1:T(8,128)(2,1)S(1)}, bf16[10,1,3,2,128]{4,0,3,2,1:T(8,128)(2,1)S(1)}, u32[]{:S(2)}, u32[]{:S(2)}) collective-permute-start(bf16[10,1,3,2,128]{4,0,3,2,1:T(8,128)(2,1)S(1)} %get-tuple-element.26), channel_id=1, source_target_pairs={{0,1},{1,2},{2,3},{4,5},{5,6},{6,7},{8,9},{9,10},{10,11},{12,13},{... | collective-permute-start | bytes 46088 | tf_op jit(solution)/shard_map/ppermute | solution.py:380
  160.4 4.6 %collective-permute-start.7 = (bf16[10,1,3,2,128]{4,0,3,2,1:T(8,128)(2,1)S(1)}, bf16[10,1,3,2,128]{4,0,3,2,1:T(8,128)(2,1)S(1)}, u32[]{:S(2)}, u32[]{:S(2)}) collective-permute-start(bf16[10,1,3,2,128]{4,0,3,2,1:T(8,128)(2,1)S(1)} %get-tuple-element.27), channel_id=1, source_target_pairs={{1,0},{2,1},{3,2},{5,4},{6,5},{7,6},{9,8},{10,9},{11,10},{13,12},{... | collective-permute-start | bytes 46088 | tf_op jit(solution)/shard_map/ppermute | solution.py:383
Sparse Core Ops, SparseCore 0:
  105.6 22.3 reduce-scatter.1

commit v2 on v1

--- a/solution.py
+++ b/solution.py
@@ -47,32 +47,47 @@
     return lax.dot_general(a, b, dims, preferred_element_type=F32)
 
 
-def slot_onehot(row_ref, col_ref, slots):
-    cells = row_ref.shape[1]
-    row, col = row_ref[...], col_ref[...]
-    before = lax.broadcasted_iota(jnp.int32, (cells, cells), 0) < lax.broadcasted_iota(
-        jnp.int32, (cells, cells), 1
-    )
-    same = jnp.where((col == row) & before, 1.0, 0.0)
-    rank = jnp.sum(same, axis=0, keepdims=True)
-    slot = row * CAP + rank.astype(jnp.int32)
-    at = lax.broadcasted_iota(jnp.int32, (slots, cells), 0)
+def slot_onehot(owner_ref, slab_count):
+    cells = owner_ref.shape[1]
+    owner = owner_ref[...]
+    slab_at = lax.broadcasted_iota(jnp.int32, (slab_count, cells), 0)
+    member = jnp.where(slab_at == owner, 1.0, 0.0)
+    first = lax.broadcasted_iota(jnp.int32, (cells, cells), 0)
+    second = lax.broadcasted_iota(jnp.int32, (cells, cells), 1)
+    before = jnp.where(first < second, 1.0, 0.0).astype(BF16)
+    rank = jnp.sum(member * dot(member.astype(BF16), before, NN), axis=0, keepdims=True)
+    slot = owner * CAP + rank.astype(jnp.int32)
+    at = lax.broadcasted_iota(jnp.int32, (slab_count * CAP, cells), 0)
     return jnp.where(at == slot, 1.0, 0.0).astype(BF16)
 
 
-def pack_kernel(row_ref, col_ref, coef_ref, offs_ref, ints_ref, out_ref, x_ref, blk_ref):
+def pack_kernel(
+    owner_ref, coef_ref, offs_ref, anchor_ref, blocks_ref, count_ref, out_ref,
+    x_ref, blk_ref, rows_ref,
+):
     slab_count = out_ref.shape[0]
     slots = slab_count * CAP
-    hot = slot_onehot(row_ref, col_ref, slots)
-    for r in range(4):
-        x_ref[r] = dot(hot, coef_ref[r], NT)
+    hot = slot_onehot(owner_ref, slab_count)
+    rows_ref[...] = jnp.zeros_like(rows_ref)
+    for k in range(3):
+        x_ref[k] = dot(hot, coef_ref[k, :128, :], NT)
+        rows_ref[k * REM : (k + 1) * REM] = coef_ref[k, 128:, :].astype(F32)
+    x_ref[3] = dot(hot, rows_ref[...].astype(BF16), NT)
+    rows_ref[...] = jnp.zeros_like(rows_ref)
     tail = jnp.zeros((slots, QP - Q), F32)
+    width = NY * LAYERS
+    lists = (blocks_ref[...] // width, blocks_ref[...] % width, None)
     for k in range(3):
+        if lists[k] is not None:
+            rows_ref[96:112] = lists[k].astype(F32)
+        place = anchor_ref[k : k + 1, :]
+        rows_ref[112:113] = (place % 128 if k == 2 else place).astype(F32)
+        rows_ref[113:114] = count_ref[...].astype(F32)
         got = dot(hot, offs_ref[k], NN)
         x_ref[4 + 3 * k] = got[:, :128]
         x_ref[5 + 3 * k] = got[:, 128:256]
         x_ref[6 + 3 * k] = jnp.concatenate([got[:, 256:], tail], axis=1) + dot(
-            hot, ints_ref[k], NT
+            hot, rows_ref[...].astype(BF16), NT
         )
 
     def step(target, carry):
@@ -85,25 +100,25 @@
     lax.fori_loop(0, slab_count, step, 0)
 
 
-def pack(row, col, coef_t, offs, ints_t, slab_count):
+def pack(owner, coef, offs, anchor, blocks, count, slab_count):
     block_rows = -(-PLANES * CAP // 16) * 16
     return pl.pallas_call(
         pack_kernel,
         out_shape=jax.ShapeDtypeStruct((slab_count, block_rows, 128), BF16),
-        in_specs=[VMEM_SPEC] * 5,
+        in_specs=[VMEM_SPEC] * 6,
         out_specs=VMEM_SPEC,
         scratch_shapes=[
             pltpu.VMEM((PLANES, slab_count * CAP, 128), F32),
             pltpu.VMEM((block_rows, 128), F32),
+            pltpu.VMEM((128, owner.shape[1]), F32),
         ],
         name="pack",
-    )(row, col, coef_t, offs, ints_t)
-
-
-def unpack_kernel(row_ref, col_ref, back_ref, out_ref, blk_ref, r_ref):
+    )(owner, coef, offs, anchor, blocks, count)
+
+
+def unpack_kernel(owner_ref, back_ref, out_ref, blk_ref, r_ref):
     slab_count = back_ref.shape[0]
-    slots = slab_count * CAP
-    hot = slot_onehot(row_ref, col_ref, slots)
+    hot = slot_onehot(owner_ref, slab_count)
 
     def step(source, carry):
         blk_ref[...] = back_ref[source].astype(F32)
@@ -118,20 +133,20 @@
         out_ref[k] = jnp.concatenate([main, rem[k * REM : (k + 1) * REM]], axis=0).astype(BF16)
 
 
-def unpack(row, col, back):
+def unpack(owner, back):
     slab_count, block_rows, _ = back.shape
-    cells = row.shape[1]
+    cells = owner.shape[1]
     return pl.pallas_call(
         unpack_kernel,
         out_shape=jax.ShapeDtypeStruct((3, L, cells), BF16),
-        in_specs=[VMEM_SPEC] * 3,
+        in_specs=[VMEM_SPEC] * 2,
         out_specs=VMEM_SPEC,
         scratch_shapes=[
             pltpu.VMEM((block_rows, 128), F32),
             pltpu.VMEM((OUT_PLANES, slab_count * CAP, 128), F32),
         ],
         name="unpack",
-    )(row, col, back)
+    )(owner, back)
 
 
 def exchange_kernel(x_ref, out_ref, send_sem, recv_sem, local_sem):
@@ -186,6 +201,16 @@
         compiler_params=pltpu.CompilerParams(collective_id=collective_id, has_side_effects=True),
         name="exchange",
     )(x)
+
+
+def basis_plane(basis_ref, wide_ref, k):
+    if k == 0:
+        wide_ref[...] = jnp.zeros_like(wide_ref)
+        wide_ref[:128, :Q] = basis_ref[:128, :].astype(F32)
+    else:
+        wide_ref[128 + (k - 1) * REM : 128 + k * REM, :Q] = jnp.zeros((REM, Q), F32)
+    wide_ref[128 + k * REM : 128 + (k + 1) * REM, :Q] = basis_ref[128:, :].astype(F32)
+    return wide_ref[...].astype(BF16)
 
 
 def z_weights(pz):
@@ -243,13 +268,13 @@
 
 def spread_kernel(
     recv_ref, syn_ref, out_ref, p_ref, tx_ref, ty_ref, idx_ref,
-    blk_ref, r_ref, f_ref, acc_ref, t_ref, idx_smem,
+    blk_ref, r_ref, f_ref, acc_ref, t_ref, idx_smem, wide_ref,
 ):
     prepare_kernel_part(recv_ref, blk_ref, r_ref, p_ref, tx_ref, ty_ref, idx_ref)
     pltpu.sync_copy(idx_ref, idx_smem)
     for k in range(3):
         coef = jnp.concatenate([r_ref[k], r_ref[3]], axis=1).astype(BF16)
-        f_ref[k] = dot(coef, syn_ref[k], NN)
+        f_ref[k] = dot(coef, basis_plane(syn_ref, wide_ref, k), NN)
     acc_ref[...] = jnp.zeros_like(acc_ref)
 
     def group(g, carry):
@@ -302,6 +327,7 @@
             pltpu.VMEM((ROWS + 8 * B, 128), F32),
             pltpu.VMEM((8, 3 * B, 128), F32),
             pltpu.SMEM((chunks, B, 128), jnp.int32),
+            pltpu.VMEM((256, QP), F32),
         ],
         name="spread",
     )(recv, syn)
@@ -309,7 +335,7 @@
 
 def sample_kernel(
     vel_ref, p_ref, tx_ref, ty_ref, idx_smem, ana_ref, out_ref,
-    v_ref, g_ref, pv_ref, c_ref, blk_ref,
+    v_ref, g_ref, pv_ref, c_ref, blk_ref, wide_ref,
 ):
     v_ref[:ROWS, :] = vel_ref[...].astype(F32)
     v_ref[ROWS:, :] = jnp.zeros((v_ref.shape[0] - ROWS, 128), F32)
@@ -339,7 +365,7 @@
     lax.fori_loop(0, slots // 8, group, 0)
     rem = jnp.zeros((slots, 128), F32)
     for k in range(3):
-        got = dot(pv_ref[k].astype(BF16), ana_ref[k], NN)
+        got = dot(pv_ref[k].astype(BF16), basis_plane(ana_ref, wide_ref, k), NT)
         c_ref[k] = got[:, :128]
         rem = rem + got[:, 128:]
     c_ref[3] = rem
@@ -367,109 +393,192 @@
             pltpu.VMEM((3, slots, QP), F32),
             pltpu.VMEM((OUT_PLANES, slots, 128), F32),
             pltpu.VMEM((block_rows, 128), F32),
+            pltpu.VMEM((256, QP), F32),
         ],
         name="sample",
     )(vel, p, tx, ty, idx, ana)
 
 
-def padded_2(block, sides, width):
-    for axis, dim in sides:
-        count = lax.axis_size(axis)
-        forward = [(i, i + 1) for i in range(count - 1)]
-        backward = [(target, source) for source, target in forward]
-        low = lax.ppermute(
-            lax.slice_in_dim(block, block.shape[dim] - width, None, axis=dim), axis, forward
+LINE = 3 * LAYERS
+
+
+def grid_kernel(
+    part_ref, vel_ref, new_ref, all_ref,
+    hop_ref, got_ref, summed_ref, drive_ref, st_ref, own_ref,
+    xs_ref, xr_ref, ys_ref, yr_ref, y32_ref, send_sem, recv_sem, local_sem,
+):
+    planes, mine, _ = vel_ref.shape
+    half = planes // 2
+    batches, slabs = lax.axis_size("batch"), lax.axis_size("slab")
+    b, s = lax.axis_index("batch"), lax.axis_index("slab")
+    right, far, left = [lax.rem(b + i, batches) for i in (1, 2, 3)]
+    above, below = lax.rem(s + 1, slabs), lax.rem(s + slabs - 1, slabs)
+
+    barrier = pltpu.get_barrier_semaphore()
+    for device in ({"batch": right}, {"batch": left}, {"slab": above}, {"slab": below}):
+        pl.semaphore_signal(
+            barrier, inc=1, device_id=device, device_id_type=pl.DeviceIdType.MESH
         )
-        high = lax.ppermute(lax.slice_in_dim(block, 0, width, axis=dim), axis, backward)
-        block = jnp.concatenate([low, block, high], axis=dim)
-    return block
-
-
-def neighbours(padded):
-    centre = padded[1:-1, 1:-1]
-    total = padded[2:, 1:-1] + padded[:-2, 1:-1] + padded[1:-1, 2:] + padded[1:-1, :-2]
-    zero_edge = jnp.zeros(centre.shape[:3] + (1, 1), centre.dtype)
-    after = jnp.concatenate([centre[:, :, :, 1:, :1], zero_edge], axis=3)
-    before = jnp.concatenate([zero_edge, centre[:, :, :, :-1, -1:]], axis=3)
-    upper = jnp.concatenate([centre[..., 1:], after], axis=-1)
-    lower = jnp.concatenate([before, centre[..., :-1]], axis=-1)
-    return total + upper + lower
-
-
-def relax(drive, widen):
-    state = drive
-    for sweep_index in range(SWEEPS):
-        state = (drive + coupling * neighbours(widen(state))) / (1.0 + 6.0 * coupling)
-    return state
-
-
-def coef_planes(values):
-    n = values.shape[2]
-    rest = jnp.concatenate(
-        [values[0, 128:], values[1, 128:], values[2, 128:], jnp.zeros((128 - 3 * REM, n), values.dtype)],
-        axis=0,
-    )
-    return jnp.concatenate([values[:, :128], rest[None]], axis=0)
-
-
-def basis_planes(basis):
-    wide = jnp.pad(basis, ((0, 0), (0, QP - Q)))
-    return jnp.stack(
-        [
-            jnp.concatenate(
-                [wide[:128], jnp.pad(wide[128:], ((k * REM, 128 - (k + 1) * REM), (0, 0)))], axis=0
+    pl.semaphore_wait(barrier, 4)
+
+    def rows(part):
+        return pl.ds(pl.multiple_of(part * mine, mine), mine)
+
+    started = []
+
+    def send(src, dst, **device):
+        n = len(started)
+        copy = pltpu.make_async_remote_copy(
+            src_ref=src, dst_ref=dst, send_sem=send_sem.at[n], recv_sem=recv_sem.at[n],
+            device_id=device, device_id_type=pl.DeviceIdType.MESH,
+        )
+        copy.start()
+        started.append(copy)
+        return copy
+
+    low, high = pl.ds(0, half), pl.ds(half, half)
+
+    hop_r = send(part_ref.at[low, rows(far)], hop_ref.at[0], batch=right)
+    hop_l = send(part_ref.at[high, rows(far)], hop_ref.at[1], batch=left)
+    near_r = send(part_ref.at[high, rows(right)], got_ref.at[0], batch=right)
+    near_l = send(part_ref.at[low, rows(left)], got_ref.at[1], batch=left)
+    hop_r.wait_recv()
+    summed_ref[0] = (
+        part_ref[low, rows(right), :].astype(F32) + hop_ref[0].astype(F32)
+    ).astype(BF16)
+    far_r = send(summed_ref.at[0], got_ref.at[2], batch=right)
+    hop_l.wait_recv()
+    summed_ref[1] = (
+        part_ref[high, rows(left), :].astype(F32) + hop_ref[1].astype(F32)
+    ).astype(BF16)
+    far_l = send(summed_ref.at[1], got_ref.at[3], batch=left)
+    drive_ref[...] = vel_ref[...] + part_ref[:, rows(b), :].astype(F32)
+    near_r.wait_recv()
+    near_l.wait_recv()
+    far_r.wait_recv()
+    far_l.wait_recv()
+    drive_ref[:half] += got_ref[1].astype(F32) + got_ref[2].astype(F32)
+    drive_ref[half:] += got_ref[0].astype(F32) + got_ref[3].astype(F32)
+
+    lane = lax.broadcasted_iota(jnp.int32, (mine, 128), 1)
+    layer = lax.broadcasted_iota(jnp.int32, (mine, 128), 0) % LAYERS
+    at_end, at_start = lane == 127, lane == 0
+    has_next, has_previous = layer < LAYERS - 1, layer > 0
+    inside = slice(8, 8 + mine)
+    for sweep in range(SWEEPS):
+        for x in range(planes):
+            st_ref[1 + x, inside, :] = drive_ref[x] if sweep == 0 else new_ref[x]
+        xs_ref[sweep, 0] = st_ref[planes, inside, :].astype(BF16)
+        xs_ref[sweep, 1] = st_ref[1, inside, :].astype(BF16)
+        for x in range(planes):
+            y32_ref[0, x * LINE : (x + 1) * LINE] = st_ref[1 + x, 2 + mine : 8 + mine, :]
+            y32_ref[1, x * LINE : (x + 1) * LINE] = st_ref[1 + x, 8 : 8 + LINE, :]
+        for side in range(2):
+            ys_ref[sweep, side] = y32_ref[side].astype(BF16)
+        copies = [
+            send(xs_ref.at[sweep, 0], xr_ref.at[sweep, 0], slab=above),
+            send(xs_ref.at[sweep, 1], xr_ref.at[sweep, 1], slab=below),
+            send(ys_ref.at[sweep, 0], yr_ref.at[sweep, 0], batch=right),
+            send(ys_ref.at[sweep, 1], yr_ref.at[sweep, 1], batch=left),
+        ]
+        for copy in copies:
+            copy.wait_recv()
+        x_low, x_high = xr_ref[sweep, 0].astype(F32), xr_ref[sweep, 1].astype(F32)
+        st_ref[0, inside, :] = jnp.where(s > 0, x_low, 0.0)
+        st_ref[planes + 1, inside, :] = jnp.where(s < slabs - 1, x_high, 0.0)
+        y32_ref[0] = jnp.where(b > 0, yr_ref[sweep, 0].astype(F32), 0.0)
+        y32_ref[1] = jnp.where(b < batches - 1, yr_ref[sweep, 1].astype(F32), 0.0)
+        for x in range(planes):
+            st_ref[1 + x, 8 - LINE : 8, :] = y32_ref[0, x * LINE : (x + 1) * LINE]
+            st_ref[1 + x, 8 + mine : 8 + mine + LINE, :] = y32_ref[1, x * LINE : (x + 1) * LINE]
+        for x in range(planes):
+            total = (
+                st_ref[x, inside, :]
+                + st_ref[x + 2, inside, :]
+                + st_ref[x + 1, 8 - LINE : 8 - LINE + mine, :]
+                + st_ref[x + 1, 8 + LINE : 8 + LINE + mine, :]
             )
-            for k in range(3)
-        ]
-    )
-
-
-def int_planes(anchor, blocks, count):
-    cells = count.shape[0]
-    anchor_t, blocks_t = anchor.T, blocks.T
-    width = NY * LAYERS
-    lists = (blocks_t // width, blocks_t % width, jnp.zeros_like(blocks_t))
-    places = (anchor_t[0:1], anchor_t[1:2], anchor_t[2:3] % 128)
-    planes = []
-    for k in range(3):
-        rows = [
-            jnp.zeros((96, cells), jnp.int32), lists[k], places[k], count[None],
-            jnp.zeros((14, cells), jnp.int32),
-        ]
-        planes.append(jnp.concatenate(rows, axis=0))
-    return jnp.stack(planes).astype(BF16)
+            centre = st_ref[x + 1, inside, :]
+            after = jnp.where(has_next, st_ref[x + 1, 9 : 9 + mine, :], 0.0)
+            before = jnp.where(has_previous, st_ref[x + 1, 7 : 7 + mine, :], 0.0)
+            upper = pltpu.roll(jnp.where(at_start, after, centre), 127, 1)
+            lower = pltpu.roll(jnp.where(at_end, before, centre), 1, 1)
+            total = total + upper + lower
+            new_ref[x] = (drive_ref[x] + coupling * total) * (1.0 / (1.0 + 6.0 * coupling))
+
+    own_ref[...] = new_ref[...].astype(BF16)
+    at_right_low = send(own_ref.at[low], all_ref.at[low, rows(b)], batch=right)
+    at_left_high = send(own_ref.at[high], all_ref.at[high, rows(b)], batch=left)
+    at_right_high = send(own_ref.at[high], all_ref.at[high, rows(b)], batch=right)
+    at_left_low = send(own_ref.at[low], all_ref.at[low, rows(b)], batch=left)
+    local = pltpu.make_async_copy(own_ref, all_ref.at[:, rows(b)], local_sem)
+    local.start()
+    at_right_low.wait_recv()
+    on_r = send(all_ref.at[low, rows(left)], all_ref.at[low, rows(left)], batch=right)
+    at_left_high.wait_recv()
+    on_l = send(all_ref.at[high, rows(right)], all_ref.at[high, rows(right)], batch=left)
+    for copy in (at_right_high, at_left_low, on_r, on_l):
+        copy.wait_recv()
+    local.wait()
+    for copy in started:
+        copy.wait_send()
+
+
+def grid_step(part, vel, collective_id):
+    planes, mine, _ = vel.shape
+    half = planes // 2
+    copies = 6 + 4 * SWEEPS + 6
+    return pl.pallas_call(
+        grid_kernel,
+        out_shape=(
+            jax.ShapeDtypeStruct(vel.shape, F32),
+            jax.ShapeDtypeStruct(part.shape, BF16),
+        ),
+        in_specs=[VMEM_SPEC] * 2,
+        out_specs=(VMEM_SPEC, ANY_SPEC),
+        scratch_shapes=[
+            pltpu.VMEM((2, half, mine, 128), BF16),
+            pltpu.VMEM((4, half, mine, 128), BF16),
+            pltpu.VMEM((2, half, mine, 128), BF16),
+            pltpu.VMEM((planes, mine, 128), F32),
+            pltpu.VMEM((planes + 2, mine + 16, 128), F32),
+            pltpu.VMEM((planes, mine, 128), BF16),
+            pltpu.VMEM((SWEEPS, 2, mine, 128), BF16),
+            pltpu.VMEM((SWEEPS, 2, mine, 128), BF16),
+            pltpu.VMEM((SWEEPS, 2, planes * LINE, 128), BF16),
+            pltpu.VMEM((SWEEPS, 2, planes * LINE, 128), BF16),
+            pltpu.VMEM((2, planes * LINE, 128), F32),
+            pltpu.SemaphoreType.DMA((copies,)),
+            pltpu.SemaphoreType.DMA((copies,)),
+            pltpu.SemaphoreType.DMA,
+        ],
+        compiler_params=pltpu.CompilerParams(collective_id=collective_id, has_side_effects=True),
+        name="grid_step",
+    )(part, vel)
 
 
 def local(
     velocity_old, traction, offsets, owner_slab, anchor, blocks, block_count, synthesis, analysis
 ):
     slab_count = lax.axis_size("slab")
-    row = owner_slab[:, 0][None, :]
+    owner = owner_slab.T
     sent = pack(
-        row,
-        owner_slab,
-        coef_planes(traction.transpose(1, 2, 0)),
+        owner,
+        traction.transpose(1, 2, 0),
         offsets.transpose(1, 0, 2),
-        int_planes(anchor, blocks, block_count),
+        anchor.T,
+        blocks.T,
+        block_count[None],
         slab_count,
     )
     received = exchange(sent, 0)
-    partial_value, p, tx, ty, idx = spread(received, basis_planes(synthesis))
-    partial_value = partial_value.reshape(GX, NY, 3, LAYERS, 128)
-    drive = velocity_old.transpose(0, 1, 3, 2, 4) + lax.psum_scatter(
-        partial_value, "batch", scatter_dimension=1, tiled=True
-    ).astype(F32)
-
-    def widen(state):
-        return padded_2(state.astype(BF16), (("slab", 0), ("batch", 1)), 1).astype(state.dtype)
-
-    velocity_new = relax(drive, widen)
-    slab_velocity = lax.all_gather(velocity_new.astype(BF16), "batch", axis=1, tiled=True)
-    coefs = sample(
-        slab_velocity.reshape(ROWS, 128), p, tx, ty, idx,
-        basis_planes(analysis).transpose(0, 2, 1), slab_count,
-    )
-    velocity_coef = unpack(row, owner_slab, exchange(coefs, 1))
+    part, p, tx, ty, idx = spread(received, synthesis)
+    planes, lines = velocity_old.shape[:2]
+    velocity = velocity_old.transpose(0, 1, 3, 2, 4).reshape(planes, lines * LINE, 128)
+    velocity_new, slab_velocity = grid_step(part.reshape(planes, NY * LINE, 128), velocity, 2)
+    coefs = sample(slab_velocity.reshape(ROWS, 128), p, tx, ty, idx, analysis, slab_count)
+    velocity_coef = unpack(owner, exchange(coefs, 1))
+    velocity_new = velocity_new.reshape(planes, lines, 3, LAYERS, 128)
     return (velocity_new.transpose(0, 1, 3, 2, 4), velocity_coef.transpose(2, 0, 1))
 
 

time: 247 us -> 170 us (0.69)
  waiting for transfers between devices: 34.8 us -> 0 us
  Pallas kernels: 143 us -> 167 us
  starting transfers between devices: 20.4 us -> 0 us
  between operations: 14.3 us -> 0.66 us
  blocking collectives: 12.8 us -> 0 us
  local copies, waits for them, and re-layouts: 12.4 us -> 0.75 us
  other arithmetic: 8.97 us -> 0 us
    pallas_call x0 -> x1, Pallas kernels: none -> 27.9 us  [grid_step(): pl.pallas_call(grid_kernel, out_shape=(jax.ShapeDtypeStruct(vel.shape, F3...]
    reduce_scatter x1 -> x0, waiting for transfers between devices: 22.4 us -> none  [local(): lax.psum_scatter(partial_value, 'batch', scatter_dimension=1, tiled=True)]
    ppermute x8 -> x0, starting transfers between devices: 20.3 us -> none  [the longest x4 13.9 us: padded_2(): lax.ppermute(lax.slice_in_dim(block, block.shape[dim] - width, None, axis...]
    all_gather x1 -> x0, blocking collectives: 12.8 us -> none  [local(): lax.all_gather(velocity_new.astype(BF16), 'batch', axis=1, tiled=True)]
    ppermute x8 -> x0, waiting for transfers between devices: 12.4 us -> none  [the longest x4 12.4 us: padded_2(): lax.ppermute(lax.slice_in_dim(block, 0, width, axis=dim), axis, backward)]
    another operation x8 -> x0, other arithmetic: 4.61 us -> none
    slice x12 -> x0, local copies, waits for them, and re-layouts: 3.39 us -> none  [the longest x1 0.94 us: coef_planes(): return jnp.concatenate([values[:, :128], rest[None]], axis=0)]
    pallas_call x2, Pallas kernels: 67.1 us -> 63.9 us  [exchange(): pl.pallas_call(exchange_kernel, out_shape=jax.ShapeDtypeStruct(x.shape, x...]
  transfers between devices with their start and end apart: 9 -> 0, of which waited for: 5 -> 0; matrix products, arithmetic and copies ran while one was open for 0% -> 0% of each run, Pallas kernels for 0% -> 0%
where the time goes in v2:
time: 170 us; the launch traced here: 169 us
  Pallas kernels  167 us (98%)
    pallas_call x2, Pallas kernels, exchange(): pl.pallas_call(exchange_kernel, out_shape=jax.ShapeDtypeStruct(x.shape, x...  63.9 us
    pallas_call x1, Pallas kernels, spread(): pl.pallas_call(spread_kernel, out_shape=(jax.ShapeDtypeStruct((ROWS, 128)...  37.5 us
    pallas_call x1, Pallas kernels, sample(): pl.pallas_call(sample_kernel, out_shape=jax.ShapeDtypeStruct((slab_count,...  30.9 us
    pallas_call x1, Pallas kernels, grid_step(): pl.pallas_call(grid_kernel, out_shape=(jax.ShapeDtypeStruct(vel.shape, F3...  27.9 us
    pallas_call x1, Pallas kernels, pack(): pl.pallas_call(pack_kernel, out_shape=jax.ShapeDtypeStruct((slab_count, b...  4.26 us

profile of v2, /device:TPU:1, one launch (start us, length us, event | category | flops | bytes accessed | tf_op | source)
XLA Modules:
  0.0 168.8 jit_solution(6059407551432996795)
XLA Ops:
  0.6 4.3 %pack.1.x_ref = bf16[64,80,128]{2,1,0:T(8,128)(2,1)} custom-call(s32[1,192]{1,0:T(1,128)} %bitcast.24, bf16[3,169,192]{2,1,0:T(8,128)(2,1)} %bitcast.20, bf16[3,192,338]{2,1,0:T(8,128)(2,1)} %bitcast.17, s32[3,192]{1,0:T(4,128)} %bitcast.23, s32[16,192]{1,0:T(8,128)} %bitcast.22, s32[1,192]{1,0:T(1,128)} %bitcast.26), custom_call_target="tpu_custom_call" | custom-call | tf_op jit(solution)/shard_map/pack/pallas_call | solution.py:105
  4.9 42.6 %exchange.2.recv_ref = bf16[64,80,128]{2,1,0:T(8,128)(2,1)} custom-call(bf16[64,80,128]{2,1,0:T(8,128)(2,1)} %pack.1.x_ref), custom_call_target="tpu_custom_call" | custom-call | tf_op jit(solution)/shard_map/exchange/pallas_call | solution.py:195
  47.5 37.5 %spread.1 = (bf16[3072,128]{1,0:T(8,128)(2,1)}, f32[3,384,384]{2,1,0:T(8,128)}, f32[3,16,128]{2,1,0:T(8,128)}, f32[3,16,128]{2,1,0:T(8,128)}, s32[3,16,128]{2,1,0:T(8,128)}) custom-call(bf16[64,80,128]{2,1,0:T(8,128)(2,1)} %exchange.2.recv_ref, bf16[169,338]{1,0:T(8,128)(2,1)} %syn_ref.1), custom_call_target="tpu_custom_call" | custom-call | tf_op jit(solution)/shard_map/spread/pallas_call | solution.py:312
  85.0 27.9 %grid_step.1 = (f32[8,96,128]{2,1,0:T(8,128)}, bf16[8,384,128]{2,1,0:T(8,128)(2,1)}) custom-call(bf16[8,384,128]{2,1,0:T(8,128)(2,1)} %bitcast.15, f32[8,96,128]{2,1,0:T(8,128)} %bitcast.19), custom_call_target="tpu_custom_call" | custom-call | tf_op jit(solution)/shard_map/grid_step/pallas_call | solution.py:531
  112.9 30.9 %sample.1.x_ref = bf16[64,24,128]{2,1,0:T(8,128)(2,1)} custom-call(bf16[3072,128]{1,0:T(8,128)(2,1)} %bitcast.16, f32[3,384,384]{2,1,0:T(8,128)} %get-tuple-element.12.p_ref, f32[3,16,128]{2,1,0:T(8,128)} %get-tuple-element.13.tx_ref, f32[3,16,128]{2,1,0:T(8,128)} %get-tuple-element.14.ty_ref, s32[3,16,128]{2,1,0:T(8,128)} %get-tuple-element.15.idx_smem, ...), custom_call_target="tpu_custom_call" | custom-call | tf_op jit(solution)/shard_map/sample/pallas_call | solution.py:385
  143.8 0.0 copy-start
  143.8 21.4 %exchange.3.back_ref = bf16[64,24,128]{2,1,0:T(8,128)(2,1)} custom-call(bf16[64,24,128]{2,1,0:T(8,128)(2,1)} %sample.1.x_ref), custom_call_target="tpu_custom_call" | custom-call | tf_op jit(solution)/shard_map/exchange/pallas_call | solution.py:195
  165.2 2.8 %unpack.1 = bf16[3,169,192]{2,1,0:T(8,128)(2,1)} custom-call(s32[1,192]{1,0:T(1,128)} %bitcast.25, bf16[64,24,128]{2,1,0:T(8,128)(2,1)} %exchange.3.back_ref), custom_call_target="tpu_custom_call" | custom-call | tf_op jit(solution)/shard_map/unpack/pallas_call | solution.py:139
  168.1 0.0 copy-done
  168.1 0.7 copy.12
Async XLA Ops:
  143.8 24.2 %copy-start = (f32[8,96,128]{2,1,0:T(8,128)S(1)}, f32[8,96,128]{2,1,0:T(8,128)}, u32[]{:S(2)}) copy-start(f32[8,96,128]{2,1,0:T(8,128)} %get-tuple-element.10) | copy-start | bytes 1179652

commit v3 on v2

v3 whole, which is shorter than its diff:
```python
import math

import jax
import jax.numpy as jnp
from jax import lax
from jax.experimental import pallas as pl
from jax.experimental.pallas import tpu as pltpu
from jax.sharding import PartitionSpec as P

SWEEPS = 2
GX = 8
NY = 64
NZ = 256
LAYERS = NZ // 128

L = 169
Q = 338
B = 16
REM = L - 128

CAP = 6
PLANES = 13
OUT_PLANES = 4
QP = 384

LINE = 3 * LAYERS
TILES = GX * NY * LAYERS
ROWS = TILES * 3

kernel_width = 0.8
coupling = 2.0
SCALE = math.sqrt(0.5 * math.log2(math.e)) / kernel_width
LOG_NORM = -math.log2(0.8 * math.sqrt(2.0 * math.pi))

F32 = jnp.float32
BF16 = jnp.bfloat16
NT = (((1,), (1,)), ((), ()))
NN = (((1,), (0,)), ((), ()))
TN = (((0,), (0,)), ((), ()))

VMEM_SPEC = pl.BlockSpec(memory_space=pltpu.VMEM)
ANY_SPEC = pl.BlockSpec(memory_space=pl.ANY)


def dot(a, b, dims):
    return lax.dot_general(a, b, dims, preferred_element_type=F32)


GROUP = 4
LINES = CAP * B
DEAD = 255


def relative(owner, me):
    y = (owner // 16 - me // 16 + 4) % 4
    z = (owner // 2 % 8 - me // 2 % 8 + 8) % 8
    core = (owner % 2 - me % 2 + 2) % 2
    return y * 16 + z * 2 + core


def peer_of(me, step):
    y = (me // 16 + step // 16) % 4
    z = (me // 2 % 8 + step // 2 % 8) % 8
    core = (me % 2 + step % 2) % 2
    return y * 16 + z * 2 + core


def slot_onehot(owner_ref, slab_count, me):
    cells = owner_ref.shape[1]
    owner = relative(owner_ref[...], me)
    slab_at = lax.broadcasted_iota(jnp.int32, (slab_count, cells), 0)
    member = jnp.where(slab_at == owner, 1.0, 0.0)
    first = lax.broadcasted_iota(jnp.int32, (cells, cells), 0)
    second = lax.broadcasted_iota(jnp.int32, (cells, cells), 1)
    before = jnp.where(first < second, 1.0, 0.0).astype(BF16)
    rank = jnp.sum(member * dot(member.astype(BF16), before, NN), axis=0, keepdims=True)
    slot = owner * CAP + rank.astype(jnp.int32)
    at = lax.broadcasted_iota(jnp.int32, (slab_count * CAP, cells), 0)
    return jnp.where(at == slot, 1.0, 0.0).astype(BF16)


def greet_all(me, count):
    barrier = pltpu.get_barrier_semaphore()

    def greet(step, carry):
        pl.semaphore_signal(
            barrier, inc=1, device_id={"slab": peer_of(me, step)},
            device_id_type=pl.DeviceIdType.MESH,
        )
        return carry

    lax.fori_loop(1, count, greet, 0)
    return barrier


def pack_blocks(
    hot, coef_ref, offs_ref, anchor_ref, blocks_ref, count_ref, send_ref, x_ref, blk_ref, rows_ref
):
    slab_count = send_ref.shape[0]
    slots = slab_count * CAP
    rows_ref[...] = jnp.zeros_like(rows_ref)
    for k in range(3):
        x_ref[k] = dot(hot, coef_ref[k, :128, :], NT)
        rows_ref[k * REM : (k + 1) * REM] = coef_ref[k, 128:, :].astype(F32)
    x_ref[3] = dot(hot, rows_ref[...].astype(BF16), NT)
    tail = jnp.zeros((slots, QP - Q), F32)
    rows_ref[...] = jnp.zeros_like(rows_ref)
    for k in range(3):
        place = anchor_ref[k : k + 1, :]
        rows_ref[112:113] = (place % 128 if k == 2 else place).astype(F32)
        got = dot(hot, offs_ref[k], NN)
        x_ref[4 + 3 * k] = got[:, :128]
        x_ref[5 + 3 * k] = got[:, 128:256]
        x_ref[6 + 3 * k] = jnp.concatenate([got[:, 256:], tail], axis=1) + dot(
            hot, rows_ref[...].astype(BF16), NT
        )
    live = lax.broadcasted_iota(jnp.int32, blocks_ref.shape, 0) < count_ref[...]
    tile = blocks_ref[...]
    y = tile // LAYERS % NY + (tile % LAYERS) * NY
    lists = (tile // (NY * LAYERS), y)
    lane = lax.broadcasted_iota(jnp.int32, (slots, 128), 1) // B
    slot = lax.broadcasted_iota(jnp.int32, (slots, 128), 0) % CAP
    for n in range(2):
        values = jnp.where(live, lists[n], DEAD).astype(F32)
        for i in range(128 // B):
            rows_ref[i * B : (i + 1) * B] = values
        x_ref[PLANES + n] = jnp.where(lane == slot, dot(hot, rows_ref[...].astype(BF16), NT), 0.0)

    def step(target, carry):
        for r in range(PLANES):
            blk_ref[pl.ds(r * CAP, CAP), :] = x_ref[r, pl.ds(target * CAP, CAP), :]
        for n in range(2):
            blk_ref[pl.ds(PLANES * CAP + n, 1), :] = jnp.sum(
                x_ref[PLANES + n, pl.ds(target * CAP, CAP), :], axis=0, keepdims=True
            )
        send_ref[target] = blk_ref[...].astype(BF16)
        return carry

    lax.fori_loop(0, slab_count, step, 0)


def basis_planes(basis_ref, wide_ref, planes_ref):
    wide_ref[...] = jnp.zeros_like(wide_ref)
    wide_ref[:128, :Q] = basis_ref[:128, :].astype(F32)
    for k in range(3):
        if k > 0:
            wide_ref[128 + (k - 1) * REM : 128 + k * REM, :Q] = jnp.zeros((REM, Q), F32)
        wide_ref[128 + k * REM : 128 + (k + 1) * REM, :Q] = basis_ref[128:, :].astype(F32)
        planes_ref[k] = wide_ref[...].astype(BF16)


def z_weights(pz):
    step = lax.broadcasted_iota(jnp.int32, (8, QP), 0).astype(F32) * SCALE
    base = pz - step
    parts = []
    for g in range(16):
        d = base - (8.0 * g * SCALE)
        parts.append(jnp.exp2(LOG_NORM - d * d))
    return jnp.concatenate(parts, axis=0).astype(BF16)


def columns(row):
    first = lax.broadcasted_iota(jnp.int32, (128, 128), 0)
    second = lax.broadcasted_iota(jnp.int32, (128, 128), 1)
    diagonal = jnp.where(first == second, row, 0.0).astype(BF16)
    return dot(diagonal, jnp.ones((128, 128), BF16), NN)


def split_y(row):
    layer = jnp.where(row >= NY, 1.0, 0.0)
    return row - NY * layer, layer


def stencil_columns(x_row, y_row, tx_ref, ty_ref):
    for n in range(QP // 128):
        tx_ref[:, n * 128 : (n + 1) * 128] = columns(x_row) * SCALE
        ty_ref[:, n * 128 : (n + 1) * 128] = columns(split_y(y_row)[0]) * SCALE


def xy_weights(px, py, tx, ty):
    dx = px - tx
    dy = py - ty
    return jnp.exp2(2.0 * LOG_NORM - (dx * dx + dy * dy))


def spread_kernel(
    owner_ref, coef_ref, offs_ref, anchor_ref, blocks_ref, count_ref, syn_ref,
    part_ref, p_ref, lists_ref, idx_ref,
    x_ref, blk_ref, rows_ref, send_ref, recv_ref, r_ref, f_ref, tx_ref, ty_ref,
    t_ref, acc_ref, part32_ref, wide_ref, basis_ref, send_sem, recv_sem,
):
    slab_count = send_ref.shape[0]
    me = lax.axis_index("slab")
    barrier = greet_all(me, slab_count)
    hot = slot_onehot(owner_ref, slab_count, me)
    pack_blocks(
        hot, coef_ref, offs_ref, anchor_ref, blocks_ref, count_ref,
        send_ref, x_ref, blk_ref, rows_ref,
    )
    pl.semaphore_wait(barrier, slab_count - 1)

    def send(step, carry):
        pltpu.make_async_remote_copy(
            src_ref=send_ref.at[step],
            dst_ref=recv_ref.at[step],
            send_sem=send_sem,
            recv_sem=recv_sem.at[step],
            device_id={"slab": peer_of(me, step)},
            device_id_type=pl.DeviceIdType.MESH,
        ).start()
        return carry

    lax.fori_loop(1, slab_count, send, 0)
    recv_ref[0] = send_ref[0]
    basis_planes(syn_ref, wide_ref, basis_ref)
    acc_ref[...] = jnp.zeros_like(acc_ref)
    t_ref[...] = jnp.zeros_like(t_ref)

    def wait(step):
        pltpu.make_async_copy(recv_ref.at[step], recv_ref.at[step], recv_sem.at[step]).wait()

    def take(g, h, wait_for):
        step = g * GROUP + h
        if wait_for:
            wait(step)
        blk_ref[...] = recv_ref[step].astype(F32)
        for r in range(PLANES):
            r_ref[r, pl.ds(h * CAP, CAP), :] = blk_ref[r * CAP : (r + 1) * CAP, :]
        lists_ref[pl.ds(step * 2, 2), :] = blk_ref[PLANES * CAP : PLANES * CAP + 2, :]

    def work(g):
        rows = pl.ds(pl.multiple_of(g * GROUP * CAP, 8), GROUP * CAP)
        for k in range(3):
            anchor = r_ref[6 + 3 * k][:, 112:113]
            for t in range(3):
                p_ref[k, rows, t * 128 : (t + 1) * 128] = (r_ref[4 + 3 * k + t] + anchor) * SCALE
            coef = jnp.concatenate([r_ref[k], r_ref[3]], axis=1).astype(BF16)
            f_ref[k] = dot(coef, basis_ref[k], NN)

        def source(h, carry):
            step = g * GROUP + h
            x_row, y_row = lists_ref[pl.ds(step * 2, 1), :], lists_ref[pl.ds(step * 2 + 1, 1), :]
            stencil_columns(x_row, y_row, tx_ref, ty_ref)
            y, layer = split_y(y_row)
            place = jnp.where(x_row < DEAD, (x_row * NY + y) * LINE + layer, 0.0)
            idx_ref[pl.ds(step, 1), :] = place.astype(jnp.int32)
            for i in range(CAP):
                c = step * CAP + i
                lines = slice(i * B, (i + 1) * B)
                wxy = xy_weights(
                    p_ref[0, pl.ds(c, 1), :], p_ref[1, pl.ds(c, 1), :],
                    tx_ref[lines], ty_ref[lines],
                )
                weighted = jnp.concatenate(
                    [wxy * f_ref[k, pl.ds(h * CAP + i, 1), :] for k in range(3)], axis=0
                ).astype(BF16)
                terms = dot(weighted, z_weights(p_ref[2, pl.ds(c, 1), :]), NT).astype(BF16)
                at = pl.ds(pl.multiple_of(h * 128 + i * B, B), B)
                for k in range(3):
                    t_ref[at, k * 128 : (k + 1) * 128] = terms[k * B : (k + 1) * B]
            return carry

        lax.fori_loop(0, GROUP, source, 0)
        tile = lax.broadcasted_iota(jnp.int32, (NY * LAYERS, 128), 0).astype(F32)
        hits, x_rows = [], []
        for h in range(GROUP):
            step = g * GROUP + h
            x_rows.append(lists_ref[pl.ds(step * 2, 1), :])
            hits.append(jnp.where(tile == lists_ref[pl.ds(step * 2 + 1, 1), :], 1.0, 0.0).astype(BF16))
        for x in range(GX):
            picked = jnp.concatenate(
                [
                    hit * jnp.where(x_row == float(x), 1.0, 0.0).astype(BF16)
                    for hit, x_row in zip(hits, x_rows)
                ],
                axis=1,
            )
            acc_ref[x] += dot(picked, t_ref[...], NN)

    for h in range(GROUP):
        take(0, h, h > 0)
    work(0)

    def group(g, carry):
        for h in range(GROUP):
            take(g, h, True)
        work(g)
        return carry

    lax.fori_loop(1, slab_count // GROUP, group, 0)
    for x in range(GX):
        for layer in range(LAYERS):
            for k in range(3):
                part32_ref[pl.ds(x * NY * LINE + k * LAYERS + layer, NY, stride=LINE), :] = acc_ref[
                    x, layer * NY : (layer + 1) * NY, k * 128 : (k + 1) * 128
                ]
    part_ref[...] = part32_ref[...].astype(BF16)
    others = pl.ds(1, slab_count - 1)
    pltpu.make_async_copy(send_ref.at[others], send_ref.at[others], send_sem).wait()


def spread(owner, coef, offs, anchor, blocks, count, syn, slab_count, collective_id):
    block_rows = PLANES * CAP + 2
    slots = slab_count * CAP
    held = GROUP * CAP
    return pl.pallas_call(
        spread_kernel,
        out_shape=(
            jax.ShapeDtypeStruct((ROWS, 128), BF16),
            jax.ShapeDtypeStruct((3, slots, QP), F32),
            jax.ShapeDtypeStruct((2 * slab_count, 128), F32),
            jax.ShapeDtypeStruct((slab_count, 128), jnp.int32),
        ),
        in_specs=[VMEM_SPEC] * 7,
        out_specs=(VMEM_SPEC,) * 4,
        scratch_shapes=[
            pltpu.VMEM((PLANES + 2, slots, 128), F32),
            pltpu.VMEM((block_rows, 128), F32),
            pltpu.VMEM((128, owner.shape[1]), F32),
            pltpu.VMEM((slab_count, block_rows, 128), BF16),
            pltpu.VMEM((slab_count, block_rows, 128), BF16),
            pltpu.VMEM((PLANES, held, 128), F32),
            pltpu.VMEM((3, held, QP), F32),
            pltpu.VMEM((128, QP), F32),
            pltpu.VMEM((128, QP), F32),
            pltpu.VMEM((GROUP * 128, QP), BF16),
            pltpu.VMEM((GX, NY * LAYERS, QP), F32),
            pltpu.VMEM((ROWS, 128), F32),
            pltpu.VMEM((256, QP), F32),
            pltpu.VMEM((3, 256, QP), BF16),
            pltpu.SemaphoreType.DMA,
            pltpu.SemaphoreType.DMA((slab_count,)),
        ],
        compiler_params=pltpu.CompilerParams(collective_id=collective_id, has_side_effects=True),
        name="spread",
    )(owner, coef, offs, anchor, blocks, count, syn)


def sample_kernel(
    owner_ref, vel_ref, p_ref, lists_ref, idx_smem, ana_ref, out_ref,
    v_ref, g_ref, pv_ref, c_ref, blk_ref, tx_ref, ty_ref, send_ref, back_ref, r_ref,
    wide_ref, basis_ref, send_sem, recv_sem,
):
    slab_count = send_ref.shape[0]
    me = lax.axis_index("slab")
    barrier = greet_all(me, slab_count)
    v_ref[...] = vel_ref[...].astype(F32)
    basis_planes(ana_ref, wide_ref, basis_ref)

    def work(g):
        def source(h, carry):
            step = g * GROUP + h
            for i in range(CAP):
                for j in range(B):
                    start = idx_smem[step, i * B + j]
                    g_ref[i, pl.ds(j, 3, stride=B), :] = v_ref[pl.ds(start, 3, stride=LAYERS), :]
            x_row, y_row = lists_ref[pl.ds(step * 2, 1), :], lists_ref[pl.ds(step * 2 + 1, 1), :]
            stencil_columns(x_row, y_row, tx_ref, ty_ref)
            for i in range(CAP):
                c = step * CAP + i
                lines = slice(i * B, (i + 1) * B)
                wxy = xy_weights(
                    p_ref[0, pl.ds(c, 1), :], p_ref[1, pl.ds(c, 1), :],
                    tx_ref[lines], ty_ref[lines],
                )
                wz = z_weights(p_ref[2, pl.ds(c, 1), :])
                projected = dot(g_ref[i].astype(BF16), wz, NN)
                for k in range(3):
                    pv_ref[k, pl.ds(h * CAP + i, 1), :] = jnp.sum(
                        projected[k * B : (k + 1) * B] * wxy, axis=0, keepdims=True
                    )
            return carry

        lax.fori_loop(0, GROUP, source, 0)
        rem = jnp.zeros((GROUP * CAP, 128), F32)
        for k in range(3):
            got = dot(pv_ref[k].astype(BF16), basis_ref[k], NT)
            c_ref[k] = got[:, :128]
            rem = rem + got[:, 128:]
        c_ref[3] = rem
        for h in range(GROUP):
            for r in range(OUT_PLANES):
                blk_ref[r * CAP : (r + 1) * CAP, :] = c_ref[r, h * CAP : (h + 1) * CAP, :]
            send_ref[g * GROUP + h] = blk_ref[...].astype(BF16)

    def send(step):
        pltpu.make_async_remote_copy(
            src_ref=send_ref.at[step],
            dst_ref=back_ref.at[step],
            send_sem=send_sem,
            recv_sem=recv_sem,
            device_id={"slab": peer_of(me, relative(0, step))},
            device_id_type=pl.DeviceIdType.MESH,
        ).start()

    groups = slab_count // GROUP
    work(groups - 1)
    pl.semaphore_wait(barrier, slab_count - 1)

    def group(n, carry):
        g = groups - 2 - n
        for h in range(GROUP):
            send((g + 1) * GROUP + h)
        work(g)
        return carry

    lax.fori_loop(0, groups - 1, group, 0)
    for h in range(1, GROUP):
        send(h)
    back_ref[0] = send_ref[0]
    hot = slot_onehot(owner_ref, slab_count, me)
    others = pl.ds(1, slab_count - 1)
    pltpu.make_async_copy(back_ref.at[others], back_ref.at[others], recv_sem).wait()

    def take(step, carry):
        blk_ref[...] = back_ref[step].astype(F32)
        for r in range(OUT_PLANES):
            r_ref[r, pl.ds(step * CAP, CAP), :] = blk_ref[r * CAP : (r + 1) * CAP, :]
        return carry

    lax.fori_loop(0, slab_count, take, 0)
    rem = dot(r_ref[3].astype(BF16), hot, TN)
    for k in range(3):
        main = dot(r_ref[k].astype(BF16), hot, TN)
        out_ref[k] = jnp.concatenate([main, rem[k * REM : (k + 1) * REM]], axis=0).astype(BF16)
    pltpu.make_async_copy(send_ref.at[others], send_ref.at[others], send_sem).wait()


def sample(owner, vel, p, lists, idx, ana, slab_count, collective_id):
    slots = slab_count * CAP
    block_rows = OUT_PLANES * CAP
    held = GROUP * CAP
    return pl.pallas_call(
        sample_kernel,
        out_shape=jax.ShapeDtypeStruct((3, L, owner.shape[1]), BF16),
        in_specs=[VMEM_SPEC] * 4 + [pl.BlockSpec(memory_space=pltpu.SMEM), VMEM_SPEC],
        out_specs=VMEM_SPEC,
        scratch_shapes=[
            pltpu.VMEM((ROWS, 128), F32),
            pltpu.VMEM((CAP, 3 * B, 128), F32),
            pltpu.VMEM((3, held, QP), F32),
            pltpu.VMEM((OUT_PLANES, held, 128), F32),
            pltpu.VMEM((block_rows, 128), F32),
            pltpu.VMEM((128, QP), F32),
            pltpu.VMEM((128, QP), F32),
            pltpu.VMEM((slab_count, block_rows, 128), BF16),
            pltpu.VMEM((slab_count, block_rows, 128), BF16),
            pltpu.VMEM((OUT_PLANES, slots, 128), F32),
            pltpu.VMEM((256, QP), F32),
            pltpu.VMEM((3, 256, QP), BF16),
            pltpu.SemaphoreType.DMA,
            pltpu.SemaphoreType.DMA,
        ],
        compiler_params=pltpu.CompilerParams(collective_id=collective_id, has_side_effects=True),
        name="sample",
    )(owner, vel, p, lists, idx, ana)


def grid_kernel(
    part_ref, vel_ref, new_ref, all_ref,
    hop_ref, got_ref, summed_ref, drive_ref, st_ref, own_ref,
    xs_ref, xr_ref, ys_ref, yr_ref, y32_ref, send_sem, recv_sem, local_sem,
):
    planes, mine, _ = vel_ref.shape
    half = planes // 2
    batches, slabs = lax.axis_size("batch"), lax.axis_size("slab")
    b, s = lax.axis_index("batch"), lax.axis_index("slab")
    right, far, left = [lax.rem(b + i, batches) for i in (1, 2, 3)]
    above, below = lax.rem(s + 1, slabs), lax.rem(s + slabs - 1, slabs)

    barrier = pltpu.get_barrier_semaphore()
    for device in ({"batch": right}, {"batch": left}, {"slab": above}, {"slab": below}):
        pl.semaphore_signal(
            barrier, inc=1, device_id=device, device_id_type=pl.DeviceIdType.MESH
        )
    pl.semaphore_wait(barrier, 4)

    def rows(part):
        return pl.ds(pl.multiple_of(part * mine, mine), mine)

    started = []

    def send(src, dst, **device):
        n = len(started)
        copy = pltpu.make_async_remote_copy(
            src_ref=src, dst_ref=dst, send_sem=send_sem.at[n], recv_sem=recv_sem.at[n],
            device_id=device, device_id_type=pl.DeviceIdType.MESH,
        )
        copy.start()
        started.append(copy)
        return copy

    low, high = pl.ds(0, half), pl.ds(half, half)

    hop_r = send(part_ref.at[low, rows(far)], hop_ref.at[0], batch=right)
    hop_l = send(part_ref.at[high, rows(far)], hop_ref.at[1], batch=left)
    near_r = send(part_ref.at[high, rows(right)], got_ref.at[0], batch=right)
    near_l = send(part_ref.at[low, rows(left)], got_ref.at[1], batch=left)
    hop_r.wait_recv()
    summed_ref[0] = (
        part_ref[low, rows(right), :].astype(F32) + hop_ref[0].astype(F32)
    ).astype(BF16)
    far_r = send(summed_ref.at[0], got_ref.at[2], batch=right)
    hop_l.wait_recv()
    summed_ref[1] = (
        part_ref[high, rows(left), :].astype(F32) + hop_ref[1].astype(F32)
    ).astype(BF16)
    far_l = send(summed_ref.at[1], got_ref.at[3], batch=left)
    drive_ref[...] = vel_ref[...] + part_ref[:, rows(b), :].astype(F32)
    near_r.wait_recv()
    near_l.wait_recv()
    far_r.wait_recv()
    far_l.wait_recv()
    drive_ref[:half] += got_ref[1].astype(F32) + got_ref[2].astype(F32)
    drive_ref[half:] += got_ref[0].astype(F32) + got_ref[3].astype(F32)

    lane = lax.broadcasted_iota(jnp.int32, (mine, 128), 1)
    layer = lax.broadcasted_iota(jnp.int32, (mine, 128), 0) % LAYERS
    at_end, at_start = lane == 127, lane == 0
    has_next, has_previous = layer < LAYERS - 1, layer > 0
    inside = slice(8, 8 + mine)
    for sweep in range(SWEEPS):
        for x in range(planes):
            st_ref[1 + x, inside, :] = drive_ref[x] if sweep == 0 else new_ref[x]
        xs_ref[sweep, 0] = st_ref[planes, inside, :].astype(BF16)
        xs_ref[sweep, 1] = st_ref[1, inside, :].astype(BF16)
        for x in range(planes):
            y32_ref[0, x * LINE : (x + 1) * LINE] = st_ref[1 + x, 2 + mine : 8 + mine, :]
            y32_ref[1, x * LINE : (x + 1) * LINE] = st_ref[1 + x, 8 : 8 + LINE, :]
        for side in range(2):
            ys_ref[sweep, side] = y32_ref[side].astype(BF16)
        copies = [
            send(xs_ref.at[sweep, 0], xr_ref.at[sweep, 0], slab=above),
            send(xs_ref.at[sweep, 1], xr_ref.at[sweep, 1], slab=below),
            send(ys_ref.at[sweep, 0], yr_ref.at[sweep, 0], batch=right),
            send(ys_ref.at[sweep, 1], yr_ref.at[sweep, 1], batch=left),
        ]
        for copy in copies:
            copy.wait_recv()
        x_low, x_high = xr_ref[sweep, 0].astype(F32), xr_ref[sweep, 1].astype(F32)
        st_ref[0, inside, :] = jnp.where(s > 0, x_low, 0.0)
        st_ref[planes + 1, inside, :] = jnp.where(s < slabs - 1, x_high, 0.0)
        y32_ref[0] = jnp.where(b > 0, yr_ref[sweep, 0].astype(F32), 0.0)
        y32_ref[1] = jnp.where(b < batches - 1, yr_ref[sweep, 1].astype(F32), 0.0)
        for x in range(planes):
            st_ref[1 + x, 8 - LINE : 8, :] = y32_ref[0, x * LINE : (x + 1) * LINE]
            st_ref[1 + x, 8 + mine : 8 + mine + LINE, :] = y32_ref[1, x * LINE : (x + 1) * LINE]
        for x in range(planes):
            total = (
                st_ref[x, inside, :]
                + st_ref[x + 2, inside, :]
                + st_ref[x + 1, 8 - LINE : 8 - LINE + mine, :]
                + st_ref[x + 1, 8 + LINE : 8 + LINE + mine, :]
            )
            centre = st_ref[x + 1, inside, :]
            after = jnp.where(has_next, st_ref[x + 1, 9 : 9 + mine, :], 0.0)
            before = jnp.where(has_previous, st_ref[x + 1, 7 : 7 + mine, :], 0.0)
            upper = pltpu.roll(jnp.where(at_start, after, centre), 127, 1)
            lower = pltpu.roll(jnp.where(at_end, before, centre), 1, 1)
            total = total + upper + lower
            new_ref[x] = (drive_ref[x] + coupling * total) * (1.0 / (1.0 + 6.0 * coupling))

    own_ref[...] = new_ref[...].astype(BF16)
    at_right_low = send(own_ref.at[low], all_ref.at[low, rows(b)], batch=right)
    at_left_high = send(own_ref.at[high], all_ref.at[high, rows(b)], batch=left)
    at_right_high = send(own_ref.at[high], all_ref.at[high, rows(b)], batch=right)
    at_left_low = send(own_ref.at[low], all_ref.at[low, rows(b)], batch=left)
    local = pltpu.make_async_copy(own_ref, all_ref.at[:, rows(b)], local_sem)
    local.start()
    at_right_low.wait_recv()
    on_r = send(all_ref.at[low, rows(left)], all_ref.at[low, rows(left)], batch=right)
    at_left_high.wait_recv()
    on_l = send(all_ref.at[high, rows(right)], all_ref.at[high, rows(right)], batch=left)
    for copy in (at_right_high, at_left_low, on_r, on_l):
        copy.wait_recv()
    local.wait()
    for copy in started:
        copy.wait_send()


def grid_step(part, vel, collective_id):
    planes, mine, _ = vel.shape
    half = planes // 2
    copies = 6 + 4 * SWEEPS + 6
    return pl.pallas_call(
        grid_kernel,
        out_shape=(
            jax.ShapeDtypeStruct(vel.shape, F32),
            jax.ShapeDtypeStruct(part.shape, BF16),
        ),
        in_specs=[VMEM_SPEC] * 2,
        out_specs=(VMEM_SPEC, ANY_SPEC),
        scratch_shapes=[
            pltpu.VMEM((2, half, mine, 128), BF16),
            pltpu.VMEM((4, half, mine, 128), BF16),
            pltpu.VMEM((2, half, mine, 128), BF16),
            pltpu.VMEM((planes, mine, 128), F32),
            pltpu.VMEM((planes + 2, mine + 16, 128), F32),
            pltpu.VMEM((planes, mine, 128), BF16),
            pltpu.VMEM((SWEEPS, 2, mine, 128), BF16),
            pltpu.VMEM((SWEEPS, 2, mine, 128), BF16),
            pltpu.VMEM((SWEEPS, 2, planes * LINE, 128), BF16),
            pltpu.VMEM((SWEEPS, 2, planes * LINE, 128), BF16),
            pltpu.VMEM((2, planes * LINE, 128), F32),
            pltpu.SemaphoreType.DMA((copies,)),
            pltpu.SemaphoreType.DMA((copies,)),
            pltpu.SemaphoreType.DMA,
        ],
        compiler_params=pltpu.CompilerParams(collective_id=collective_id, has_side_effects=True),
        name="grid_step",
    )(part, vel)


def local(
    velocity_old, traction, offsets, owner_slab, anchor, blocks, block_count, synthesis, analysis
):
    slab_count = lax.axis_size("slab")
    owner = owner_slab.T
    part, p, lists, idx = spread(
        owner,
        traction.transpose(1, 2, 0),
        offsets.transpose(1, 0, 2),
        anchor.T,
        blocks.T,
        block_count[None],
        synthesis,
        slab_count,
        0,
    )
    planes, lines = velocity_old.shape[:2]
    velocity = velocity_old.transpose(0, 1, 3, 2, 4).reshape(planes, lines * LINE, 128)
    velocity_new, slab_velocity = grid_step(part.reshape(planes, NY * LINE, 128), velocity, 2)
    velocity_coef = sample(
        owner, slab_velocity.reshape(ROWS, 128), p, lists, idx, analysis, slab_count, 1
    )
    velocity_new = velocity_new.reshape(planes, lines, 3, LAYERS, 128)
    return (velocity_new.transpose(0, 1, 3, 2, 4), velocity_coef.transpose(2, 0, 1))


def solution(mesh):
    in_specs = (
        P("slab", "batch", None, None, None),
        P(("slab", "batch"), None, None),
        P(("slab", "batch"), None, None),
        P(("slab", "batch"), None),
        P(("slab", "batch"), None),
        P(("slab", "batch"), None),
        P(("slab", "batch")),
        P(),
        P(),
    )
    out_specs = (P("slab", "batch", None, None, None), P(("slab", "batch"), None, None))
    return jax.shard_map(local, mesh=mesh, in_specs=in_specs, out_specs=out_specs, check_vma=False)
```

time: 170 us -> 151 us (0.89)
  Pallas kernels: 167 us -> 147 us
    pallas_call x5 -> x1, Pallas kernels: 102 us -> 50 us  [sample(): pl.pallas_call(sample_kernel, out_shape=jax.ShapeDtypeStruct((3, L, owner...]
    pallas_call x1, Pallas kernels: 37.5 us -> 69 us  [spread(): pl.pallas_call(spread_kernel, out_shape=(jax.ShapeDtypeStruct((ROWS, 128)...]
where the time goes in v3:
time: 151 us; the launch traced here: 150 us
  Pallas kernels  147 us (97%)
  local copies, waits for them, and re-layouts  2.43 us (2%)
    pallas_call x1, Pallas kernels, spread(): pl.pallas_call(spread_kernel, out_shape=(jax.ShapeDtypeStruct((ROWS, 128)...  69 us
    pallas_call x1, Pallas kernels, sample(): pl.pallas_call(sample_kernel, out_shape=jax.ShapeDtypeStruct((3, L, owner...  50 us
    pallas_call x1, Pallas kernels, grid_step(): pl.pallas_call(grid_kernel, out_shape=(jax.ShapeDtypeStruct(vel.shape, F3...  28.3 us

profile of v3, /device:TPU:1, one launch (start us, length us, event | category | flops | bytes accessed | tf_op | source)
XLA Modules:
  0.0 150.4 jit_solution(4259669224952328261)
XLA Ops:
  0.6 69.0 %spread.1 = (bf16[3072,128]{1,0:T(8,128)(2,1)}, f32[3,384,384]{2,1,0:T(8,128)}, f32[128,128]{1,0:T(8,128)}, s32[64,128]{1,0:T(8,128)}) custom-call(s32[1,192]{1,0:T(1,128)} %bitcast.24, bf16[3,169,192]{2,1,0:T(8,128)(2,1)} %bitcast.21, bf16[3,192,338]{2,1,0:T(8,128)(2,1)} %bitcast.18, s32[3,192]{1,0:T(4,128)} %bitcast.23, s32[16,192]{1,0:T(8,128)} %bitcast.22, ...), custom_call_target="tpu_custom_call" | custom-call | tf_op jit(solution)/shard_map/spread/pallas_call | solution.py:306
  69.6 28.3 %grid_step.1 = (f32[8,96,128]{2,1,0:T(8,128)}, bf16[8,384,128]{2,1,0:T(8,128)(2,1)}) custom-call(bf16[8,384,128]{2,1,0:T(8,128)(2,1)} %bitcast.16, f32[8,96,128]{2,1,0:T(8,128)} %bitcast.20), custom_call_target="tpu_custom_call" | custom-call | tf_op jit(solution)/shard_map/grid_step/pallas_call | solution.py:585
  97.9 0.0 copy-start
  97.9 50.0 %sample.1 = bf16[3,169,192]{2,1,0:T(8,128)(2,1)} custom-call(s32[1,192]{1,0:T(1,128)} %bitcast.25, bf16[3072,128]{1,0:T(8,128)(2,1)} %bitcast.17, f32[3,384,384]{2,1,0:T(8,128)} %get-tuple-element.11.p_ref, f32[128,128]{1,0:T(8,128)} %get-tuple-element.12.lists_ref, s32[64,128]{1,0:T(8,128)} %get-tuple-element.13.idx_smem, bf16[169,338]{1,0:T(8,128)(2,1)} %ana_ref.1), custom_call_target="tpu_custom_call" | custom-call | tf_op jit(solution)/shard_map/sample/pallas_call | solution.py:433
  148.0 0.0 copy-done
  148.0 0.7 copy.13
  148.7 1.7 %copy.14 = bf16[192,3,169]{0,2,1:T(8,128)(2,1)} copy(bf16[192,3,169]{0,2,1:T(8,128)(2,1)} %bitcast.15) | data formatting | bytes 389376
Async XLA Ops:
  97.9 50.0 %copy-start = (f32[8,96,128]{2,1,0:T(8,128)S(1)}, f32[8,96,128]{2,1,0:T(8,128)}, u32[]{:S(2)}) copy-start(f32[8,96,128]{2,1,0:T(8,128)} %get-tuple-element.9) | copy-start | bytes 1179652

commit v4 on v3

--- a/solution.py
+++ b/solution.py
@@ -39,7 +39,6 @@
 TN = (((0,), (0,)), ((), ()))
 
 VMEM_SPEC = pl.BlockSpec(memory_space=pltpu.VMEM)
-ANY_SPEC = pl.BlockSpec(memory_space=pl.ANY)
 
 
 def dot(a, b, dims):
@@ -171,33 +170,22 @@
     return row - NY * layer, layer
 
 
-def stencil_columns(x_row, y_row, tx_ref, ty_ref):
+def xy_weights(px, py, tx, ty):
+    parts = []
     for n in range(QP // 128):
-        tx_ref[:, n * 128 : (n + 1) * 128] = columns(x_row) * SCALE
-        ty_ref[:, n * 128 : (n + 1) * 128] = columns(split_y(y_row)[0]) * SCALE
-
-
-def xy_weights(px, py, tx, ty):
-    dx = px - tx
-    dy = py - ty
-    return jnp.exp2(2.0 * LOG_NORM - (dx * dx + dy * dy))
-
-
-def spread_kernel(
-    owner_ref, coef_ref, offs_ref, anchor_ref, blocks_ref, count_ref, syn_ref,
-    part_ref, p_ref, lists_ref, idx_ref,
-    x_ref, blk_ref, rows_ref, send_ref, recv_ref, r_ref, f_ref, tx_ref, ty_ref,
-    t_ref, acc_ref, part32_ref, wide_ref, basis_ref, send_sem, recv_sem,
+        lanes = slice(n * 128, (n + 1) * 128)
+        dx = px[:, lanes] - tx
+        dy = py[:, lanes] - ty
+        parts.append(jnp.exp2(2.0 * LOG_NORM - (dx * dx + dy * dy)))
+    return jnp.concatenate(parts, axis=1)
+
+
+def spread_cells(
+    me, syn_ref, send_ref, recv_ref, send_sem, recv_sem, part_ref, wz_ref, wxy_ref, idx_ref,
+    blk_ref, r_ref, p_ref, f_ref, lists_ref, tx_ref, ty_ref,
+    t_ref, t_old_ref, hit_ref, x_old_ref, acc_ref, part32_ref, wide_ref, basis_ref,
 ):
     slab_count = send_ref.shape[0]
-    me = lax.axis_index("slab")
-    barrier = greet_all(me, slab_count)
-    hot = slot_onehot(owner_ref, slab_count, me)
-    pack_blocks(
-        hot, coef_ref, offs_ref, anchor_ref, blocks_ref, count_ref,
-        send_ref, x_ref, blk_ref, rows_ref,
-    )
-    pl.semaphore_wait(barrier, slab_count - 1)
 
     def send(step, carry):
         pltpu.make_async_remote_copy(
@@ -211,141 +199,92 @@
         return carry
 
     lax.fori_loop(1, slab_count, send, 0)
-    recv_ref[0] = send_ref[0]
+    pltpu.make_async_copy(send_ref.at[0], recv_ref.at[0], recv_sem.at[0]).start()
     basis_planes(syn_ref, wide_ref, basis_ref)
-    acc_ref[...] = jnp.zeros_like(acc_ref)
-    t_ref[...] = jnp.zeros_like(t_ref)
-
-    def wait(step):
-        pltpu.make_async_copy(recv_ref.at[step], recv_ref.at[step], recv_sem.at[step]).wait()
-
-    def take(g, h, wait_for):
-        step = g * GROUP + h
-        if wait_for:
-            wait(step)
-        blk_ref[...] = recv_ref[step].astype(F32)
-        for r in range(PLANES):
-            r_ref[r, pl.ds(h * CAP, CAP), :] = blk_ref[r * CAP : (r + 1) * CAP, :]
-        lists_ref[pl.ds(step * 2, 2), :] = blk_ref[PLANES * CAP : PLANES * CAP + 2, :]
-
-    def work(g):
-        rows = pl.ds(pl.multiple_of(g * GROUP * CAP, 8), GROUP * CAP)
+    for ref in (acc_ref, t_ref, t_old_ref, hit_ref, x_old_ref):
+        ref[...] = jnp.zeros_like(ref)
+
+    per_source = GX // GROUP
+
+    def group(g, carry):
+        for h in range(GROUP):
+            step = g * GROUP + h
+            pltpu.make_async_copy(recv_ref.at[step], recv_ref.at[step], recv_sem.at[step]).wait()
+            blk_ref[...] = recv_ref[step].astype(F32)
+            for r in range(PLANES):
+                r_ref[r, h * CAP : (h + 1) * CAP, :] = blk_ref[r * CAP : (r + 1) * CAP, :]
+            lists_ref[h] = blk_ref[PLANES * CAP : PLANES * CAP + 2, :]
         for k in range(3):
             anchor = r_ref[6 + 3 * k][:, 112:113]
             for t in range(3):
-                p_ref[k, rows, t * 128 : (t + 1) * 128] = (r_ref[4 + 3 * k + t] + anchor) * SCALE
+                p_ref[k, :, t * 128 : (t + 1) * 128] = (r_ref[4 + 3 * k + t] + anchor) * SCALE
             coef = jnp.concatenate([r_ref[k], r_ref[3]], axis=1).astype(BF16)
             f_ref[k] = dot(coef, basis_ref[k], NN)
 
         def source(h, carry):
             step = g * GROUP + h
-            x_row, y_row = lists_ref[pl.ds(step * 2, 1), :], lists_ref[pl.ds(step * 2 + 1, 1), :]
-            stencil_columns(x_row, y_row, tx_ref, ty_ref)
+            x_row, y_row = lists_ref[h, 0:1, :], lists_ref[h, 1:2, :]
             y, layer = split_y(y_row)
             place = jnp.where(x_row < DEAD, (x_row * NY + y) * LINE + layer, 0.0)
-            idx_ref[pl.ds(step, 1), :] = place.astype(jnp.int32)
+            idx_ref[pl.ds(step, 1), :] = jnp.clip(place.astype(jnp.int32), 0, ROWS - LINE + LAYERS - 1)
+            tx_ref[...] = columns(x_row) * SCALE
+            ty_ref[...] = columns(y) * SCALE
+            for d in range(per_source):
+                x = h * per_source + d
+                mask = jnp.where(x_old_ref[...] == x.astype(F32), 1.0, 0.0).astype(BF16)
+                acc_ref[x] += dot(hit_ref[...] * mask, t_old_ref[...], NN)
             for i in range(CAP):
                 c = step * CAP + i
+                here = pl.ds(h * CAP + i, 1)
                 lines = slice(i * B, (i + 1) * B)
                 wxy = xy_weights(
-                    p_ref[0, pl.ds(c, 1), :], p_ref[1, pl.ds(c, 1), :],
-                    tx_ref[lines], ty_ref[lines],
+                    p_ref[0, here, :], p_ref[1, here, :], tx_ref[lines], ty_ref[lines]
                 )
+                wxy_ref[c] = wxy
                 weighted = jnp.concatenate(
-                    [wxy * f_ref[k, pl.ds(h * CAP + i, 1), :] for k in range(3)], axis=0
+                    [wxy * f_ref[k, here, :] for k in range(3)], axis=0
                 ).astype(BF16)
-                terms = dot(weighted, z_weights(p_ref[2, pl.ds(c, 1), :]), NT).astype(BF16)
+                wz = z_weights(p_ref[2, here, :])
+                wz_ref[c] = wz
+                terms = dot(weighted, wz, NT).astype(BF16)
                 at = pl.ds(pl.multiple_of(h * 128 + i * B, B), B)
                 for k in range(3):
                     t_ref[at, k * 128 : (k + 1) * 128] = terms[k * B : (k + 1) * B]
             return carry
 
         lax.fori_loop(0, GROUP, source, 0)
+        t_old_ref[...] = t_ref[...]
         tile = lax.broadcasted_iota(jnp.int32, (NY * LAYERS, 128), 0).astype(F32)
-        hits, x_rows = [], []
         for h in range(GROUP):
-            step = g * GROUP + h
-            x_rows.append(lists_ref[pl.ds(step * 2, 1), :])
-            hits.append(jnp.where(tile == lists_ref[pl.ds(step * 2 + 1, 1), :], 1.0, 0.0).astype(BF16))
-        for x in range(GX):
-            picked = jnp.concatenate(
-                [
-                    hit * jnp.where(x_row == float(x), 1.0, 0.0).astype(BF16)
-                    for hit, x_row in zip(hits, x_rows)
-                ],
-                axis=1,
-            )
-            acc_ref[x] += dot(picked, t_ref[...], NN)
-
-    for h in range(GROUP):
-        take(0, h, h > 0)
-    work(0)
-
-    def group(g, carry):
-        for h in range(GROUP):
-            take(g, h, True)
-        work(g)
+            lanes = slice(h * 128, (h + 1) * 128)
+            x_old_ref[:, lanes] = lists_ref[h, 0:1, :]
+            hit_ref[:, lanes] = jnp.where(tile == lists_ref[h, 1:2, :], 1.0, 0.0).astype(BF16)
         return carry
 
-    lax.fori_loop(1, slab_count // GROUP, group, 0)
+    lax.fori_loop(0, slab_count // GROUP, group, 0)
+    for x in range(GX):
+        mask = jnp.where(x_old_ref[...] == float(x), 1.0, 0.0).astype(BF16)
+        acc_ref[x] += dot(hit_ref[...] * mask, t_old_ref[...], NN)
     for x in range(GX):
         for layer in range(LAYERS):
             for k in range(3):
                 part32_ref[pl.ds(x * NY * LINE + k * LAYERS + layer, NY, stride=LINE), :] = acc_ref[
                     x, layer * NY : (layer + 1) * NY, k * 128 : (k + 1) * 128
                 ]
-    part_ref[...] = part32_ref[...].astype(BF16)
+    for x in range(GX):
+        part_ref[x] = part32_ref[x * NY * LINE : (x + 1) * NY * LINE, :].astype(BF16)
     others = pl.ds(1, slab_count - 1)
     pltpu.make_async_copy(send_ref.at[others], send_ref.at[others], send_sem).wait()
 
 
-def spread(owner, coef, offs, anchor, blocks, count, syn, slab_count, collective_id):
-    block_rows = PLANES * CAP + 2
-    slots = slab_count * CAP
-    held = GROUP * CAP
-    return pl.pallas_call(
-        spread_kernel,
-        out_shape=(
-            jax.ShapeDtypeStruct((ROWS, 128), BF16),
-            jax.ShapeDtypeStruct((3, slots, QP), F32),
-            jax.ShapeDtypeStruct((2 * slab_count, 128), F32),
-            jax.ShapeDtypeStruct((slab_count, 128), jnp.int32),
-        ),
-        in_specs=[VMEM_SPEC] * 7,
-        out_specs=(VMEM_SPEC,) * 4,
-        scratch_shapes=[
-            pltpu.VMEM((PLANES + 2, slots, 128), F32),
-            pltpu.VMEM((block_rows, 128), F32),
-            pltpu.VMEM((128, owner.shape[1]), F32),
-            pltpu.VMEM((slab_count, block_rows, 128), BF16),
-            pltpu.VMEM((slab_count, block_rows, 128), BF16),
-            pltpu.VMEM((PLANES, held, 128), F32),
-            pltpu.VMEM((3, held, QP), F32),
-            pltpu.VMEM((128, QP), F32),
-            pltpu.VMEM((128, QP), F32),
-            pltpu.VMEM((GROUP * 128, QP), BF16),
-            pltpu.VMEM((GX, NY * LAYERS, QP), F32),
-            pltpu.VMEM((ROWS, 128), F32),
-            pltpu.VMEM((256, QP), F32),
-            pltpu.VMEM((3, 256, QP), BF16),
-            pltpu.SemaphoreType.DMA,
-            pltpu.SemaphoreType.DMA((slab_count,)),
-        ],
-        compiler_params=pltpu.CompilerParams(collective_id=collective_id, has_side_effects=True),
-        name="spread",
-    )(owner, coef, offs, anchor, blocks, count, syn)
-
-
-def sample_kernel(
-    owner_ref, vel_ref, p_ref, lists_ref, idx_smem, ana_ref, out_ref,
-    v_ref, g_ref, pv_ref, c_ref, blk_ref, tx_ref, ty_ref, send_ref, back_ref, r_ref,
+def sample_cells(
+    me, hot, all_ref, ana_ref, out_ref, wz_ref, wxy_ref, idx_smem,
+    v_ref, g_ref, pv_ref, c_ref, blk_ref, send_ref, back_ref, r_ref,
     wide_ref, basis_ref, send_sem, recv_sem,
 ):
     slab_count = send_ref.shape[0]
-    me = lax.axis_index("slab")
-    barrier = greet_all(me, slab_count)
-    v_ref[...] = vel_ref[...].astype(F32)
-    basis_planes(ana_ref, wide_ref, basis_ref)
+    for x in range(GX):
+        v_ref[x * NY * LINE : (x + 1) * NY * LINE, :] = all_ref[x].astype(F32)
 
     def work(g):
         def source(h, carry):
@@ -354,17 +293,10 @@
                 for j in range(B):
                     start = idx_smem[step, i * B + j]
                     g_ref[i, pl.ds(j, 3, stride=B), :] = v_ref[pl.ds(start, 3, stride=LAYERS), :]
-            x_row, y_row = lists_ref[pl.ds(step * 2, 1), :], lists_ref[pl.ds(step * 2 + 1, 1), :]
-            stencil_columns(x_row, y_row, tx_ref, ty_ref)
             for i in range(CAP):
                 c = step * CAP + i
-                lines = slice(i * B, (i + 1) * B)
-                wxy = xy_weights(
-                    p_ref[0, pl.ds(c, 1), :], p_ref[1, pl.ds(c, 1), :],
-                    tx_ref[lines], ty_ref[lines],
-                )
-                wz = z_weights(p_ref[2, pl.ds(c, 1), :])
-                projected = dot(g_ref[i].astype(BF16), wz, NN)
+                projected = dot(g_ref[i].astype(BF16), wz_ref[c], NN)
+                wxy = wxy_ref[c]
                 for k in range(3):
                     pv_ref[k, pl.ds(h * CAP + i, 1), :] = jnp.sum(
                         projected[k * B : (k + 1) * B] * wxy, axis=0, keepdims=True
@@ -381,7 +313,7 @@
         for h in range(GROUP):
             for r in range(OUT_PLANES):
                 blk_ref[r * CAP : (r + 1) * CAP, :] = c_ref[r, h * CAP : (h + 1) * CAP, :]
-            send_ref[g * GROUP + h] = blk_ref[...].astype(BF16)
+            send_ref[g * GROUP + h] = blk_ref[: OUT_PLANES * CAP, :].astype(BF16)
 
     def send(step):
         pltpu.make_async_remote_copy(
@@ -395,7 +327,6 @@
 
     groups = slab_count // GROUP
     work(groups - 1)
-    pl.semaphore_wait(barrier, slab_count - 1)
 
     def group(n, carry):
         g = groups - 2 - n
@@ -408,12 +339,11 @@
     for h in range(1, GROUP):
         send(h)
     back_ref[0] = send_ref[0]
-    hot = slot_onehot(owner_ref, slab_count, me)
     others = pl.ds(1, slab_count - 1)
     pltpu.make_async_copy(back_ref.at[others], back_ref.at[others], recv_sem).wait()
 
     def take(step, carry):
-        blk_ref[...] = back_ref[step].astype(F32)
+        blk_ref[: OUT_PLANES * CAP, :] = back_ref[step].astype(F32)
         for r in range(OUT_PLANES):
             r_ref[r, pl.ds(step * CAP, CAP), :] = blk_ref[r * CAP : (r + 1) * CAP, :]
         return carry
@@ -426,37 +356,12 @@
     pltpu.make_async_copy(send_ref.at[others], send_ref.at[others], send_sem).wait()
 
 
-def sample(owner, vel, p, lists, idx, ana, slab_count, collective_id):
-    slots = slab_count * CAP
-    block_rows = OUT_PLANES * CAP
-    held = GROUP * CAP
-    return pl.pallas_call(
-        sample_kernel,
-        out_shape=jax.ShapeDtypeStruct((3, L, owner.shape[1]), BF16),
-        in_specs=[VMEM_SPEC] * 4 + [pl.BlockSpec(memory_space=pltpu.SMEM), VMEM_SPEC],
-        out_specs=VMEM_SPEC,
-        scratch_shapes=[
-            pltpu.VMEM((ROWS, 128), F32),
-            pltpu.VMEM((CAP, 3 * B, 128), F32),
-            pltpu.VMEM((3, held, QP), F32),
-            pltpu.VMEM((OUT_PLANES, held, 128), F32),
-            pltpu.VMEM((block_rows, 128), F32),
-            pltpu.VMEM((128, QP), F32),
-            pltpu.VMEM((128, QP), F32),
-            pltpu.VMEM((slab_count, block_rows, 128), BF16),
-            pltpu.VMEM((slab_count, block_rows, 128), BF16),
-            pltpu.VMEM((OUT_PLANES, slots, 128), F32),
-            pltpu.VMEM((256, QP), F32),
-            pltpu.VMEM((3, 256, QP), BF16),
-            pltpu.SemaphoreType.DMA,
-            pltpu.SemaphoreType.DMA,
-        ],
-        compiler_params=pltpu.CompilerParams(collective_id=collective_id, has_side_effects=True),
-        name="sample",
-    )(owner, vel, p, lists, idx, ana)
-
-
-def grid_kernel(
+def batch_neighbours():
+    batches, b = lax.axis_size("batch"), lax.axis_index("batch")
+    return [lax.rem(b + i, batches) for i in range(1, batches)]
+
+
+def grid_steps(
     part_ref, vel_ref, new_ref, all_ref,
     hop_ref, got_ref, summed_ref, drive_ref, st_ref, own_ref,
     xs_ref, xr_ref, ys_ref, yr_ref, y32_ref, send_sem, recv_sem, local_sem,
@@ -465,15 +370,8 @@
     half = planes // 2
     batches, slabs = lax.axis_size("batch"), lax.axis_size("slab")
     b, s = lax.axis_index("batch"), lax.axis_index("slab")
-    right, far, left = [lax.rem(b + i, batches) for i in (1, 2, 3)]
+    right, far, left = batch_neighbours()
     above, below = lax.rem(s + 1, slabs), lax.rem(s + slabs - 1, slabs)
-
-    barrier = pltpu.get_barrier_semaphore()
-    for device in ({"batch": right}, {"batch": left}, {"slab": above}, {"slab": below}):
-        pl.semaphore_signal(
-            barrier, inc=1, device_id=device, device_id_type=pl.DeviceIdType.MESH
-        )
-    pl.semaphore_wait(barrier, 4)
 
     def rows(part):
         return pl.ds(pl.multiple_of(part * mine, mine), mine)
@@ -578,19 +476,97 @@
         copy.wait_send()
 
 
-def grid_step(part, vel, collective_id):
+def step_kernel(
+    owner_ref, coef_ref, offs_ref, anchor_ref, blocks_ref, count_ref, syn_ref, ana_ref, vel_ref,
+    new_ref, out_ref,
+    x_ref, blk_ref, rows_ref, hot_ref, send_ref, recv_ref, send_sem, recv_sem,
+    part_ref, wz_ref, wxy_ref, idx_ref, idx_smem,
+    r_ref, p_ref, f_ref, lists_ref, tx_ref, ty_ref, t_ref, t_old_ref, hit_ref, x_old_ref,
+    acc_ref, part32_ref, wide_ref, basis_ref,
+    all_ref, hop_ref, got_ref, summed_ref, drive_ref, st_ref, own_ref,
+    xs_ref, xr_ref, ys_ref, yr_ref, y32_ref, grid_send_sem, grid_recv_sem, local_sem,
+    g_ref, pv_ref, c_ref, coef_send_ref, back_ref, back_send_sem, back_recv_sem,
+):
+    slab_count = send_ref.shape[0]
+    me = lax.axis_index("slab")
+    barrier = greet_all(me, slab_count)
+    right, _, left = batch_neighbours()
+    for device in ({"batch": right}, {"batch": left}):
+        pl.semaphore_signal(
+            barrier, inc=1, device_id=device, device_id_type=pl.DeviceIdType.MESH
+        )
+    hot_ref[...] = slot_onehot(owner_ref, slab_count, me)
+    pack_blocks(
+        hot_ref[...], coef_ref, offs_ref, anchor_ref, blocks_ref, count_ref,
+        send_ref, x_ref, blk_ref, rows_ref,
+    )
+    pl.semaphore_wait(barrier, slab_count + 1)
+    spread_cells(
+        me, syn_ref, send_ref, recv_ref, send_sem, recv_sem, part_ref, wz_ref, wxy_ref, idx_ref,
+        blk_ref, r_ref, p_ref, f_ref, lists_ref, tx_ref, ty_ref,
+        t_ref, t_old_ref, hit_ref, x_old_ref, acc_ref, part32_ref, wide_ref, basis_ref,
+    )
+    pltpu.sync_copy(idx_ref, idx_smem)
+    basis_planes(ana_ref, wide_ref, basis_ref)
+    grid_steps(
+        part_ref, vel_ref, new_ref, all_ref,
+        hop_ref, got_ref, summed_ref, drive_ref, st_ref, own_ref,
+        xs_ref, xr_ref, ys_ref, yr_ref, y32_ref, grid_send_sem, grid_recv_sem, local_sem,
+    )
+    sample_cells(
+        me, hot_ref[...], all_ref, ana_ref, out_ref, wz_ref, wxy_ref, idx_smem,
+        part32_ref, g_ref, pv_ref, c_ref, blk_ref, coef_send_ref, back_ref, x_ref,
+        wide_ref, basis_ref, back_send_sem, back_recv_sem,
+    )
+
+
+def whole_step(owner, coef, offs, anchor, blocks, count, syn, ana, vel, slab_count):
     planes, mine, _ = vel.shape
     half = planes // 2
     copies = 6 + 4 * SWEEPS + 6
+    cells = owner.shape[1]
+    slots = slab_count * CAP
+    held = GROUP * CAP
+    block_rows = PLANES * CAP + 2
+    back_rows = OUT_PLANES * CAP
+    dma = pltpu.SemaphoreType.DMA
     return pl.pallas_call(
-        grid_kernel,
+        step_kernel,
         out_shape=(
             jax.ShapeDtypeStruct(vel.shape, F32),
-            jax.ShapeDtypeStruct(part.shape, BF16),
+            jax.ShapeDtypeStruct((3, L, cells), BF16),
         ),
-        in_specs=[VMEM_SPEC] * 2,
-        out_specs=(VMEM_SPEC, ANY_SPEC),
+        in_specs=[VMEM_SPEC] * 9,
+        out_specs=(VMEM_SPEC, VMEM_SPEC),
         scratch_shapes=[
+            pltpu.VMEM((PLANES + 2, slots, 128), F32),
+            pltpu.VMEM((block_rows, 128), F32),
+            pltpu.VMEM((128, cells), F32),
+            pltpu.VMEM((slots, cells), BF16),
+            pltpu.VMEM((slab_count, block_rows, 128), BF16),
+            pltpu.VMEM((slab_count, block_rows, 128), BF16),
+            dma,
+            dma((slab_count,)),
+            pltpu.VMEM((planes, NY * LINE, 128), BF16),
+            pltpu.VMEM((slots, 128, QP), BF16),
+            pltpu.VMEM((slots, B, QP), F32),
+            pltpu.VMEM((slab_count, 128), jnp.int32),
+            pltpu.SMEM((slab_count, 128), jnp.int32),
+            pltpu.VMEM((PLANES, held, 128), F32),
+            pltpu.VMEM((3, held, QP), F32),
+            pltpu.VMEM((3, held, QP), F32),
+            pltpu.VMEM((GROUP, 2, 128), F32),
+            pltpu.VMEM((128, 128), F32),
+            pltpu.VMEM((128, 128), F32),
+            pltpu.VMEM((GROUP * 128, QP), BF16),
+            pltpu.VMEM((GROUP * 128, QP), BF16),
+            pltpu.VMEM((NY * LAYERS, GROUP * 128), BF16),
+            pltpu.VMEM((1, GROUP * 128), F32),
+            pltpu.VMEM((GX, NY * LAYERS, QP), F32),
+            pltpu.VMEM((ROWS, 128), F32),
+            pltpu.VMEM((256, QP), F32),
+            pltpu.VMEM((3, 256, QP), BF16),
+            pltpu.VMEM((planes, NY * LINE, 128), BF16),
             pltpu.VMEM((2, half, mine, 128), BF16),
             pltpu.VMEM((4, half, mine, 128), BF16),
             pltpu.VMEM((2, half, mine, 128), BF16),
@@ -602,13 +578,22 @@
             pltpu.VMEM((SWEEPS, 2, planes * LINE, 128), BF16),
             pltpu.VMEM((SWEEPS, 2, planes * LINE, 128), BF16),
             pltpu.VMEM((2, planes * LINE, 128), F32),
-            pltpu.SemaphoreType.DMA((copies,)),
-            pltpu.SemaphoreType.DMA((copies,)),
-            pltpu.SemaphoreType.DMA,
+            dma((copies,)),
+            dma((copies,)),
+            dma,
+            pltpu.VMEM((CAP, 3 * B, 128), F32),
+            pltpu.VMEM((3, held, QP), F32),
+            pltpu.VMEM((OUT_PLANES, held, 128), F32),
+            pltpu.VMEM((slab_count, back_rows, 128), BF16),
+            pltpu.VMEM((slab_count, back_rows, 128), BF16),
+            dma,
+            dma,
         ],
-        compiler_params=pltpu.CompilerParams(collective_id=collective_id, has_side_effects=True),
-        name="grid_step",
-    )(part, vel)
+        compiler_params=pltpu.CompilerParams(
+            collective_id=0, has_side_effects=True, vmem_limit_bytes=67_043_328
+        ),
+        name="whole_step",
+    )(owner, coef, offs, anchor, blocks, count, syn, ana, vel)
 
 
 def local(
@@ -616,7 +601,8 @@
 ):
     slab_count = lax.axis_size("slab")
     owner = owner_slab.T
-    part, p, lists, idx = spread(
+    planes, lines = velocity_old.shape[:2]
+    velocity_new, velocity_coef = whole_step(
         owner,
         traction.transpose(1, 2, 0),
         offsets.transpose(1, 0, 2),
@@ -624,14 +610,9 @@
         blocks.T,
         block_count[None],
         synthesis,
+        analysis,
+        velocity_old.transpose(0, 1, 3, 2, 4).reshape(planes, lines * LINE, 128),
         slab_count,
-        0,
-    )
-    planes, lines = velocity_old.shape[:2]
-    velocity = velocity_old.transpose(0, 1, 3, 2, 4).reshape(planes, lines * LINE, 128)
-    velocity_new, slab_velocity = grid_step(part.reshape(planes, NY * LINE, 128), velocity, 2)
-    velocity_coef = sample(
-        owner, slab_velocity.reshape(ROWS, 128), p, lists, idx, analysis, slab_count, 1
     )
     velocity_new = velocity_new.reshape(planes, lines, 3, LAYERS, 128)
     return (velocity_new.transpose(0, 1, 3, 2, 4), velocity_coef.transpose(2, 0, 1))

time: 151 us -> 126 us (0.83)
  Pallas kernels: 147 us -> 122 us
    pallas_call x3 -> x1, Pallas kernels: 147 us -> 122 us  [whole_step(): pl.pallas_call(step_kernel, out_shape=(jax.ShapeDtypeStruct(vel.shape, F3...]
where the time goes in v4:
time: 126 us
  Pallas kernels  122 us (97%)
  local copies, waits for them, and re-layouts  2.58 us (2%)
    pallas_call x1, Pallas kernels, whole_step(): pl.pallas_call(step_kernel, out_shape=(jax.ShapeDtypeStruct(vel.shape, F3...  122 us
    unnamed x4, local copies, waits for them, and re-layouts  2.58 us

profile of v4, /device:TPU:1, one launch (start us, length us, event | category | flops | bytes accessed | tf_op | source)
XLA Modules:
  0.0 125.7 jit_solution(12950773353569056279)
XLA Ops:
  0.6 122.5 %whole_step.1 = (f32[8,96,128]{2,1,0:T(8,128)}, bf16[3,169,192]{2,1,0:T(8,128)(2,1)}) custom-call(s32[1,192]{1,0:T(1,128)} %bitcast.20, bf16[3,169,192]{2,1,0:T(8,128)(2,1)} %bitcast.17, bf16[3,192,338]{2,1,0:T(8,128)(2,1)} %bitcast.13, s32[3,192]{1,0:T(4,128)} %bitcast.19, s32[16,192]{1,0:T(8,128)} %bitcast.18, s32[1,192]{1,0:T(1,128)} %bitcast.21, ...), custom_call_target="tpu_custom_call" | custom-call | tf_op jit(solution)/shard_map/whole_step/pallas_call | solution.py:533
  123.1 0.0 copy-start
  123.2 1.9 %copy.13 = f32[8,16,2,3,128]{4,2,3,1,0:T(2,128)} copy(f32[8,16,2,3,128]{4,2,3,1,0:T(2,128)} %bitcast.14) | data formatting | bytes 786432
  125.0 0.0 copy-done
  125.0 0.7 copy.14
Async XLA Ops:
  123.1 1.9 %copy-start = (bf16[3,169,192]{2,1,0:T(8,128)(2,1)S(1)}, bf16[3,169,192]{2,1,0:T(8,128)(2,1)}, u32[]{:S(2)}) copy-start(bf16[3,169,192]{2,1,0:T(8,128)(2,1)} %get-tuple-element.5) | copy-start | bytes 584068

commit v5 on v4

--- a/solution.py
+++ b/solution.py
@@ -57,11 +57,22 @@
     return y * 16 + z * 2 + core
 
 
-def peer_of(me, step):
-    y = (me // 16 + step // 16) % 4
-    z = (me // 2 % 8 + step // 2 % 8) % 8
-    core = (me % 2 + step % 2) % 2
-    return y * 16 + z * 2 + core
+def wrap(value, size):
+    value = jnp.where(value >= size, value - size, value)
+    return jnp.where(value < 0, value + size, value)
+
+
+def each_peer(me, sign, count, visit):
+    my_y, my_z, my_core = me // 16, me // 2 % 8, me % 2
+    for dy in range(count // 16):
+        for core in range(2):
+            base = wrap(my_y + sign * dy, count // 16) * 16 + wrap(my_core + sign * core, 2)
+
+            def along(dz, carry, dy=dy, core=core, base=base):
+                visit(dy * 16 + dz * 2 + core, base + 2 * wrap(my_z + sign * dz, 8))
+                return carry
+
+            lax.fori_loop(1 if dy == core == 0 else 0, 8, along, 0)
 
 
 def slot_onehot(owner_ref, slab_count, me):
@@ -83,7 +94,7 @@
 
     def greet(step, carry):
         pl.semaphore_signal(
-            barrier, inc=1, device_id={"slab": peer_of(me, step)},
+            barrier, inc=1, device_id={"slab": wrap(me + step, count)},
             device_id_type=pl.DeviceIdType.MESH,
         )
         return carry
@@ -149,13 +160,19 @@
 
 
 def z_weights(pz):
+    stride = 8.0 * SCALE
     step = lax.broadcasted_iota(jnp.int32, (8, QP), 0).astype(F32) * SCALE
-    base = pz - step
-    parts = []
-    for g in range(16):
-        d = base - (8.0 * g * SCALE)
-        parts.append(jnp.exp2(LOG_NORM - d * d))
-    return jnp.concatenate(parts, axis=0).astype(BF16)
+    d = pz - step - 8.0 * stride
+    middle = LOG_NORM - d * d
+    twice = d * (2.0 * stride)
+    powers = {8: middle}
+    for sign, last in ((1, 15), (-1, 0)):
+        value, change = middle, sign * twice - stride * stride
+        for g in range(8 + sign, last + sign, sign):
+            value = value + change
+            change = change - 2.0 * stride * stride
+            powers[g] = value
+    return jnp.concatenate([jnp.exp2(powers[g]) for g in range(16)], axis=0).astype(BF16)
 
 
 def columns(row):
@@ -182,23 +199,22 @@
 
 def spread_cells(
     me, syn_ref, send_ref, recv_ref, send_sem, recv_sem, part_ref, wz_ref, wxy_ref, idx_ref,
-    blk_ref, r_ref, p_ref, f_ref, lists_ref, tx_ref, ty_ref,
+    blk_ref, r_ref, p_ref, f_ref, lists_ref, next_ref, tx_ref, ty_ref,
     t_ref, t_old_ref, hit_ref, x_old_ref, acc_ref, part32_ref, wide_ref, basis_ref,
 ):
     slab_count = send_ref.shape[0]
 
-    def send(step, carry):
+    def send(step, peer):
         pltpu.make_async_remote_copy(
             src_ref=send_ref.at[step],
             dst_ref=recv_ref.at[step],
             send_sem=send_sem,
             recv_sem=recv_sem.at[step],
-            device_id={"slab": peer_of(me, step)},
+            device_id={"slab": peer},
             device_id_type=pl.DeviceIdType.MESH,
         ).start()
-        return carry
-
-    lax.fori_loop(1, slab_count, send, 0)
+
+    each_peer(me, 1, slab_count, send)
     pltpu.make_async_copy(send_ref.at[0], recv_ref.at[0], recv_sem.at[0]).start()
     basis_planes(syn_ref, wide_ref, basis_ref)
     for ref in (acc_ref, t_ref, t_old_ref, hit_ref, x_old_ref):
@@ -206,14 +222,15 @@
 
     per_source = GX // GROUP
 
-    def group(g, carry):
-        for h in range(GROUP):
-            step = g * GROUP + h
-            pltpu.make_async_copy(recv_ref.at[step], recv_ref.at[step], recv_sem.at[step]).wait()
-            blk_ref[...] = recv_ref[step].astype(F32)
-            for r in range(PLANES):
-                r_ref[r, h * CAP : (h + 1) * CAP, :] = blk_ref[r * CAP : (r + 1) * CAP, :]
-            lists_ref[h] = blk_ref[PLANES * CAP : PLANES * CAP + 2, :]
+    def take(step, h):
+        pltpu.make_async_copy(recv_ref.at[step], recv_ref.at[step], recv_sem.at[step]).wait()
+        blk_ref[...] = recv_ref[step].astype(F32)
+        for r in range(PLANES):
+            r_ref[r, pl.ds(h * CAP, CAP), :] = blk_ref[r * CAP : (r + 1) * CAP, :]
+        next_ref[h] = blk_ref[PLANES * CAP : PLANES * CAP + 2, :]
+
+    def group(g, take_next):
+        lists_ref[...] = next_ref[...]
         for k in range(3):
             anchor = r_ref[6 + 3 * k][:, 112:113]
             for t in range(3):
@@ -223,6 +240,8 @@
 
         def source(h, carry):
             step = g * GROUP + h
+            if take_next:
+                take(step + GROUP, h)
             x_row, y_row = lists_ref[h, 0:1, :], lists_ref[h, 1:2, :]
             y, layer = split_y(y_row)
             place = jnp.where(x_row < DEAD, (x_row * NY + y) * LINE + layer, 0.0)
@@ -259,9 +278,16 @@
             lanes = slice(h * 128, (h + 1) * 128)
             x_old_ref[:, lanes] = lists_ref[h, 0:1, :]
             hit_ref[:, lanes] = jnp.where(tile == lists_ref[h, 1:2, :], 1.0, 0.0).astype(BF16)
+
+    for h in range(GROUP):
+        take(h, h)
+
+    def all_but_last(g, carry):
+        group(g, True)
         return carry
 
-    lax.fori_loop(0, slab_count // GROUP, group, 0)
+    lax.fori_loop(0, slab_count // GROUP - 1, all_but_last, 0)
+    group(slab_count // GROUP - 1, False)
     for x in range(GX):
         mask = jnp.where(x_old_ref[...] == float(x), 1.0, 0.0).astype(BF16)
         acc_ref[x] += dot(hit_ref[...] * mask, t_old_ref[...], NN)
@@ -279,31 +305,40 @@
 
 def sample_cells(
     me, hot, all_ref, ana_ref, out_ref, wz_ref, wxy_ref, idx_smem,
-    v_ref, g_ref, pv_ref, c_ref, blk_ref, send_ref, back_ref, r_ref,
+    v_ref, even_ref, odd_ref, pv_ref, c_ref, blk_ref, send_ref, back_ref, r_ref,
     wide_ref, basis_ref, send_sem, recv_sem,
 ):
     slab_count = send_ref.shape[0]
     for x in range(GX):
         v_ref[x * NY * LINE : (x + 1) * NY * LINE, :] = all_ref[x].astype(F32)
 
+    def gather(step, to_ref):
+        for i in range(CAP):
+            for j in range(B):
+                start = idx_smem[step, i * B + j]
+                to_ref[i, pl.ds(j, 3, stride=B), :] = v_ref[pl.ds(start, 3, stride=LAYERS), :]
+
+    def project(step, h, from_ref):
+        for i in range(CAP):
+            c = step * CAP + i
+            projected = dot(from_ref[i].astype(BF16), wz_ref[c], NN)
+            wxy = wxy_ref[c]
+            for k in range(3):
+                pv_ref[k, pl.ds(h * CAP + i, 1), :] = jnp.sum(
+                    projected[k * B : (k + 1) * B] * wxy, axis=0, keepdims=True
+                )
+
     def work(g):
-        def source(h, carry):
-            step = g * GROUP + h
-            for i in range(CAP):
-                for j in range(B):
-                    start = idx_smem[step, i * B + j]
-                    g_ref[i, pl.ds(j, 3, stride=B), :] = v_ref[pl.ds(start, 3, stride=LAYERS), :]
-            for i in range(CAP):
-                c = step * CAP + i
-                projected = dot(g_ref[i].astype(BF16), wz_ref[c], NN)
-                wxy = wxy_ref[c]
-                for k in range(3):
-                    pv_ref[k, pl.ds(h * CAP + i, 1), :] = jnp.sum(
-                        projected[k * B : (k + 1) * B] * wxy, axis=0, keepdims=True
-                    )
+        def pair(n, carry):
+            step = g * GROUP + 2 * n
+            later = jnp.where(n < GROUP // 2 - 1, step + 2, (g - 1) * GROUP)
+            gather(step + 1, odd_ref)
+            project(step, 2 * n, even_ref)
+            gather(jnp.where(later < 0, 0, later), even_ref)
+            project(step + 1, 2 * n + 1, odd_ref)
             return carry
 
-        lax.fori_loop(0, GROUP, source, 0)
+        lax.fori_loop(0, GROUP // 2, pair, 0)
         rem = jnp.zeros((GROUP * CAP, 128), F32)
         for k in range(3):
             got = dot(pv_ref[k].astype(BF16), basis_ref[k], NT)
@@ -315,29 +350,35 @@
                 blk_ref[r * CAP : (r + 1) * CAP, :] = c_ref[r, h * CAP : (h + 1) * CAP, :]
             send_ref[g * GROUP + h] = blk_ref[: OUT_PLANES * CAP, :].astype(BF16)
 
-    def send(step):
-        pltpu.make_async_remote_copy(
-            src_ref=send_ref.at[step],
-            dst_ref=back_ref.at[step],
-            send_sem=send_sem,
-            recv_sem=recv_sem,
-            device_id={"slab": peer_of(me, relative(0, step))},
-            device_id_type=pl.DeviceIdType.MESH,
-        ).start()
+    my_y, my_z, my_core = me // 16, me // 2 % 8, me % 2
+
+    def send(g, first=0):
+        dy = g // (16 // GROUP)
+        base = wrap(my_y - dy, slab_count // 16) * 16
+        for h in range(first, GROUP):
+            dz = (g - dy * (16 // GROUP)) * (GROUP // 2) + h // 2
+            place = base + 2 * wrap(my_z - dz, 8) + wrap(my_core - h % 2, 2)
+            pltpu.make_async_remote_copy(
+                src_ref=send_ref.at[g * GROUP + h],
+                dst_ref=back_ref.at[g * GROUP + h],
+                send_sem=send_sem,
+                recv_sem=recv_sem,
+                device_id={"slab": place},
+                device_id_type=pl.DeviceIdType.MESH,
+            ).start()
 
     groups = slab_count // GROUP
+    gather((groups - 1) * GROUP, even_ref)
     work(groups - 1)
 
     def group(n, carry):
         g = groups - 2 - n
-        for h in range(GROUP):
-            send((g + 1) * GROUP + h)
+        send(g + 1)
         work(g)
         return carry
 
     lax.fori_loop(0, groups - 1, group, 0)
-    for h in range(1, GROUP):
-        send(h)
+    send(0, 1)
     back_ref[0] = send_ref[0]
     others = pl.ds(1, slab_count - 1)
     pltpu.make_async_copy(back_ref.at[others], back_ref.at[others], recv_sem).wait()
@@ -481,11 +522,11 @@
     new_ref, out_ref,
     x_ref, blk_ref, rows_ref, hot_ref, send_ref, recv_ref, send_sem, recv_sem,
     part_ref, wz_ref, wxy_ref, idx_ref, idx_smem,
-    r_ref, p_ref, f_ref, lists_ref, tx_ref, ty_ref, t_ref, t_old_ref, hit_ref, x_old_ref,
+    r_ref, p_ref, f_ref, lists_ref, next_ref, tx_ref, ty_ref, t_ref, t_old_ref, hit_ref, x_old_ref,
     acc_ref, part32_ref, wide_ref, basis_ref,
     all_ref, hop_ref, got_ref, summed_ref, drive_ref, st_ref, own_ref,
     xs_ref, xr_ref, ys_ref, yr_ref, y32_ref, grid_send_sem, grid_recv_sem, local_sem,
-    g_ref, pv_ref, c_ref, coef_send_ref, back_ref, back_send_sem, back_recv_sem,
+    even_ref, odd_ref, pv_ref, c_ref, coef_send_ref, back_ref, back_send_sem, back_recv_sem,
 ):
     slab_count = send_ref.shape[0]
     me = lax.axis_index("slab")
@@ -503,7 +544,7 @@
     pl.semaphore_wait(barrier, slab_count + 1)
     spread_cells(
         me, syn_ref, send_ref, recv_ref, send_sem, recv_sem, part_ref, wz_ref, wxy_ref, idx_ref,
-        blk_ref, r_ref, p_ref, f_ref, lists_ref, tx_ref, ty_ref,
+        blk_ref, r_ref, p_ref, f_ref, lists_ref, next_ref, tx_ref, ty_ref,
         t_ref, t_old_ref, hit_ref, x_old_ref, acc_ref, part32_ref, wide_ref, basis_ref,
     )
     pltpu.sync_copy(idx_ref, idx_smem)
@@ -515,7 +556,7 @@
     )
     sample_cells(
         me, hot_ref[...], all_ref, ana_ref, out_ref, wz_ref, wxy_ref, idx_smem,
-        part32_ref, g_ref, pv_ref, c_ref, blk_ref, coef_send_ref, back_ref, x_ref,
+        part32_ref, even_ref, odd_ref, pv_ref, c_ref, blk_ref, coef_send_ref, back_ref, x_ref,
         wide_ref, basis_ref, back_send_sem, back_recv_sem,
     )
 
@@ -556,6 +597,7 @@
             pltpu.VMEM((3, held, QP), F32),
             pltpu.VMEM((3, held, QP), F32),
             pltpu.VMEM((GROUP, 2, 128), F32),
+            pltpu.VMEM((GROUP, 2, 128), F32),
             pltpu.VMEM((128, 128), F32),
             pltpu.VMEM((128, 128), F32),
             pltpu.VMEM((GROUP * 128, QP), BF16),
@@ -582,6 +624,7 @@
             dma((copies,)),
             dma,
             pltpu.VMEM((CAP, 3 * B, 128), F32),
+            pltpu.VMEM((CAP, 3 * B, 128), F32),
             pltpu.VMEM((3, held, QP), F32),
             pltpu.VMEM((OUT_PLANES, held, 128), F32),
             pltpu.VMEM((slab_count, back_rows, 128), BF16),

time: 126 us -> 117 us (0.929)
  Pallas kernels: 122 us -> 114 us
    pallas_call x1, Pallas kernels: 122 us -> 114 us  [whole_step(): pl.pallas_call(step_kernel, out_shape=(jax.ShapeDtypeStruct(vel.shape, F3...]
where the time goes in v5:
time: 117 us
  Pallas kernels  114 us (97%)
  local copies, waits for them, and re-layouts  2.58 us (2%)
    pallas_call x1, Pallas kernels, whole_step(): pl.pallas_call(step_kernel, out_shape=(jax.ShapeDtypeStruct(vel.shape, F3...  114 us
    unnamed x4, local copies, waits for them, and re-layouts  2.58 us

profile of v5, /device:TPU:1, one launch (start us, length us, event | category | flops | bytes accessed | tf_op | source)
XLA Modules:
  0.0 117.2 jit_solution(12851279038951263457)
XLA Ops:
  0.6 114.0 %whole_step.1 = (f32[8,96,128]{2,1,0:T(8,128)}, bf16[3,169,192]{2,1,0:T(8,128)(2,1)}) custom-call(s32[1,192]{1,0:T(1,128)} %bitcast.20, bf16[3,169,192]{2,1,0:T(8,128)(2,1)} %bitcast.17, bf16[3,192,338]{2,1,0:T(8,128)(2,1)} %bitcast.13, s32[3,192]{1,0:T(4,128)} %bitcast.19, s32[16,192]{1,0:T(8,128)} %bitcast.18, s32[1,192]{1,0:T(1,128)} %bitcast.21, ...), custom_call_target="tpu_custom_call" | custom-call | tf_op jit(solution)/shard_map/whole_step/pallas_call | solution.py:574
  114.6 0.0 copy-start
  114.6 1.9 %copy.13 = f32[8,16,2,3,128]{4,2,3,1,0:T(2,128)} copy(f32[8,16,2,3,128]{4,2,3,1,0:T(2,128)} %bitcast.14) | data formatting | bytes 786432
  116.5 0.0 copy-done
  116.5 0.7 copy.14
Async XLA Ops:
  114.6 1.9 %copy-start = (bf16[3,169,192]{2,1,0:T(8,128)(2,1)S(1)}, bf16[3,169,192]{2,1,0:T(8,128)(2,1)}, u32[]{:S(2)}) copy-start(bf16[3,169,192]{2,1,0:T(8,128)(2,1)} %get-tuple-element.5) | copy-start | bytes 584068

commit v6 on v5

--- a/solution.py
+++ b/solution.py
@@ -172,7 +172,11 @@
             value = value + change
             change = change - 2.0 * stride * stride
             powers[g] = value
-    return jnp.concatenate([jnp.exp2(powers[g]) for g in range(16)], axis=0).astype(BF16)
+    rows = [jnp.exp2(powers[g]) for g in range(16)]
+    return [
+        jnp.concatenate([row[:, n * 128 : (n + 1) * 128] for row in rows], axis=0).astype(BF16)
+        for n in range(QP // 128)
+    ]
 
 
 def columns(row):
@@ -248,10 +252,22 @@
             idx_ref[pl.ds(step, 1), :] = jnp.clip(place.astype(jnp.int32), 0, ROWS - LINE + LAYERS - 1)
             tx_ref[...] = columns(x_row) * SCALE
             ty_ref[...] = columns(y) * SCALE
+            picked = []
             for d in range(per_source):
-                x = h * per_source + d
-                mask = jnp.where(x_old_ref[...] == x.astype(F32), 1.0, 0.0).astype(BF16)
-                acc_ref[x] += dot(hit_ref[...] * mask, t_old_ref[...], NN)
+                x = (h * per_source + d).astype(F32)
+                mask = jnp.where(x_old_ref[...] == x, 1.0, 0.0).astype(BF16)
+                picked.append(
+                    jnp.concatenate(
+                        [hit_ref[n] * mask[:, n * 128 : (n + 1) * 128] for n in range(GROUP)], axis=1
+                    )
+                )
+            joined = dot(
+                jnp.concatenate(picked, axis=0),
+                jnp.concatenate([t_old_ref[k] for k in range(3)], axis=1),
+                NN,
+            )
+            for d in range(per_source):
+                acc_ref[h * per_source + d] += joined[d * NY * LAYERS : (d + 1) * NY * LAYERS]
             for i in range(CAP):
                 c = step * CAP + i
                 here = pl.ds(h * CAP + i, 1)
@@ -264,11 +280,12 @@
                     [wxy * f_ref[k, here, :] for k in range(3)], axis=0
                 ).astype(BF16)
                 wz = z_weights(p_ref[2, here, :])
-                wz_ref[c] = wz
-                terms = dot(weighted, wz, NT).astype(BF16)
+                for n, part in enumerate(wz):
+                    wz_ref[c, n] = part
+                terms = dot(weighted, jnp.concatenate(wz, axis=1), NT).astype(BF16)
                 at = pl.ds(pl.multiple_of(h * 128 + i * B, B), B)
                 for k in range(3):
-                    t_ref[at, k * 128 : (k + 1) * 128] = terms[k * B : (k + 1) * B]
+                    t_ref[k, at, :] = terms[k * B : (k + 1) * B]
             return carry
 
         lax.fori_loop(0, GROUP, source, 0)
@@ -277,7 +294,7 @@
         for h in range(GROUP):
             lanes = slice(h * 128, (h + 1) * 128)
             x_old_ref[:, lanes] = lists_ref[h, 0:1, :]
-            hit_ref[:, lanes] = jnp.where(tile == lists_ref[h, 1:2, :], 1.0, 0.0).astype(BF16)
+            hit_ref[h] = jnp.where(tile == lists_ref[h, 1:2, :], 1.0, 0.0).astype(BF16)
 
     for h in range(GROUP):
         take(h, h)
@@ -288,9 +305,11 @@
 
     lax.fori_loop(0, slab_count // GROUP - 1, all_but_last, 0)
     group(slab_count // GROUP - 1, False)
+    terms = jnp.concatenate([t_old_ref[k] for k in range(3)], axis=1)
     for x in range(GX):
         mask = jnp.where(x_old_ref[...] == float(x), 1.0, 0.0).astype(BF16)
-        acc_ref[x] += dot(hit_ref[...] * mask, t_old_ref[...], NN)
+        picked = [hit_ref[n] * mask[:, n * 128 : (n + 1) * 128] for n in range(GROUP)]
+        acc_ref[x] += dot(jnp.concatenate(picked, axis=1), terms, NN)
     for x in range(GX):
         for layer in range(LAYERS):
             for k in range(3):
@@ -321,7 +340,8 @@
     def project(step, h, from_ref):
         for i in range(CAP):
             c = step * CAP + i
-            projected = dot(from_ref[i].astype(BF16), wz_ref[c], NN)
+            wz = jnp.concatenate([wz_ref[c, n] for n in range(QP // 128)], axis=1)
+            projected = dot(from_ref[i].astype(BF16), wz, NN)
             wxy = wxy_ref[c]
             for k in range(3):
                 pv_ref[k, pl.ds(h * CAP + i, 1), :] = jnp.sum(
@@ -389,11 +409,12 @@
             r_ref[r, pl.ds(step * CAP, CAP), :] = blk_ref[r * CAP : (r + 1) * CAP, :]
         return carry
 
-    lax.fori_loop(0, slab_count, take, 0)
+    lax.fori_loop(0, slab_count, take, 0, unroll=2)
     rem = dot(r_ref[3].astype(BF16), hot, TN)
     for k in range(3):
         main = dot(r_ref[k].astype(BF16), hot, TN)
-        out_ref[k] = jnp.concatenate([main, rem[k * REM : (k + 1) * REM]], axis=0).astype(BF16)
+        out_ref[k, :128] = main
+        out_ref[k, 128:] = rem[k * REM : (k + 1) * REM]
     pltpu.make_async_copy(send_ref.at[others], send_ref.at[others], send_sem).wait()
 
 
@@ -575,7 +596,7 @@
         step_kernel,
         out_shape=(
             jax.ShapeDtypeStruct(vel.shape, F32),
-            jax.ShapeDtypeStruct((3, L, cells), BF16),
+            jax.ShapeDtypeStruct((3, L, cells), F32),
         ),
         in_specs=[VMEM_SPEC] * 9,
         out_specs=(VMEM_SPEC, VMEM_SPEC),
@@ -589,7 +610,7 @@
             dma,
             dma((slab_count,)),
             pltpu.VMEM((planes, NY * LINE, 128), BF16),
-            pltpu.VMEM((slots, 128, QP), BF16),
+            pltpu.VMEM((slots, QP // 128, 128, 128), BF16),
             pltpu.VMEM((slots, B, QP), F32),
             pltpu.VMEM((slab_count, 128), jnp.int32),
             pltpu.SMEM((slab_count, 128), jnp.int32),
@@ -600,9 +621,9 @@
             pltpu.VMEM((GROUP, 2, 128), F32),
             pltpu.VMEM((128, 128), F32),
             pltpu.VMEM((128, 128), F32),
-            pltpu.VMEM((GROUP * 128, QP), BF16),
-            pltpu.VMEM((GROUP * 128, QP), BF16),
-            pltpu.VMEM((NY * LAYERS, GROUP * 128), BF16),
+            pltpu.VMEM((3, GROUP * 128, 128), BF16),
+            pltpu.VMEM((3, GROUP * 128, 128), BF16),
+            pltpu.VMEM((GROUP, NY * LAYERS, 128), BF16),
             pltpu.VMEM((1, GROUP * 128), F32),
             pltpu.VMEM((GX, NY * LAYERS, QP), F32),
             pltpu.VMEM((ROWS, 128), F32),
@@ -658,7 +679,7 @@
         slab_count,
     )
     velocity_new = velocity_new.reshape(planes, lines, 3, LAYERS, 128)
-    return (velocity_new.transpose(0, 1, 3, 2, 4), velocity_coef.transpose(2, 0, 1))
+    return (velocity_new.transpose(0, 1, 3, 2, 4), velocity_coef.astype(BF16).transpose(2, 0, 1))
 
 
 def solution(mesh):

time: 117 us -> 115 us (0.983)
  Pallas kernels: 114 us -> 112 us
  other arithmetic: 0 us -> 1.83 us
  local copies, waits for them, and re-layouts: 2.58 us -> 0.75 us
    pallas_call x1, Pallas kernels: 114 us -> 112 us  [whole_step(): pl.pallas_call(step_kernel, out_shape=(jax.ShapeDtypeStruct(vel.shape, F3...]
    unnamed x4 -> x3, local copies, waits for them, and re-layouts: 2.58 us -> 0.75 us
    transpose x0 -> x1, other arithmetic: none -> 1.83 us  [local(): velocity_coef.astype(BF16).transpose(2, 0, 1)]
where the time goes in v6:
time: 115 us
  Pallas kernels  112 us (97%)
  other arithmetic  1.83 us (2%)
    pallas_call x1, Pallas kernels, whole_step(): pl.pallas_call(step_kernel, out_shape=(jax.ShapeDtypeStruct(vel.shape, F3...  112 us

profile of v6, /device:TPU:1, one launch (start us, length us, event | category | flops | bytes accessed | tf_op | source)
XLA Modules:
  0.0 114.9 jit_solution(14772419159974720838)
XLA Ops:
  0.6 111.7 %whole_step.1 = (f32[8,96,128]{2,1,0:T(8,128)}, f32[3,169,192]{2,1,0:T(8,128)}) custom-call(s32[1,192]{1,0:T(1,128)} %bitcast.20, bf16[3,169,192]{2,1,0:T(8,128)(2,1)} %bitcast.17, bf16[3,192,338]{2,1,0:T(8,128)(2,1)} %bitcast.14, s32[3,192]{1,0:T(4,128)} %bitcast.19, s32[16,192]{1,0:T(8,128)} %bitcast.18, s32[1,192]{1,0:T(1,128)} %bitcast.21, ...), custom_call_target="tpu_custom_call" | custom-call | tf_op jit(solution)/shard_map/whole_step/pallas_call | solution.py:595
  112.3 0.0 copy-start
  112.4 1.8 %convert_bitcast_fusion = bf16[192,3,169]{0,2,1:T(8,128)(2,1)} fusion(f32[3,169,192]{2,1,0:T(8,128)} %get-tuple-element.5), kind=kLoop, calls=%fused_computation | loop fusion | flops 97344 | bytes 584064 | tf_op jit(solution)/shard_map/transpose | solution.py:682
  114.2 0.0 copy-done
  114.2 0.7 copy.12
Async XLA Ops:
  112.3 1.8 %copy-start = (f32[8,96,128]{2,1,0:T(8,128)S(1)}, f32[8,96,128]{2,1,0:T(8,128)}, u32[]{:S(2)}) copy-start(f32[8,96,128]{2,1,0:T(8,128)} %get-tuple-element.4) | copy-start | bytes 1179652

commit v7 on v6

--- a/solution.py
+++ b/solution.py
@@ -54,7 +54,7 @@
     y = (owner // 16 - me // 16 + 4) % 4
     z = (owner // 2 % 8 - me // 2 % 8 + 8) % 8
     core = (owner % 2 - me % 2 + 2) % 2
-    return y * 16 + z * 2 + core
+    return y * 16 + core * 8 + z
 
 
 def wrap(value, size):
@@ -69,7 +69,7 @@
             base = wrap(my_y + sign * dy, count // 16) * 16 + wrap(my_core + sign * core, 2)
 
             def along(dz, carry, dy=dy, core=core, base=base):
-                visit(dy * 16 + dz * 2 + core, base + 2 * wrap(my_z + sign * dz, 8))
+                visit(dy * 16 + core * 8 + dz, base + 2 * wrap(my_z + sign * dz, 8))
                 return carry
 
             lax.fori_loop(1 if dy == core == 0 else 0, 8, along, 0)
@@ -138,12 +138,12 @@
 
     def step(target, carry):
         for r in range(PLANES):
-            blk_ref[pl.ds(r * CAP, CAP), :] = x_ref[r, pl.ds(target * CAP, CAP), :]
+            blk_ref[0, pl.ds(r * CAP, CAP), :] = x_ref[r, pl.ds(target * CAP, CAP), :]
         for n in range(2):
-            blk_ref[pl.ds(PLANES * CAP + n, 1), :] = jnp.sum(
+            blk_ref[0, pl.ds(PLANES * CAP + n, 1), :] = jnp.sum(
                 x_ref[PLANES + n, pl.ds(target * CAP, CAP), :], axis=0, keepdims=True
             )
-        send_ref[target] = blk_ref[...].astype(BF16)
+        send_ref[target] = blk_ref[0].astype(BF16)
         return carry
 
     lax.fori_loop(0, slab_count, step, 0)
@@ -224,14 +224,13 @@
     for ref in (acc_ref, t_ref, t_old_ref, hit_ref, x_old_ref):
         ref[...] = jnp.zeros_like(ref)
 
-    per_source = GX // GROUP
-
-    def take(step, h):
+
+    def take(step, h, side):
         pltpu.make_async_copy(recv_ref.at[step], recv_ref.at[step], recv_sem.at[step]).wait()
-        blk_ref[...] = recv_ref[step].astype(F32)
+        blk_ref[side] = recv_ref[step].astype(F32)
         for r in range(PLANES):
-            r_ref[r, pl.ds(h * CAP, CAP), :] = blk_ref[r * CAP : (r + 1) * CAP, :]
-        next_ref[h] = blk_ref[PLANES * CAP : PLANES * CAP + 2, :]
+            r_ref[r, pl.ds(h * CAP, CAP), :] = blk_ref[side, r * CAP : (r + 1) * CAP, :]
+        next_ref[h] = blk_ref[side, PLANES * CAP : PLANES * CAP + 2, :]
 
     def group(g, take_next):
         lists_ref[...] = next_ref[...]
@@ -242,23 +241,28 @@
             coef = jnp.concatenate([r_ref[k], r_ref[3]], axis=1).astype(BF16)
             f_ref[k] = dot(coef, basis_ref[k], NN)
 
-        def source(h, carry):
-            step = g * GROUP + h
-            if take_next:
-                take(step + GROUP, h)
-            x_row, y_row = lists_ref[h, 0:1, :], lists_ref[h, 1:2, :]
-            y, layer = split_y(y_row)
-            place = jnp.where(x_row < DEAD, (x_row * NY + y) * LINE + layer, 0.0)
-            idx_ref[pl.ds(step, 1), :] = jnp.clip(place.astype(jnp.int32), 0, ROWS - LINE + LAYERS - 1)
-            tx_ref[...] = columns(x_row) * SCALE
-            ty_ref[...] = columns(y) * SCALE
+        def pair(n, carry):
+            sources = [2 * n, 2 * n + 1]
+            for side, h in enumerate(sources):
+                step = g * GROUP + h
+                if take_next:
+                    take(step + GROUP, h, side)
+                x_row, y_row = lists_ref[h, 0:1, :], lists_ref[h, 1:2, :]
+                y, layer = split_y(y_row)
+                place = jnp.where(x_row < DEAD, (x_row * NY + y) * LINE + layer, 0.0)
+                idx_ref[pl.ds(step, 1), :] = jnp.clip(
+                    place.astype(jnp.int32), 0, ROWS - LINE + LAYERS - 1
+                )
+                tx_ref[side] = columns(x_row) * SCALE
+                ty_ref[side] = columns(y) * SCALE
+            held = 2 * GX // GROUP
             picked = []
-            for d in range(per_source):
-                x = (h * per_source + d).astype(F32)
+            for d in range(held):
+                x = (n * held + d).astype(F32)
                 mask = jnp.where(x_old_ref[...] == x, 1.0, 0.0).astype(BF16)
                 picked.append(
                     jnp.concatenate(
-                        [hit_ref[n] * mask[:, n * 128 : (n + 1) * 128] for n in range(GROUP)], axis=1
+                        [hit_ref[q] * mask[:, q * 128 : (q + 1) * 128] for q in range(GROUP)], axis=1
                     )
                 )
             joined = dot(
@@ -266,29 +270,31 @@
                 jnp.concatenate([t_old_ref[k] for k in range(3)], axis=1),
                 NN,
             )
-            for d in range(per_source):
-                acc_ref[h * per_source + d] += joined[d * NY * LAYERS : (d + 1) * NY * LAYERS]
-            for i in range(CAP):
-                c = step * CAP + i
-                here = pl.ds(h * CAP + i, 1)
-                lines = slice(i * B, (i + 1) * B)
-                wxy = xy_weights(
-                    p_ref[0, here, :], p_ref[1, here, :], tx_ref[lines], ty_ref[lines]
-                )
-                wxy_ref[c] = wxy
-                weighted = jnp.concatenate(
-                    [wxy * f_ref[k, here, :] for k in range(3)], axis=0
-                ).astype(BF16)
-                wz = z_weights(p_ref[2, here, :])
-                for n, part in enumerate(wz):
-                    wz_ref[c, n] = part
-                terms = dot(weighted, jnp.concatenate(wz, axis=1), NT).astype(BF16)
-                at = pl.ds(pl.multiple_of(h * 128 + i * B, B), B)
-                for k in range(3):
-                    t_ref[k, at, :] = terms[k * B : (k + 1) * B]
+            for d in range(held):
+                acc_ref[n * held + d] += joined[d * NY * LAYERS : (d + 1) * NY * LAYERS]
+            for side, h in enumerate(sources):
+                for i in range(CAP):
+                    c = (g * GROUP + h) * CAP + i
+                    here = pl.ds(h * CAP + i, 1)
+                    lines = slice(i * B, (i + 1) * B)
+                    wxy = xy_weights(
+                        p_ref[0, here, :], p_ref[1, here, :],
+                        tx_ref[side, lines, :], ty_ref[side, lines, :],
+                    )
+                    wxy_ref[c] = wxy
+                    weighted = jnp.concatenate(
+                        [wxy * f_ref[k, here, :] for k in range(3)], axis=0
+                    ).astype(BF16)
+                    wz = z_weights(p_ref[2, here, :])
+                    for q, part in enumerate(wz):
+                        wz_ref[c, q] = part
+                    terms = dot(weighted, jnp.concatenate(wz, axis=1), NT).astype(BF16)
+                    at = pl.ds(pl.multiple_of(h * 128 + i * B, B), B)
+                    for k in range(3):
+                        t_ref[k, at, :] = terms[k * B : (k + 1) * B]
             return carry
 
-        lax.fori_loop(0, GROUP, source, 0)
+        lax.fori_loop(0, GROUP // 2, pair, 0)
         t_old_ref[...] = t_ref[...]
         tile = lax.broadcasted_iota(jnp.int32, (NY * LAYERS, 128), 0).astype(F32)
         for h in range(GROUP):
@@ -297,7 +303,7 @@
             hit_ref[h] = jnp.where(tile == lists_ref[h, 1:2, :], 1.0, 0.0).astype(BF16)
 
     for h in range(GROUP):
-        take(h, h)
+        take(h, h, h % 2)
 
     def all_but_last(g, carry):
         group(g, True)
@@ -349,16 +355,16 @@
                 )
 
     def work(g):
-        def pair(n, carry):
-            step = g * GROUP + 2 * n
-            later = jnp.where(n < GROUP // 2 - 1, step + 2, (g - 1) * GROUP)
-            gather(step + 1, odd_ref)
-            project(step, 2 * n, even_ref)
-            gather(jnp.where(later < 0, 0, later), even_ref)
-            project(step + 1, 2 * n + 1, odd_ref)
-            return carry
-
-        lax.fori_loop(0, GROUP // 2, pair, 0)
+        buffers = (even_ref, odd_ref)
+        for h in range(GROUP):
+            step = g * GROUP + h
+            if h < GROUP - 1:
+                later = step + 1
+            else:
+                later = jnp.maximum((g - 1) * GROUP, 0)
+            gather(later, buffers[(h + 1) % 2])
+            project(step, h, buffers[h % 2])
+
         rem = jnp.zeros((GROUP * CAP, 128), F32)
         for k in range(3):
             got = dot(pv_ref[k].astype(BF16), basis_ref[k], NT)
@@ -367,17 +373,19 @@
         c_ref[3] = rem
         for h in range(GROUP):
             for r in range(OUT_PLANES):
-                blk_ref[r * CAP : (r + 1) * CAP, :] = c_ref[r, h * CAP : (h + 1) * CAP, :]
-            send_ref[g * GROUP + h] = blk_ref[: OUT_PLANES * CAP, :].astype(BF16)
+                blk_ref[h % 2, r * CAP : (r + 1) * CAP, :] = c_ref[r, h * CAP : (h + 1) * CAP, :]
+            send_ref[g * GROUP + h] = blk_ref[h % 2, : OUT_PLANES * CAP, :].astype(BF16)
 
     my_y, my_z, my_core = me // 16, me // 2 % 8, me % 2
 
     def send(g, first=0):
         dy = g // (16 // GROUP)
-        base = wrap(my_y - dy, slab_count // 16) * 16
+        rest = g - dy * (16 // GROUP)
+        core = rest // (8 // GROUP)
+        base = wrap(my_y - dy, slab_count // 16) * 16 + wrap(my_core - core, 2)
         for h in range(first, GROUP):
-            dz = (g - dy * (16 // GROUP)) * (GROUP // 2) + h // 2
-            place = base + 2 * wrap(my_z - dz, 8) + wrap(my_core - h % 2, 2)
+            dz = (rest - core * (8 // GROUP)) * GROUP + h
+            place = base + 2 * wrap(my_z - dz, 8)
             pltpu.make_async_remote_copy(
                 src_ref=send_ref.at[g * GROUP + h],
                 dst_ref=back_ref.at[g * GROUP + h],
@@ -404,12 +412,14 @@
     pltpu.make_async_copy(back_ref.at[others], back_ref.at[others], recv_sem).wait()
 
     def take(step, carry):
-        blk_ref[: OUT_PLANES * CAP, :] = back_ref[step].astype(F32)
-        for r in range(OUT_PLANES):
-            r_ref[r, pl.ds(step * CAP, CAP), :] = blk_ref[r * CAP : (r + 1) * CAP, :]
+        for side in range(2):
+            at = 2 * step + side
+            blk_ref[side, : OUT_PLANES * CAP, :] = back_ref[at].astype(F32)
+            for r in range(OUT_PLANES):
+                r_ref[r, pl.ds(at * CAP, CAP), :] = blk_ref[side, r * CAP : (r + 1) * CAP, :]
         return carry
 
-    lax.fori_loop(0, slab_count, take, 0, unroll=2)
+    lax.fori_loop(0, slab_count // 2, take, 0)
     rem = dot(r_ref[3].astype(BF16), hot, TN)
     for k in range(3):
         main = dot(r_ref[k].astype(BF16), hot, TN)
@@ -602,7 +612,7 @@
         out_specs=(VMEM_SPEC, VMEM_SPEC),
         scratch_shapes=[
             pltpu.VMEM((PLANES + 2, slots, 128), F32),
-            pltpu.VMEM((block_rows, 128), F32),
+            pltpu.VMEM((2, block_rows, 128), F32),
             pltpu.VMEM((128, cells), F32),
             pltpu.VMEM((slots, cells), BF16),
             pltpu.VMEM((slab_count, block_rows, 128), BF16),
@@ -619,8 +629,8 @@
             pltpu.VMEM((3, held, QP), F32),
             pltpu.VMEM((GROUP, 2, 128), F32),
             pltpu.VMEM((GROUP, 2, 128), F32),
-            pltpu.VMEM((128, 128), F32),
-            pltpu.VMEM((128, 128), F32),
+            pltpu.VMEM((2, 128, 128), F32),
+            pltpu.VMEM((2, 128, 128), F32),
             pltpu.VMEM((3, GROUP * 128, 128), BF16),
             pltpu.VMEM((3, GROUP * 128, 128), BF16),
             pltpu.VMEM((GROUP, NY * LAYERS, 128), BF16),

time: 115 us -> 118 us (1.026)
  Pallas kernels: 112 us -> 114 us
    pallas_call x1, Pallas kernels: 112 us -> 114 us  [whole_step(): pl.pallas_call(step_kernel, out_shape=(jax.ShapeDtypeStruct(vel.shape, F3...]
where the time goes in v7:
time: 118 us
  Pallas kernels  114 us (97%)
  other arithmetic  1.83 us (2%)
    pallas_call x1, Pallas kernels, whole_step(): pl.pallas_call(step_kernel, out_shape=(jax.ShapeDtypeStruct(vel.shape, F3...  114 us

profile of v7, /device:TPU:1, one launch (start us, length us, event | category | flops | bytes accessed | tf_op | source)
XLA Modules:
  0.0 117.7 jit_solution(5278880768620461064)
XLA Ops:
  0.6 114.4 %whole_step.1 = (f32[8,96,128]{2,1,0:T(8,128)}, f32[3,169,192]{2,1,0:T(8,128)}) custom-call(s32[1,192]{1,0:T(1,128)} %bitcast.20, bf16[3,169,192]{2,1,0:T(8,128)(2,1)} %bitcast.17, bf16[3,192,338]{2,1,0:T(8,128)(2,1)} %bitcast.14, s32[3,192]{1,0:T(4,128)} %bitcast.19, s32[16,192]{1,0:T(8,128)} %bitcast.18, s32[1,192]{1,0:T(1,128)} %bitcast.21, ...), custom_call_target="tpu_custom_call" | custom-call | tf_op jit(solution)/shard_map/whole_step/pallas_call | solution.py:605
  115.1 0.0 copy-start
  115.1 1.8 %convert_bitcast_fusion = bf16[192,3,169]{0,2,1:T(8,128)(2,1)} fusion(f32[3,169,192]{2,1,0:T(8,128)} %get-tuple-element.5), kind=kLoop, calls=%fused_computation | loop fusion | flops 97344 | bytes 584064 | tf_op jit(solution)/shard_map/transpose | solution.py:692
  116.9 0.0 copy-done
  116.9 0.7 copy.12
Async XLA Ops:
  115.1 1.8 %copy-start = (f32[8,96,128]{2,1,0:T(8,128)S(1)}, f32[8,96,128]{2,1,0:T(8,128)}, u32[]{:S(2)}) copy-start(f32[8,96,128]{2,1,0:T(8,128)} %get-tuple-element.4) | copy-start | bytes 1179652
